TPU v7x, 32 devices: a whole 2x2x4 slice. The times are simulated.
32 devices in a mesh: dp: 4 (over z), mp: 8 (over y, x, core).
Axes of the slice: x: 2, y: 2, z: 4, core: 2. Of those that a mesh axis runs over, the one named last changes fastest.
Arguments:
- grad_partial: bfloat16 [4, 4, 576, 576], P('dp', None, 'mp'), may hold values from -1.796875 to 1.796875
- owner: int32 [4], replicated, may hold values from 0 to 7, as said below
- offset: int32 [4], replicated, may hold values from 0 to 3, each once
- left_factor: float32 [8, 576, 576], P('mp', None, 'dp'), may hold values from -3 to 3
- right_factor: float32 [8, 576, 576], P('mp', None, 'dp'), may hold values from -3 to 3
- left_basis: bfloat16 [8, 576, 576], P('mp'), may hold values from -0.25 to 0.25
- right_basis: bfloat16 [8, 576, 576], P('mp'), may hold values from -0.25 to 0.25
- momentum: bfloat16 [8, 576, 576], P('mp'), may hold values from -6 to 6
- second_moment: float32 [8, 576, 576], P('mp'), may hold values from 0.2 to 2
Outputs:
- update: bfloat16 [4, 576, 576], P(None, 'mp', 'dp')
- new_left: float32 [8, 576, 576], P('mp', None, 'dp')
- new_right: float32 [8, 576, 576], P('mp', None, 'dp')
- new_momentum: bfloat16 [8, 576, 576], P('mp')
- new_second: float32 [8, 576, 576], P('mp')
Inputs may be any that keep to these rules, and one draw needn't show every extreme that they name: No two blocks have the same owner. `offset`: every position belongs to exactly one block.
All inputs are finite; a program needn't handle non-finite values.
Results may differ from a plain program's by a relative error of at most 0.015.
Values may be sent and summed in bfloat16 or wider, within the bound.
No kernel may reach another device: no remote copies, remote signals or barrier semaphores. Data moves between devices by JAX's collectives and lax.ppermute only.
A program may use at most 64 MiB of HBM per device.

v0:
```python
import jax
import jax.numpy as jnp
from jax import lax
from jax.sharding import PartitionSpec as P


def contract_first(matrix_a, matrix_b):
    return lax.dot_general(
        matrix_a, matrix_b, (((0,), (0,)), ((), ())), preferred_element_type=jnp.float32
    )


def contract_last(matrix_a, matrix_b):
    return lax.dot_general(
        matrix_a, matrix_b, (((1,), (1,)), ((), ())), preferred_element_type=jnp.float32
    )


def per_device(
    grad_partial,
    owner,
    offset,
    left_factor,
    right_factor,
    left_basis,
    right_basis,
    momentum,
    second_moment,
):
    pieces = grad_partial[0]
    blocks, row_count, columns = pieces.shape
    groups = lax.axis_size("mp")
    replicas = lax.axis_size("dp")
    col_share = columns // replicas
    column = lax.axis_index("dp") * col_share
    my_group = lax.axis_index("mp")
    targets = lax.broadcasted_iota(jnp.int32, (groups, blocks), 0)
    positions = lax.broadcasted_iota(jnp.int32, (blocks, blocks), 0)
    routing = (owner[None, :] == targets).astype(jnp.float32)
    where_at = (offset[None, :] == positions).astype(jnp.float32)
    select = contract_last(routing, where_at).astype(jnp.bfloat16)
    occupied = jnp.any(owner == my_group)
    swapped = lax.all_to_all(grad_partial, "dp", split_axis=3, concat_axis=0, tiled=True)
    summed = jnp.sum(swapped.astype(jnp.float32), axis=0).astype(jnp.bfloat16)
    outgoing = jnp.dot(
        select, summed.reshape(blocks, row_count * col_share), preferred_element_type=jnp.float32
    )
    outgoing = outgoing.astype(jnp.bfloat16).reshape(groups, row_count, col_share)
    landed = lax.all_to_all(outgoing, "mp", split_axis=0, concat_axis=0, tiled=True)
    arrived = lax.all_gather(landed, "dp", axis=2, tiled=True)
    gradient = arrived.reshape(groups * row_count, columns)

    def refresh(operands):
        grad_in, left_fac, right_fac, lbasis, rbasis, moment, second = operands
        grad_rows = lax.dynamic_slice_in_dim(grad_in, column, col_share, 0)
        grad_cols = lax.dynamic_slice_in_dim(grad_in, column, col_share, 1)
        new_left = 0.95 * left_fac + 0.05 * contract_last(grad_in, grad_rows)
        new_right = 0.95 * right_fac + 0.05 * contract_first(grad_in, grad_cols)
        new_moment = (0.9 * moment.astype(jnp.float32) + 0.1 * grad_in.astype(jnp.float32)).astype(
            jnp.bfloat16
        )
        turned = contract_first(lbasis, grad_in).astype(jnp.bfloat16)
        rotated = jnp.dot(turned, rbasis, preferred_element_type=jnp.float32)
        turned_mom = contract_first(lbasis, new_moment).astype(jnp.bfloat16)
        rotated_mom = jnp.dot(turned_mom, rbasis, preferred_element_type=jnp.float32)
        new_second = 0.95 * second + 0.05 * rotated * rotated
        scaled = (rotated_mom / (jnp.sqrt(new_second) + 1e-08)).astype(jnp.bfloat16)
        unrotated = jnp.dot(lbasis, scaled, preferred_element_type=jnp.float32).astype(jnp.bfloat16)
        back_rows = lax.dynamic_slice_in_dim(rbasis, column, col_share, 0)
        return (new_left, new_right, new_moment, new_second, contract_last(unrotated, back_rows))

    def keep_old(operands):
        grad_in, left_fac, right_fac, lbasis, rbasis, moment, second = operands
        return (left_fac, right_fac, moment, second, jnp.zeros((columns, col_share), jnp.float32))

    operands = (
        gradient,
        left_factor[0],
        right_factor[0],
        left_basis[0],
        right_basis[0],
        momentum[0],
        second_moment[0],
    )
    new_left, new_right, new_moment, new_second, turned_cols = lax.cond(
        occupied, refresh, keep_old, operands
    )
    outgoing_back = turned_cols.astype(jnp.bfloat16).reshape(groups, row_count, col_share)
    returned = lax.all_to_all(outgoing_back, "mp", split_axis=0, concat_axis=0, tiled=True)
    update = contract_first(select, returned.reshape(groups, row_count * col_share)).astype(
        jnp.bfloat16
    )
    update = update.reshape(blocks, row_count, col_share)
    return (update, new_left[None], new_right[None], new_moment[None], new_second[None])


def solution(mesh):
    placed = (
        P("dp", None, "mp", None),
        P(),
        P(),
        P("mp", None, "dp"),
        P("mp", None, "dp"),
        P("mp", None, None),
        P("mp", None, None),
        P("mp", None, None),
        P("mp", None, None),
    )
    return jax.shard_map(
        per_device,
        mesh=mesh,
        in_specs=placed,
        out_specs=(
            P(None, "mp", "dp"),
            P("mp", None, "dp"),
            P("mp", None, "dp"),
            P("mp", None, None),
            P("mp", None, None),
        ),
        check_vma=False,
    )
```

profile of v0, /device:TPU:0, one launch (start us, length us, event | category | flops | bytes accessed | tf_op | source)
XLA Modules:
  0.0 89.3 jit_solution(13324079998786778093)
XLA Ops:
  0.6 1.4 %copy-done.2 = f32[1,576,576]{2,1,0:T(8,128)S(1)} copy-done((f32[1,576,576]{2,1,0:T(8,128)S(1)}, f32[1,576,576]{2,1,0:T(8,128)}, u32[]{:S(2)}) %copy-start.2) | copy-done | bytes 1327128
  2.0 1.1 %copy.50 = f32[1,576,576]{2,1,0:T(8,128)} copy(f32[1,576,576]{2,1,0:T(8,128)S(1)} %copy-done.2) | data formatting | bytes 2654208
  3.2 1.1 %copy.26 = bf16[1,4,72,576]{2,1,0,3:T(4,128)(2,1)} copy(bf16[1,4,72,576]{3,2,1,0:T(8,128)(2,1)S(1)} %copy-done.7) | data formatting | bytes 663552 | tf_op args[0]
  4.3 6.3 %all-to-all-start = ((bf16[1,4,72,576]{2,1,0,3:T(4,128)(2,1)}), bf16[1,4,72,576]{2,1,0,3:T(4,128)(2,1)S(1)}, u32[]{:S(2)}, u32[]{:S(2)}) async-start(bf16[1,4,72,576]{2,1,0,3:T(4,128)(2,1)} %copy.26), calls=%async_computation | async-start | bytes 1179648 | tf_op jit(solution)/shard_map/all_to_all | solution.py:43
  10.8 15.8 %all-to-all-done = bf16[1,4,72,576]{2,1,0,3:T(4,128)(2,1)S(1)} async-done(((bf16[1,4,72,576]{2,1,0,3:T(4,128)(2,1)}), bf16[1,4,72,576]{2,1,0,3:T(4,128)(2,1)S(1)}, u32[]{:S(2)}, u32[]{:S(2)}) %all-to-all-start) | async-done | bytes 331808 | tf_op jit(solution)/shard_map/all_to_all | solution.py:43
  26.6 0.5 reduce_sum.12
  27.7 0.4 reshape.36
  28.1 0.9 %copy.28 = bf16[8,72,144]{1,2,0:T(8,128)(2,1)} copy(bf16[8,72,144]{2,1,0:T(8,128)(2,1)S(1)} %reshape.36) | data formatting | bytes 331776 | tf_op jit(solution)/shard_map/reshape | solution.py:48
  29.0 3.9 %all-to-all-start.1 = ((bf16[8,72,144]{1,2,0:T(8,128)(2,1)}), bf16[8,72,144]{1,2,0:T(8,128)(2,1)S(1)}, u32[]{:S(2)}, u32[]{:S(2)}) async-start(bf16[8,72,144]{1,2,0:T(8,128)(2,1)} %copy.28), calls=%async_computation.1 | async-start | bytes 589824 | tf_op jit(solution)/shard_map/all_to_all | solution.py:49
  32.9 0.6 compare_reduce_fusion
  34.1 6.0 %all-to-all-done.1 = bf16[8,72,144]{1,2,0:T(8,128)(2,1)S(1)} async-done(((bf16[8,72,144]{1,2,0:T(8,128)(2,1)}), bf16[8,72,144]{1,2,0:T(8,128)(2,1)S(1)}, u32[]{:S(2)}, u32[]{:S(2)}) %all-to-all-start.1) | async-done | bytes 165920 | tf_op jit(solution)/shard_map/all_to_all | solution.py:49
  40.2 22.7 %all_gather.3 = bf16[8,72,576]{1,0,2:T(8,128)(2,1)S(1)} all-gather(bf16[8,72,144]{1,0,2:T(8,128)(2,1)S(1)} %copy.29), channel_id=1, replica_groups=mesh['dp'=4,'mp'=8] {'dp'}, dimensions={2}, use_global_device_ids=true | all-gather | bytes 829440 | tf_op jit(solution)/shard_map/all_gather | solution.py:50
  62.9 14.0 %conditional.1 = (f32[576,144]{0,1:T(8,128)S(1)}, f32[576,144]{0,1:T(8,128)S(1)}, bf16[576,576]{1,0:T(8,128)(2,1)S(1)}, f32[576,576]{1,0:T(8,128)}, bf16[576,144]{0,1:T(8,128)(2,1)}) conditional(s32[]{:T(128)} %convert_element_type.50, (f32[576,144]{0,1:T(8,128)S(1)}, f32[576,144]{0,1:T(8,128)S(1)}, bf16[576,576]{1,0:T(8,128)(2,1)S(1)}, ...), branch_computations={%region_2.0_spmd, %region_3.0_spmd} | conditional | flops 2203490304 | bytes 19630206 | solution.py:85
  62.9 1.2 %copy.30 = bf16[8,72,576]{2,1,0:T(8,128)(2,1)S(1)} copy(bf16[8,72,576]{1,0,2:T(8,128)(2,1)S(1)} %get-tuple-element.93) | data formatting | bytes 1327104 | tf_op jit(solution)/shard_map
  64.2 4.7 %fusion = f32[576,576]{1,0:T(8,128)} fusion(f32[576,576]{1,0:T(8,128)} %get-tuple-element.54, bf16[576,576]{1,0:T(8,128)(2,1)S(1)} %bitcast.47, bf16[1,576,576]{2,1,0:T(8,128)(2,1)} %get-tuple-element.75, bf16[1,576,576]{2,1,0:T(8,128)(2,1)} %get-tuple-element.74), kind=kOutput, calls=%fused_computation.1 | convolution fusion | flops 766070784 | bytes 4644864 | tf_op jit(solution)/shard_map/cond/branch_1_fun/dot_general | solution.py:63
  68.8 0.5 add_convert_fusion
  69.3 0.5 fusion.6
  69.8 0.6 fusion.4
  70.4 3.8 %divide_convert_fusion = bf16[576,576]{1,0:T(8,128)(2,1)S(1)} fusion(f32[576,576]{1,0:T(8,128)} %fusion, bf16[576,576]{1,0:T(8,128)(2,1)S(1)} %add_convert_fusion, bf16[1,576,576]{2,1,0:T(8,128)(2,1)} %get-tuple-element.75, bf16[1,576,576]{2,1,0:T(8,128)(2,1)S(1)} %copy-done.8), kind=kOutput, calls=%fused_computation.2 | convolution fusion | flops 765739008 | bytes 3981312 | tf_op jit(solution)/shard_map/cond/branch_1_fun/dot_general | solution.py:65
  74.2 2.7 %fusion.1 = bf16[576,144]{0,1:T(8,128)(2,1)} fusion(bf16[576,576]{1,0:T(8,128)(2,1)S(1)} %divide_convert_fusion, bf16[1,576,576]{2,1,0:T(8,128)(2,1)S(1)} %copy-done.8, bf16[1,576,576]{2,1,0:T(8,128)(2,1)} %get-tuple-element.75, s32[]{:T(128)S(6)} %select_n.2), kind=kOutput, calls=%fused_computation.7 | convolution fusion | flops 478089216 | bytes 1677316 | tf_op jit(solution)/shard_map/cond/branch_1_fun/dot_general | solution.py:14
  77.0 1.3 %copy.32 = bf16[576,144]{1,0:T(8,128)(2,1)S(1)} copy(bf16[576,144]{0,1:T(8,128)(2,1)} %get-tuple-element.67) | data formatting | bytes 331776 | tf_op jit(solution)/shard_map/reshape | solution.py:88
  78.2 9.7 %all_to_all.22 = bf16[8,72,144]{2,1,0:T(8,128)(2,1)S(1)} all-to-all(bf16[8,72,144]{2,1,0:T(8,128)(2,1)S(1)} %bitcast.63), channel_id=1, replica_groups=mesh['dp'=4,'mp'=8] {'mp'}, dimensions={0} | all-to-all | bytes 331776 | tf_op jit(solution)/shard_map/all_to_all | solution.py:89
  87.9 0.3 reshape.38
  88.4 0.9 %reshape.39 = bf16[4,72,144]{2,1,0:T(8,128)(2,1)} reshape(bf16[4,10368]{1,0:T(4,128)(2,1)S(1)} %convolution_convert_fusion.4) | data formatting | bytes 165888 | tf_op jit(solution)/shard_map/reshape | solution.py:93
  (27 shorter events, 1.1 us)
Async XLA Ops:
  0.6 1.4 %copy-start.2 = (f32[1,576,576]{2,1,0:T(8,128)S(1)}, f32[1,576,576]{2,1,0:T(8,128)}, u32[]{:S(2)}) copy-start(f32[1,576,576]{2,1,0:T(8,128)} %param.19) | copy-start | bytes 3981316
  2.0 1.2 %copy-start.7 = (bf16[1,4,72,576]{3,2,1,0:T(8,128)(2,1)S(1)}, bf16[1,4,72,576]{3,2,1,0:T(8,128)(2,1)}, u32[]{:S(2)}) copy-start(bf16[1,4,72,576]{3,2,1,0:T(8,128)(2,1)} %param.11) | copy-start | bytes 995332
  3.2 7.5 %copy-start.9 = (s32[4]{0:T(128)S(1)}, s32[4]{0:T(128)}, u32[]{:S(2)}) copy-start(s32[4]{0:T(128)} %param.13) | copy-start | bytes 52
  3.2 7.5 %copy-start.10 = (s32[4]{0:T(128)S(1)}, s32[4]{0:T(128)}, u32[]{:S(2)}) copy-start(s32[4]{0:T(128)} %param.12) | copy-start | bytes 52
  4.3 22.2 %all-to-all-start = ((bf16[1,4,72,576]{2,1,0,3:T(4,128)(2,1)}), bf16[1,4,72,576]{2,1,0,3:T(4,128)(2,1)S(1)}, u32[]{:S(2)}, u32[]{:S(2)}) async-start(bf16[1,4,72,576]{2,1,0,3:T(4,128)(2,1)} %copy.26), calls=%async_computation | async-start | bytes 1179648 | tf_op jit(solution)/shard_map/all_to_all | solution.py:43
  29.0 33.9 %copy-start.1 = (bf16[1,576,576]{2,1,0:T(8,128)(2,1)S(1)}, bf16[1,576,576]{2,1,0:T(8,128)(2,1)}, u32[]{:S(2)}) copy-start(bf16[1,576,576]{2,1,0:T(8,128)(2,1)} %param.18) | copy-start | bytes 1990660
  29.0 33.9 %copy-start.4 = (f32[1,576,144]{1,2,0:T(8,128)S(1)}, f32[1,576,144]{1,2,0:T(8,128)}, u32[]{:S(2)}) copy-start(f32[1,576,144]{1,2,0:T(8,128)} %param.15) | copy-start | bytes 995332
  29.0 33.9 %copy-start.6 = (f32[1,576,144]{1,2,0:T(8,128)S(1)}, f32[1,576,144]{1,2,0:T(8,128)}, u32[]{:S(2)}) copy-start(f32[1,576,144]{1,2,0:T(8,128)} %param.14) | copy-start | bytes 995332
  29.0 11.1 %all-to-all-start.1 = ((bf16[8,72,144]{1,2,0:T(8,128)(2,1)}), bf16[8,72,144]{1,2,0:T(8,128)(2,1)S(1)}, u32[]{:S(2)}, u32[]{:S(2)}) async-start(bf16[8,72,144]{1,2,0:T(8,128)(2,1)} %copy.28), calls=%async_computation.1 | async-start | bytes 589824 | tf_op jit(solution)/shard_map/all_to_all | solution.py:49
  69.3 1.1 %copy-start.8 = (bf16[1,576,576]{2,1,0:T(8,128)(2,1)S(1)}, bf16[1,576,576]{2,1,0:T(8,128)(2,1)}, u32[]{:S(2)}) copy-start(bf16[1,576,576]{2,1,0:T(8,128)(2,1)} %get-tuple-element.74) | copy-start | bytes 1990660 | tf_op jit(solution)/shard_map/cond
  77.0 12.4 %copy-start = (bf16[576,576]{1,0:T(8,128)(2,1)}, bf16[576,576]{1,0:T(8,128)(2,1)S(1)}, u32[]{:S(2)}) copy-start(bf16[576,576]{1,0:T(8,128)(2,1)S(1)} %get-tuple-element.70) | copy-start | bytes 1990660
  77.0 12.4 %copy-start.3 = (f32[576,144]{0,1:T(8,128)}, f32[576,144]{0,1:T(8,128)S(1)}, u32[]{:S(2)}) copy-start(f32[576,144]{0,1:T(8,128)S(1)} %get-tuple-element.69) | copy-start | bytes 995332
  77.0 12.4 %copy-start.5 = (f32[576,144]{0,1:T(8,128)}, f32[576,144]{0,1:T(8,128)S(1)}, u32[]{:S(2)}) copy-start(f32[576,144]{0,1:T(8,128)S(1)} %get-tuple-element.68) | copy-start | bytes 995332
where the time goes:
time: 89.9 us; the launch traced here: 89.3 us
  blocking collectives  32.4 us (36%)
  waiting for transfers between devices  21.7 us (24%)
  matrix products  12.8 us (14%)
  starting transfers between devices  10.2 us (11%)
  local copies, waits for them, and re-layouts  9.16 us (10%)
  other arithmetic  1.6 us (2%)
  between operations  1.34 us (1%)
    all_gather x1, blocking collectives, per_device(): arrived = lax.all_gather(landed, 'dp', axis=2, tiled=True)  22.7 us
    all_to_all x1, waiting for transfers between devices, per_device(): lax.all_to_all(grad_partial, 'dp', split_axis=3, concat_axis=0, tiled=True)  15.8 us
    all_to_all x1, blocking collectives, per_device(): lax.all_to_all(outgoing_back, 'mp', split_axis=0, concat_axis=0, tiled=True)  9.72 us
    all_to_all x1, starting transfers between devices, per_device(): lax.all_to_all(grad_partial, 'dp', split_axis=3, concat_axis=0, tiled=True)  6.35 us
    all_to_all x1, waiting for transfers between devices, per_device(): lax.all_to_all(outgoing, 'mp', split_axis=0, concat_axis=0, tiled=True)  5.97 us
    dot_general x1, matrix products, refresh(): rotated = jnp.dot(turned, rbasis, preferred_element_type=jnp.float32)  4.65 us
    all_to_all x1, starting transfers between devices, per_device(): lax.all_to_all(outgoing, 'mp', split_axis=0, concat_axis=0, tiled=True)  3.85 us
    dot_general x1, matrix products, refresh(): jnp.dot(turned_mom, rbasis, preferred_element_type=jnp.float32)  3.78 us
  transfers between devices with their start and end apart: 2, of which 2 were waited for; matrix products, arithmetic and copies ran while one was open for 1% of the time, Pallas kernels for 0%

commit v1 on v0

--- a/solution.py
+++ b/solution.py
@@ -1,8 +1,14 @@
 import jax
 import jax.numpy as jnp
 from jax import lax
+from jax.experimental import pallas as pl
+from jax.experimental.pallas import tpu as pltpu
 from jax.sharding import PartitionSpec as P
 
+LANES = 128
+SUBLANES = 8
+VMEM = pl.BlockSpec(memory_space=pltpu.VMEM)
+SMEM = pl.BlockSpec(memory_space=pltpu.SMEM)
 
 def contract_first(matrix_a, matrix_b):
     return lax.dot_general(
@@ -16,7 +22,277 @@
     )
 
 
-def per_device(
+def matmul(matrix_a, matrix_b):
+    return jnp.dot(matrix_a, matrix_b, preferred_element_type=jnp.float32)
+
+
+def tail_start(share):
+    return jnp.where(share == 0, 0, 2 * share + 1) if not isinstance(share, int) else (
+        0 if share == 0 else 2 * share + 1
+    )
+
+
+def packed_fits(rows, columns, replicas):
+    return (
+        columns == replicas * LANES + LANES // 2
+        and rows == (2 * replicas + 1) * SUBLANES
+        and rows % SUBLANES == 0
+    )
+
+
+def pack_kernel(me_ref, grad_ref, *outs):
+    replicas = len(outs)
+    blocks, rows, columns = grad_ref.shape
+    half = LANES // 2
+    for step in range(replicas):
+        share = lax.rem(me_ref[0] + step, replicas)
+        col = pl.multiple_of(share * LANES, LANES)
+        start = tail_start(share)
+        row = pl.multiple_of(start * SUBLANES, SUBLANES)
+        row_third = pl.multiple_of(
+            jnp.minimum(start + 2, rows // SUBLANES - 1) * SUBLANES, SUBLANES
+        )
+        out = outs[step]
+        for b in range(blocks):
+            out[b, :rows, :] = grad_ref[b, :, pl.ds(col, LANES)]
+            out[b, rows : rows + SUBLANES, :half] = grad_ref[
+                b, pl.ds(row, SUBLANES), columns - half :
+            ]
+            row_next = pl.multiple_of(row + SUBLANES, SUBLANES)
+            out[b, rows + SUBLANES :, :half] = grad_ref[
+                b, pl.ds(row_next, SUBLANES), columns - half :
+            ]
+            out[b, rows : rows + SUBLANES, half:] = grad_ref[
+                b, pl.ds(row_third, SUBLANES), columns - half :
+            ]
+            out[b, rows + SUBLANES :, half:] = jnp.zeros((SUBLANES, half), out.dtype)
+
+
+def slot_of(owner_ref, group):
+    found = jnp.int32(0)
+    block = jnp.int32(0)
+    for b in range(owner_ref.shape[0]):
+        hit = owner_ref[b] == group
+        block = jnp.where(hit, b, block)
+        found = jnp.where(hit, 1, found)
+    return block, found
+
+
+def route_kernel(owner_ref, offset_ref, *refs):
+    parts, out, summed = refs[:-2], refs[-2], refs[-1]
+    replicas = len(parts)
+    groups = out.shape[0] // replicas
+    blocks = summed.shape[0]
+    for b in range(blocks):
+        total = parts[0][b].astype(jnp.float32)
+        for part in parts[1:]:
+            total = total + part[b].astype(jnp.float32)
+        summed[b] = total.astype(jnp.bfloat16)
+    for group in range(groups):
+        block, _ = slot_of(owner_ref, group)
+        piece = summed[offset_ref[block]]
+        for r in range(replicas):
+            out[r * groups + group] = piece
+
+
+def prepare_kernel(group_ref, owner_ref, lbasis, rbasis, moment, lbasis_t, turned_back):
+    _, found = slot_of(owner_ref, group_ref[0])
+
+    @pl.when(found == 1)
+    def _():
+        transposed = lbasis[...].T
+        lbasis_t[...] = transposed
+        turned = matmul(transposed, moment[...]).astype(jnp.bfloat16)
+        turned_back[...] = 0.9 * matmul(turned, rbasis[...])
+
+
+def owner_kernel(
+    group_ref, share_ref, owner_ref, arrived, lbasis, rbasis, lbasis_t, old_part, second,
+    gradient, new_second, back, turned, unrotated,
+):
+    _, found = slot_of(owner_ref, group_ref[0])
+    groups, rows, col_share = back.shape
+    columns = gradient.shape[1]
+    replicas = arrived.shape[0] // groups
+    half = LANES // 2
+    tail = columns - half
+
+    @pl.when(found == 1)
+    def _():
+        for r in range(replicas):
+            start = tail_start(r)
+            count = 3 if r == 0 else 2
+            for m in range(groups):
+                piece = r * groups + m
+                base = m * rows
+                gradient[base : base + rows, r * LANES : (r + 1) * LANES] = arrived[piece, :rows, :]
+                for g in range(count):
+                    row = base + (start + g) * SUBLANES
+                    below = rows + (g % 2) * SUBLANES
+                    beside = (g // 2) * half
+                    gradient[row : row + SUBLANES, tail:] = arrived[
+                        piece, below : below + SUBLANES, beside : beside + half
+                    ]
+        turned[...] = matmul(lbasis_t[...], gradient[...]).astype(jnp.bfloat16)
+        cut = 2 * LANES
+        for first in range(0, columns, cut):
+            cols = slice(first, min(first + cut, columns))
+            rotated = matmul(turned[...], rbasis[:, cols])
+            fresh = 0.95 * second[:, cols] + 0.05 * rotated * rotated
+            new_second[:, cols] = fresh
+            rotated_mom = old_part[:, cols] + 0.1 * rotated
+            scaled = (rotated_mom / (jnp.sqrt(fresh) + 1e-08)).astype(jnp.bfloat16)
+            unrotated[:, cols] = matmul(lbasis[...], scaled).astype(jnp.bfloat16)
+        own = pl.ds(pl.multiple_of(share_ref[0] * col_share, 16), col_share)
+        result = contract_last(unrotated[...], rbasis[own, :]).astype(jnp.bfloat16)
+        for m in range(groups):
+            back[m] = result[m * rows : (m + 1) * rows]
+
+    @pl.when(found == 0)
+    def _():
+        new_second[...] = second[...]
+
+
+def factor_kernel(
+    group_ref, share_ref, owner_ref, gradient, left_t, right_t, moment, new_left_t, new_right_t,
+    new_moment,
+):
+    _, found = slot_of(owner_ref, group_ref[0])
+    col_share, columns = left_t.shape
+
+    @pl.when(found == 1)
+    def _():
+        first = pl.multiple_of(share_ref[0] * col_share, 16)
+        grad = gradient[...]
+        new_left_t[...] = 0.95 * left_t[...] + 0.05 * contract_last(
+            gradient[pl.ds(first, col_share), :], grad
+        )
+        rows = lax.broadcasted_iota(jnp.int32, (col_share, columns), 0) + first
+        cols = lax.broadcasted_iota(jnp.int32, (col_share, columns), 1)
+        pick = jnp.where(rows == cols, 1.0, 0.0).astype(jnp.bfloat16)
+        grad_cols_t = contract_last(pick, grad).astype(jnp.bfloat16)
+        new_right_t[...] = 0.95 * right_t[...] + 0.05 * matmul(grad_cols_t, grad)
+        new_moment[...] = (
+            0.9 * moment[...].astype(jnp.float32) + 0.1 * grad.astype(jnp.float32)
+        ).astype(jnp.bfloat16)
+
+    @pl.when(found == 0)
+    def _():
+        new_left_t[...] = left_t[...]
+        new_right_t[...] = right_t[...]
+        new_moment[...] = moment[...]
+
+
+def place_kernel(owner_ref, offset_ref, returned, update):
+    for b in range(update.shape[0]):
+        update[offset_ref[b]] = returned[owner_ref[b]]
+
+
+def cost(flops, *arrays):
+    return pl.CostEstimate(
+        flops=flops, bytes_accessed=sum(a.size * a.dtype.itemsize for a in arrays), transcendentals=0
+    )
+
+
+def per_device_packed(
+    grad_partial,
+    owner,
+    offset,
+    left_factor,
+    right_factor,
+    left_basis,
+    right_basis,
+    momentum,
+    second_moment,
+):
+    pieces = grad_partial[0]
+    blocks, rows, columns = pieces.shape
+    groups = lax.axis_size("mp")
+    replicas = lax.axis_size("dp")
+    col_share = columns // replicas
+    share = lax.axis_index("dp").astype(jnp.int32).reshape(1)
+    group = lax.axis_index("mp").astype(jnp.int32).reshape(1)
+    bf16, f32 = jnp.bfloat16, jnp.float32
+    shape = jax.ShapeDtypeStruct
+    packed = shape((blocks, rows + 2 * SUBLANES, LANES), bf16)
+    square = (columns, columns)
+    lbasis, rbasis, moment, second = left_basis[0], right_basis[0], momentum[0], second_moment[0]
+    left_t, right_t = left_factor[0].T, right_factor[0].T
+    product = 2 * columns**3
+
+    parts = pl.pallas_call(
+        pack_kernel,
+        out_shape=[packed] * replicas,
+        in_specs=[SMEM, VMEM],
+        out_specs=[VMEM] * replicas,
+        name="pack",
+    )(share, pieces)
+    parts = [parts[0]] + [
+        lax.ppermute(parts[s], "dp", [(i, (i + s) % replicas) for i in range(replicas)])
+        for s in range(1, replicas)
+    ]
+    lbasis_t, old_part = pl.pallas_call(
+        prepare_kernel,
+        out_shape=[shape(square, bf16), shape(square, f32)],
+        in_specs=[SMEM, SMEM] + [VMEM] * 3,
+        out_specs=[VMEM] * 2,
+        cost_estimate=cost(2 * product, lbasis, rbasis, moment, lbasis, second),
+        name="prepare",
+    )(group, owner, lbasis, rbasis, moment)
+    outgoing = pl.pallas_call(
+        route_kernel,
+        out_shape=shape((replicas * groups,) + packed.shape[1:], bf16),
+        in_specs=[SMEM, SMEM] + [VMEM] * replicas,
+        out_specs=VMEM,
+        scratch_shapes=[pltpu.VMEM(packed.shape, bf16)],
+        name="route",
+    )(owner, offset, *parts)
+    arrived = lax.all_to_all(outgoing, ("dp", "mp"), split_axis=0, concat_axis=0, tiled=True)
+    gradient, new_second, back = pl.pallas_call(
+        owner_kernel,
+        out_shape=[
+            shape(square, bf16),
+            shape(square, f32),
+            shape((groups, rows, col_share), bf16),
+        ],
+        in_specs=[SMEM] * 3 + [VMEM] * 6,
+        out_specs=[VMEM] * 3,
+        scratch_shapes=[pltpu.VMEM(square, bf16), pltpu.VMEM(square, bf16)],
+        cost_estimate=cost(3 * product, lbasis, rbasis, lbasis_t, old_part, second, second),
+        name="owner_step",
+    )(group, share, owner, arrived, lbasis, rbasis, lbasis_t, old_part, second)
+    returned = lax.all_to_all(back, "mp", split_axis=0, concat_axis=0, tiled=True)
+    new_left_t, new_right_t, new_moment = pl.pallas_call(
+        factor_kernel,
+        out_shape=[shape(left_t.shape, f32), shape(right_t.shape, f32), shape(square, bf16)],
+        in_specs=[SMEM] * 3 + [VMEM] * 4,
+        out_specs=[VMEM] * 3,
+        cost_estimate=cost(product, left_t, left_t, right_t, right_t, moment, moment),
+        name="factors",
+    )(group, share, owner, gradient, left_t, right_t, moment)
+    update = pl.pallas_call(
+        place_kernel,
+        out_shape=shape((blocks, rows, col_share), bf16),
+        in_specs=[SMEM, SMEM, VMEM],
+        out_specs=VMEM,
+        name="place",
+    )(owner, offset, returned)
+    return (
+        update,
+        new_left_t.T[None],
+        new_right_t.T[None],
+        new_moment[None],
+        new_second[None],
+    )
+
+
+def per_device(grad_partial, *rest):
+    _, _, rows, columns = grad_partial.shape
+    fits = packed_fits(rows, columns, lax.axis_size("dp"))
+    return (per_device_packed if fits else per_device_general)(grad_partial, *rest)
+
+
+def per_device_general(
     grad_partial,
     owner,
     offset,

time: 89.9 us -> 63.9 us (0.71)
  blocking collectives: 32.4 us -> 0 us
  Pallas kernels: 0 us -> 15.5 us
  matrix products: 12.8 us -> 0 us
  starting transfers between devices: 10.2 us -> 19.4 us
  local copies, waits for them, and re-layouts: 9.16 us -> 2.21 us
  waiting for transfers between devices: 21.7 us -> 25.8 us
  other arithmetic: 1.6 us -> 0 us
    all_gather x1 -> x0, blocking collectives: 22.7 us -> none  [per_device(): arrived = lax.all_gather(landed, 'dp', axis=2, tiled=True)]
    pallas_call x0 -> x6, Pallas kernels: none -> 15.5 us  [the longest x1 4.27 us: per_device_packed(): pl.pallas_call(owner_kernel, out_shape=[shape(square, bf16), shape(square...]
    dot_general x8 -> x0, matrix products: 12.8 us -> none  [the longest x1 4.65 us: refresh(): rotated = jnp.dot(turned, rbasis, preferred_element_type=jnp.float32)]
    all_to_all x1 -> x0, blocking collectives: 9.72 us -> none  [per_device(): lax.all_to_all(outgoing_back, 'mp', split_axis=0, concat_axis=0, tiled=True)]
    ppermute x0 -> x3, starting transfers between devices: none -> 6.99 us  [per_device_packed(): lax.ppermute(parts[s], 'dp', [(i, (i + s) % replicas) for i in range(repl...]
    ppermute x0 -> x3, waiting for transfers between devices: none -> 5.11 us  [per_device_packed(): lax.ppermute(parts[s], 'dp', [(i, (i + s) % replicas) for i in range(repl...]
    reshape x6 -> x0, local copies, waits for them, and re-layouts: 3.97 us -> none  [the longest x2 1.31 us: per_device(): outgoing.astype(jnp.bfloat16).reshape(groups, row_count, col_share)]
    all_to_all x2, starting transfers between devices: 10.2 us -> 12.4 us  [the longest x1 6.86 us: per_device_packed(): lax.all_to_all(back, 'mp', split_axis=0, concat_axis=0, tiled=True)]
  transfers between devices with their start and end apart: 2 -> 5, of which waited for: 2 -> 5; matrix products, arithmetic and copies ran while one was open for 1% -> 0% of each run, Pallas kernels for 0% -> 9%
where the time goes in v1:
time: 63.9 us; the launch traced here: 63.6 us
  waiting for transfers between devices  25.8 us (40%)
  starting transfers between devices  19.4 us (30%)
  Pallas kernels  15.5 us (24%)
  local copies, waits for them, and re-layouts  2.21 us (3%)
  between operations  0.66 us (1%)
    all_to_all x1, waiting for transfers between devices, per_device_packed(): lax.all_to_all(outgoing, ('dp', 'mp'), split_axis=0, concat_axis=0, tiled...  16.2 us
    ppermute x3, starting transfers between devices, per_device_packed(): lax.ppermute(parts[s], 'dp', [(i, (i + s) % replicas) for i in range(repl...  6.99 us
    all_to_all x1, starting transfers between devices, per_device_packed(): lax.all_to_all(back, 'mp', split_axis=0, concat_axis=0, tiled=True)  6.86 us
    all_to_all x1, starting transfers between devices, per_device_packed(): lax.all_to_all(outgoing, ('dp', 'mp'), split_axis=0, concat_axis=0, tiled...  5.55 us
    ppermute x3, waiting for transfers between devices, per_device_packed(): lax.ppermute(parts[s], 'dp', [(i, (i + s) % replicas) for i in range(repl...  5.11 us
    all_to_all x1, waiting for transfers between devices, per_device_packed(): lax.all_to_all(back, 'mp', split_axis=0, concat_axis=0, tiled=True)  4.46 us
    pallas_call x1, Pallas kernels, per_device_packed(): pl.pallas_call(owner_kernel, out_shape=[shape(square, bf16), shape(square...  4.27 us
    pallas_call x1, Pallas kernels, per_device_packed(): pl.pallas_call(prepare_kernel, out_shape=[shape(square, bf16), shape(squa...  2.94 us
  transfers between devices with their start and end apart: 5, of which 5 were waited for; matrix products, arithmetic and copies ran while one was open for 0% of the time, Pallas kernels for 9%

profile of v1, /device:TPU:0, one launch (start us, length us, event | category | flops | bytes accessed | tf_op | source)
XLA Modules:
  0.0 63.6 jit_solution(16244172971278575306)
XLA Ops:
  0.6 1.8 %pack.1 = (bf16[4,88,128]{2,1,0:T(8,128)(2,1)}, bf16[4,88,128]{2,1,0:T(8,128)(2,1)}, bf16[4,88,128]{2,1,0:T(8,128)(2,1)}, bf16[4,88,128]{2,1,0:T(8,128)(2,1)}) custom-call(s32[1]{0:T(128)} %bitcast.1.me_ref.share_ref, bf16[4,72,576]{2,1,0:T(8,128)(2,1)} %bitcast.30), custom_call_target="tpu_custom_call" | custom-call | tf_op jit(solution)/shard_map/pack/pallas_call | solution.py:223
  2.4 3.1 %collective-permute-start = (bf16[4,88,128]{2,1,0:T(8,128)(2,1)}, bf16[4,88,128]{2,1,0:T(8,128)(2,1)S(1)}, u32[]{:S(2)}, u32[]{:S(2)}) collective-permute-start(bf16[4,88,128]{2,1,0:T(8,128)(2,1)} %get-tuple-element.18), channel_id=1, source_target_pairs={{0,8},{8,16},{16,24},{24,0},{1,9},{9,17},{17,25},{25,1},{2,10},{10... | collective-permute-start | bytes 270344 | tf_op jit(solution)/shard_map/ppermute | solution.py:231
  5.5 2.6 %collective-permute-start.1 = (bf16[4,88,128]{2,1,0:T(8,128)(2,1)}, bf16[4,88,128]{2,1,0:T(8,128)(2,1)S(1)}, u32[]{:S(2)}, u32[]{:S(2)}) collective-permute-start(bf16[4,88,128]{2,1,0:T(8,128)(2,1)} %get-tuple-element.19), channel_id=1, source_target_pairs={{0,16},{8,24},{16,0},{24,8},{1,17},{9,25},{17,1},{25,9},{2,18},{10... | collective-permute-start | bytes 270344 | tf_op jit(solution)/shard_map/ppermute | solution.py:231
  8.1 1.3 %collective-permute-start.2 = (bf16[4,88,128]{2,1,0:T(8,128)(2,1)}, bf16[4,88,128]{2,1,0:T(8,128)(2,1)S(1)}, u32[]{:S(2)}, u32[]{:S(2)}) collective-permute-start(bf16[4,88,128]{2,1,0:T(8,128)(2,1)} %get-tuple-element.20), channel_id=1, source_target_pairs={{0,24},{8,0},{16,8},{24,16},{1,25},{9,1},{17,9},{25,17},{2,26},{10... | collective-permute-start | bytes 270344 | tf_op jit(solution)/shard_map/ppermute | solution.py:231
  9.4 1.6 %collective-permute-done.refs_1_ = bf16[4,88,128]{2,1,0:T(8,128)(2,1)S(1)} collective-permute-done((bf16[4,88,128]{2,1,0:T(8,128)(2,1)}, bf16[4,88,128]{2,1,0:T(8,128)(2,1)S(1)}, u32[]{:S(2)}, u32[]{:S(2)}) %collective-permute-start) | collective-permute-done | bytes 90144 | tf_op jit(solution)/shard_map/ppermute | solution.py:231
  11.0 0.0 copy-start.2
  11.0 3.3 %collective-permute-done.1.refs_2_ = bf16[4,88,128]{2,1,0:T(8,128)(2,1)S(1)} collective-permute-done((bf16[4,88,128]{2,1,0:T(8,128)(2,1)}, bf16[4,88,128]{2,1,0:T(8,128)(2,1)S(1)}, u32[]{:S(2)}, u32[]{:S(2)}) %collective-permute-start.1) | collective-permute-done | bytes 90144 | tf_op jit(solution)/shard_map/ppermute | solution.py:231
  14.3 0.0 copy-start.3
  14.3 0.2 collective-permute-done.2.refs_3_
  14.5 0.0 copy-start.4
  14.5 0.0 copy-done.2
  14.5 0.4 copy-done.3
  15.0 0.2 copy-done.4
  15.2 2.0 %route.1 = bf16[32,88,128]{2,1,0:T(8,128)(2,1)} custom-call(s32[4]{0:T(128)} %owner_ref.9, s32[4]{0:T(128)} %offset_ref.3, bf16[4,88,128]{2,1,0:T(8,128)(2,1)} %get-tuple-element.17.refs_0_, bf16[4,88,128]{2,1,0:T(8,128)(2,1)} %copy-done.2, bf16[4,88,128]{2,1,0:T(8,128)(2,1)} %copy-done.3, bf16[4,88,128]{2,1,0:T(8,128)(2,1)} %copy-done.4), custom_call_target="tpu_custom_call" | custom-call | tf_op jit(solution)/shard_map/route/pallas_call | solution.py:242
  17.2 5.5 %all-to-all-start = ((bf16[32,88,128]{2,1,0:T(8,128)(2,1)}), bf16[32,88,128]{2,1,0:T(8,128)(2,1)S(1)}, u32[]{:S(2)}, u32[]{:S(2)}) async-start(bf16[32,88,128]{2,1,0:T(8,128)(2,1)} %route.1), calls=%async_computation | async-start | bytes 1441792 | tf_op jit(solution)/shard_map/all_to_all | solution.py:250
  22.8 2.9 %prepare.1 = (bf16[576,576]{1,0:T(8,128)(2,1)}, f32[576,576]{1,0:T(8,128)}) custom-call(s32[1]{0:T(128)} %bitcast.group_ref, s32[4]{0:T(128)} %owner_ref.9, bf16[576,576]{1,0:T(8,128)(2,1)} %bitcast.22, bf16[576,576]{1,0:T(8,128)(2,1)} %bitcast.24, bf16[576,576]{1,0:T(8,128)(2,1)} %bitcast.26), custom_call_target="tpu_custom_call" | custom-call | flops 764411904 | bytes 3981312 | tf_op jit(solution)/shard_map/prepare/pallas_call | solution.py:234
  25.7 16.2 %all-to-all-done.arrived = bf16[32,88,128]{2,1,0:T(8,128)(2,1)S(1)} async-done(((bf16[32,88,128]{2,1,0:T(8,128)(2,1)}), bf16[32,88,128]{2,1,0:T(8,128)(2,1)S(1)}, u32[]{:S(2)}, u32[]{:S(2)}) %all-to-all-start) | async-done | bytes 720928 | tf_op jit(solution)/shard_map/all_to_all | solution.py:250
  42.0 0.9 %copy-done = bf16[32,88,128]{2,1,0:T(8,128)(2,1)} copy-done((bf16[32,88,128]{2,1,0:T(8,128)(2,1)}, bf16[32,88,128]{2,1,0:T(8,128)(2,1)S(1)}, u32[]{:S(2)}) %copy-start) | copy-done | bytes 720920
  42.8 4.3 %owner_step.1 = (bf16[576,576]{1,0:T(8,128)(2,1)}, f32[576,576]{1,0:T(8,128)}, bf16[8,72,144]{2,1,0:T(8,128)(2,1)}) custom-call(s32[1]{0:T(128)} %bitcast.group_ref, s32[1]{0:T(128)} %bitcast.1.me_ref.share_ref, s32[4]{0:T(128)} %owner_ref.9, bf16[32,88,128]{2,1,0:T(8,128)(2,1)} %copy-done, bf16[576,576]{1,0:T(8,128)(2,1)} %bitcast.23, ...), custom_call_target="tpu_custom_call" | custom-call | flops 1146617856 | bytes 5971968 | tf_op jit(solution)/shard_map/owner_step/pallas_call | solution.py:251
  47.1 6.9 %all-to-all-start.1 = ((bf16[8,72,144]{2,1,0:T(8,128)(2,1)}), bf16[8,72,144]{2,1,0:T(8,128)(2,1)S(1)}, u32[]{:S(2)}, u32[]{:S(2)}) async-start(bf16[8,72,144]{2,1,0:T(8,128)(2,1)} %get-tuple-element.23), calls=%async_computation.1 | async-start | bytes 589824 | tf_op jit(solution)/shard_map/all_to_all | solution.py:264
  54.0 2.8 %factors.1 = (f32[144,576]{1,0:T(8,128)}, f32[144,576]{1,0:T(8,128)}, bf16[576,576]{1,0:T(8,128)(2,1)}) custom-call(s32[1]{0:T(128)} %bitcast.group_ref, s32[1]{0:T(128)} %bitcast.1.me_ref.share_ref, s32[4]{0:T(128)} %owner_ref.9, bf16[576,576]{1,0:T(8,128)(2,1)} %get-tuple-element.24.gradient, f32[144,576]{1,0:T(8,128)} %bitcast.28, f32[144,576]{1,0:T(8,128)} %bitcast.29, ...), custom_call_target="tpu_custom_call" | custom-call | flops 382205952 | bytes 2654208 | tf_op jit(solution)/shard_map/factors/pallas_call | solution.py:265
  56.7 4.5 %all-to-all-done.1.returned = bf16[8,72,144]{2,1,0:T(8,128)(2,1)S(1)} async-done(((bf16[8,72,144]{2,1,0:T(8,128)(2,1)}), bf16[8,72,144]{2,1,0:T(8,128)(2,1)S(1)}, u32[]{:S(2)}, u32[]{:S(2)}) %all-to-all-start.1) | async-done | bytes 165920 | tf_op jit(solution)/shard_map/all_to_all | solution.py:264
  61.2 0.7 %copy-done.1 = bf16[8,72,144]{2,1,0:T(8,128)(2,1)} copy-done((bf16[8,72,144]{2,1,0:T(8,128)(2,1)}, bf16[8,72,144]{2,1,0:T(8,128)(2,1)S(1)}, u32[]{:S(2)}) %copy-start.1) | copy-done | bytes 165912
  61.9 1.6 %place.1 = bf16[4,72,144]{2,1,0:T(8,128)(2,1)} custom-call(s32[4]{0:T(128)} %owner_ref.9, s32[4]{0:T(128)} %offset_ref.3, bf16[8,72,144]{2,1,0:T(8,128)(2,1)} %copy-done.1), custom_call_target="tpu_custom_call" | custom-call | tf_op jit(solution)/shard_map/place/pallas_call | solution.py:273
  (2 shorter events, 0.0 us)
Async XLA Ops:
  2.4 8.6 %collective-permute-start = (bf16[4,88,128]{2,1,0:T(8,128)(2,1)}, bf16[4,88,128]{2,1,0:T(8,128)(2,1)S(1)}, u32[]{:S(2)}, u32[]{:S(2)}) collective-permute-start(bf16[4,88,128]{2,1,0:T(8,128)(2,1)} %get-tuple-element.18), channel_id=1, source_target_pairs={{0,8},{8,16},{16,24},{24,0},{1,9},{9,17},{17,25},{25,1},{2,10},{10... | collective-permute-start | bytes 270344 | tf_op jit(solution)/shard_map/ppermute | solution.py:231
  5.5 8.9 %collective-permute-start.1 = (bf16[4,88,128]{2,1,0:T(8,128)(2,1)}, bf16[4,88,128]{2,1,0:T(8,128)(2,1)S(1)}, u32[]{:S(2)}, u32[]{:S(2)}) collective-permute-start(bf16[4,88,128]{2,1,0:T(8,128)(2,1)} %get-tuple-element.19), channel_id=1, source_target_pairs={{0,16},{8,24},{16,0},{24,8},{1,17},{9,25},{17,1},{25,9},{2,18},{10... | collective-permute-start | bytes 270344 | tf_op jit(solution)/shard_map/ppermute | solution.py:231
  8.1 6.5 %collective-permute-start.2 = (bf16[4,88,128]{2,1,0:T(8,128)(2,1)}, bf16[4,88,128]{2,1,0:T(8,128)(2,1)S(1)}, u32[]{:S(2)}, u32[]{:S(2)}) collective-permute-start(bf16[4,88,128]{2,1,0:T(8,128)(2,1)} %get-tuple-element.20), channel_id=1, source_target_pairs={{0,24},{8,0},{16,8},{24,16},{1,25},{9,1},{17,9},{25,17},{2,26},{10... | collective-permute-start | bytes 270344 | tf_op jit(solution)/shard_map/ppermute | solution.py:231
  11.0 3.5 %copy-start.2 = (bf16[4,88,128]{2,1,0:T(8,128)(2,1)}, bf16[4,88,128]{2,1,0:T(8,128)(2,1)S(1)}, u32[]{:S(2)}) copy-start(bf16[4,88,128]{2,1,0:T(8,128)(2,1)S(1)} %collective-permute-done.refs_1_) | copy-start | bytes 270340
  14.3 0.6 %copy-start.3 = (bf16[4,88,128]{2,1,0:T(8,128)(2,1)}, bf16[4,88,128]{2,1,0:T(8,128)(2,1)S(1)}, u32[]{:S(2)}) copy-start(bf16[4,88,128]{2,1,0:T(8,128)(2,1)S(1)} %collective-permute-done.1.refs_2_) | copy-start | bytes 270340
  14.5 0.6 %copy-start.4 = (bf16[4,88,128]{2,1,0:T(8,128)(2,1)}, bf16[4,88,128]{2,1,0:T(8,128)(2,1)S(1)}, u32[]{:S(2)}) copy-start(bf16[4,88,128]{2,1,0:T(8,128)(2,1)S(1)} %collective-permute-done.2.refs_3_) | copy-start | bytes 270340
  17.2 24.7 %all-to-all-start = ((bf16[32,88,128]{2,1,0:T(8,128)(2,1)}), bf16[32,88,128]{2,1,0:T(8,128)(2,1)S(1)}, u32[]{:S(2)}, u32[]{:S(2)}) async-start(bf16[32,88,128]{2,1,0:T(8,128)(2,1)} %route.1), calls=%async_computation | async-start | bytes 1441792 | tf_op jit(solution)/shard_map/all_to_all | solution.py:250
  41.9 0.9 %copy-start = (bf16[32,88,128]{2,1,0:T(8,128)(2,1)}, bf16[32,88,128]{2,1,0:T(8,128)(2,1)S(1)}, u32[]{:S(2)}) copy-start(bf16[32,88,128]{2,1,0:T(8,128)(2,1)S(1)} %all-to-all-done.arrived) | copy-start | bytes 2162692
  47.1 14.1 %all-to-all-start.1 = ((bf16[8,72,144]{2,1,0:T(8,128)(2,1)}), bf16[8,72,144]{2,1,0:T(8,128)(2,1)S(1)}, u32[]{:S(2)}, u32[]{:S(2)}) async-start(bf16[8,72,144]{2,1,0:T(8,128)(2,1)} %get-tuple-element.23), calls=%async_computation.1 | async-start | bytes 589824 | tf_op jit(solution)/shard_map/all_to_all | solution.py:264
  61.2 0.7 %copy-start.1 = (bf16[8,72,144]{2,1,0:T(8,128)(2,1)}, bf16[8,72,144]{2,1,0:T(8,128)(2,1)S(1)}, u32[]{:S(2)}) copy-start(bf16[8,72,144]{2,1,0:T(8,128)(2,1)S(1)} %all-to-all-done.1.returned) | copy-start | bytes 497668

commit v2 on v1

--- a/solution.py
+++ b/solution.py
@@ -9,6 +9,7 @@
 SUBLANES = 8
 VMEM = pl.BlockSpec(memory_space=pltpu.VMEM)
 SMEM = pl.BlockSpec(memory_space=pltpu.SMEM)
+VMEM_GRANT = 16 * 2**20
 
 def contract_first(matrix_a, matrix_b):
     return lax.dot_general(
@@ -107,8 +108,9 @@
 
 
 def owner_kernel(
-    group_ref, share_ref, owner_ref, arrived, lbasis, rbasis, lbasis_t, old_part, second,
-    gradient, new_second, back, turned, unrotated,
+    group_ref, share_ref, owner_ref, arrived, lbasis, rbasis, lbasis_t, old_part, second, moment,
+    left_t, right_t, back, new_second, new_moment, new_left_t, new_right_t, gradient, turned,
+    unrotated,
 ):
     _, found = slot_of(owner_ref, group_ref[0])
     groups, rows, col_share = back.shape
@@ -133,43 +135,26 @@
                     gradient[row : row + SUBLANES, tail:] = arrived[
                         piece, below : below + SUBLANES, beside : beside + half
                     ]
+        first = pl.multiple_of(share_ref[0] * col_share, 16)
+        own = pl.ds(first, col_share)
         turned[...] = matmul(lbasis_t[...], gradient[...]).astype(jnp.bfloat16)
         cut = 2 * LANES
-        for first in range(0, columns, cut):
-            cols = slice(first, min(first + cut, columns))
+        for low in range(0, columns, cut):
+            cols = slice(low, min(low + cut, columns))
             rotated = matmul(turned[...], rbasis[:, cols])
             fresh = 0.95 * second[:, cols] + 0.05 * rotated * rotated
             new_second[:, cols] = fresh
             rotated_mom = old_part[:, cols] + 0.1 * rotated
             scaled = (rotated_mom / (jnp.sqrt(fresh) + 1e-08)).astype(jnp.bfloat16)
             unrotated[:, cols] = matmul(lbasis[...], scaled).astype(jnp.bfloat16)
-        own = pl.ds(pl.multiple_of(share_ref[0] * col_share, 16), col_share)
         result = contract_last(unrotated[...], rbasis[own, :]).astype(jnp.bfloat16)
         for m in range(groups):
             back[m] = result[m * rows : (m + 1) * rows]
-
-    @pl.when(found == 0)
-    def _():
-        new_second[...] = second[...]
-
-
-def factor_kernel(
-    group_ref, share_ref, owner_ref, gradient, left_t, right_t, moment, new_left_t, new_right_t,
-    new_moment,
-):
-    _, found = slot_of(owner_ref, group_ref[0])
-    col_share, columns = left_t.shape
-
-    @pl.when(found == 1)
-    def _():
-        first = pl.multiple_of(share_ref[0] * col_share, 16)
         grad = gradient[...]
-        new_left_t[...] = 0.95 * left_t[...] + 0.05 * contract_last(
-            gradient[pl.ds(first, col_share), :], grad
-        )
-        rows = lax.broadcasted_iota(jnp.int32, (col_share, columns), 0) + first
-        cols = lax.broadcasted_iota(jnp.int32, (col_share, columns), 1)
-        pick = jnp.where(rows == cols, 1.0, 0.0).astype(jnp.bfloat16)
+        new_left_t[...] = 0.95 * left_t[...] + 0.05 * contract_last(gradient[own, :], grad)
+        picked = lax.broadcasted_iota(jnp.int32, (col_share, columns), 0) + first
+        places = lax.broadcasted_iota(jnp.int32, (col_share, columns), 1)
+        pick = jnp.where(picked == places, 1.0, 0.0).astype(jnp.bfloat16)
         grad_cols_t = contract_last(pick, grad).astype(jnp.bfloat16)
         new_right_t[...] = 0.95 * right_t[...] + 0.05 * matmul(grad_cols_t, grad)
         new_moment[...] = (
@@ -178,9 +163,10 @@
 
     @pl.when(found == 0)
     def _():
+        new_second[...] = second[...]
+        new_moment[...] = moment[...]
         new_left_t[...] = left_t[...]
         new_right_t[...] = right_t[...]
-        new_moment[...] = moment[...]
 
 
 def place_kernel(owner_ref, offset_ref, returned, update):
@@ -188,10 +174,18 @@
         update[offset_ref[b]] = returned[owner_ref[b]]
 
 
-def cost(flops, *arrays):
-    return pl.CostEstimate(
-        flops=flops, bytes_accessed=sum(a.size * a.dtype.itemsize for a in arrays), transcendentals=0
-    )
+def run(name, kernel, scalars, arrays, outs, scratch=(), flops=0):
+    moved = sum(a.size * a.dtype.itemsize for a in list(arrays) + list(outs))
+    return pl.pallas_call(
+        kernel,
+        out_shape=[pltpu.VMEM(o.shape, o.dtype) for o in outs],
+        in_specs=[SMEM] * len(scalars) + [VMEM] * len(arrays),
+        out_specs=[VMEM] * len(outs),
+        scratch_shapes=[pltpu.VMEM(o.shape, o.dtype) for o in scratch],
+        compiler_params=pltpu.CompilerParams(vmem_limit_bytes=VMEM_GRANT),
+        cost_estimate=pl.CostEstimate(flops=flops, bytes_accessed=moved, transcendentals=0),
+        name=name,
+    )(*scalars, *(pltpu.with_memory_space_constraint(a, pltpu.VMEM) for a in arrays))
 
 
 def per_device_packed(
@@ -220,63 +214,52 @@
     left_t, right_t = left_factor[0].T, right_factor[0].T
     product = 2 * columns**3
 
-    parts = pl.pallas_call(
-        pack_kernel,
-        out_shape=[packed] * replicas,
-        in_specs=[SMEM, VMEM],
-        out_specs=[VMEM] * replicas,
-        name="pack",
-    )(share, pieces)
+    parts = run("pack", pack_kernel, [share], [pieces], [packed] * replicas)
     parts = [parts[0]] + [
         lax.ppermute(parts[s], "dp", [(i, (i + s) % replicas) for i in range(replicas)])
         for s in range(1, replicas)
     ]
-    lbasis_t, old_part = pl.pallas_call(
+    lbasis_t, old_part = run(
+        "prepare",
         prepare_kernel,
-        out_shape=[shape(square, bf16), shape(square, f32)],
-        in_specs=[SMEM, SMEM] + [VMEM] * 3,
-        out_specs=[VMEM] * 2,
-        cost_estimate=cost(2 * product, lbasis, rbasis, moment, lbasis, second),
-        name="prepare",
-    )(group, owner, lbasis, rbasis, moment)
-    outgoing = pl.pallas_call(
+        [group, owner],
+        [lbasis, rbasis, moment],
+        [shape(square, bf16), shape(square, f32)],
+        flops=2 * product,
+    )
+    parts, lbasis_t, old_part = lax.optimization_barrier((parts, lbasis_t, old_part))
+    (outgoing,) = run(
+        "route",
         route_kernel,
-        out_shape=shape((replicas * groups,) + packed.shape[1:], bf16),
-        in_specs=[SMEM, SMEM] + [VMEM] * replicas,
-        out_specs=VMEM,
-        scratch_shapes=[pltpu.VMEM(packed.shape, bf16)],
-        name="route",
-    )(owner, offset, *parts)
+        [owner, offset],
+        parts,
+        [shape((replicas * groups,) + packed.shape[1:], bf16)],
+        scratch=[packed],
+    )
     arrived = lax.all_to_all(outgoing, ("dp", "mp"), split_axis=0, concat_axis=0, tiled=True)
-    gradient, new_second, back = pl.pallas_call(
+    back, new_second, new_moment, new_left_t, new_right_t = run(
+        "owner_step",
         owner_kernel,
-        out_shape=[
+        [group, share, owner],
+        [arrived, lbasis, rbasis, lbasis_t, old_part, second, moment, left_t, right_t],
+        [
+            shape((groups, rows, col_share), bf16),
+            shape(square, f32),
             shape(square, bf16),
-            shape(square, f32),
-            shape((groups, rows, col_share), bf16),
+            shape(left_t.shape, f32),
+            shape(right_t.shape, f32),
         ],
-        in_specs=[SMEM] * 3 + [VMEM] * 6,
-        out_specs=[VMEM] * 3,
-        scratch_shapes=[pltpu.VMEM(square, bf16), pltpu.VMEM(square, bf16)],
-        cost_estimate=cost(3 * product, lbasis, rbasis, lbasis_t, old_part, second, second),
-        name="owner_step",
-    )(group, share, owner, arrived, lbasis, rbasis, lbasis_t, old_part, second)
+        scratch=[shape(square, bf16)] * 3,
+        flops=4 * product,
+    )
     returned = lax.all_to_all(back, "mp", split_axis=0, concat_axis=0, tiled=True)
-    new_left_t, new_right_t, new_moment = pl.pallas_call(
-        factor_kernel,
-        out_shape=[shape(left_t.shape, f32), shape(right_t.shape, f32), shape(square, bf16)],
-        in_specs=[SMEM] * 3 + [VMEM] * 4,
-        out_specs=[VMEM] * 3,
-        cost_estimate=cost(product, left_t, left_t, right_t, right_t, moment, moment),
-        name="factors",
-    )(group, share, owner, gradient, left_t, right_t, moment)
-    update = pl.pallas_call(
+    (update,) = run(
+        "place",
         place_kernel,
-        out_shape=shape((blocks, rows, col_share), bf16),
-        in_specs=[SMEM, SMEM, VMEM],
-        out_specs=VMEM,
-        name="place",
-    )(owner, offset, returned)
+        [owner, offset],
+        [returned],
+        [shape((blocks, rows, col_share), bf16)],
+    )
     return (
         update,
         new_left_t.T[None],

time: 63.9 us -> 56.6 us (0.89)
  blocking collectives: 0 us -> 23.4 us
  waiting for transfers between devices: 25.8 us -> 3.75 us
  starting transfers between devices: 19.4 us -> 10.4 us
  local copies, waits for them, and re-layouts: 2.21 us -> 9.13 us
  Pallas kernels: 15.5 us -> 8.71 us
    all_to_all x0 -> x1, blocking collectives: none -> 23.4 us  [per_device_packed(): lax.all_to_all(outgoing, ('dp', 'mp'), split_axis=0, concat_axis=0, tiled...]
    all_to_all x1 -> x0, waiting for transfers between devices: 16.2 us -> none  [per_device_packed(): lax.all_to_all(outgoing, ('dp', 'mp'), split_axis=0, concat_axis=0, tiled...]
    unnamed x10 -> x29, local copies, waits for them, and re-layouts: 2.21 us -> 9.13 us
    pallas_call x6 -> x5, Pallas kernels: 15.5 us -> 8.71 us  [run(): pl.pallas_call(kernel, out_shape=[pltpu.VMEM(o.shape, o.dtype) for o in o...]
    all_to_all x1 -> x0, starting transfers between devices: 5.55 us -> none  [per_device_packed(): lax.all_to_all(outgoing, ('dp', 'mp'), split_axis=0, concat_axis=0, tiled...]
    ppermute x3, waiting for transfers between devices: 5.11 us -> 0.01 us  [per_device_packed(): lax.ppermute(parts[s], 'dp', [(i, (i + s) % replicas) for i in range(repl...]
    all_to_all x1, starting transfers between devices: 6.86 us -> 3.42 us  [per_device_packed(): lax.all_to_all(back, 'mp', split_axis=0, concat_axis=0, tiled=True)]
    all_to_all x1, waiting for transfers between devices: 4.46 us -> 3.74 us  [per_device_packed(): lax.all_to_all(back, 'mp', split_axis=0, concat_axis=0, tiled=True)]
  transfers between devices with their start and end apart: 5 -> 4, of which waited for: 5 -> 1; matrix products, arithmetic and copies ran while one was open for 0% -> 6% of each run, Pallas kernels for 9% -> 4%
where the time goes in v2:
time: 56.6 us; the launch traced here: 56.2 us
  blocking collectives  23.4 us (41%)
  starting transfers between devices  10.4 us (18%)
  local copies, waits for them, and re-layouts  9.13 us (16%)
  Pallas kernels  8.71 us (15%)
  waiting for transfers between devices  3.75 us (7%)
  between operations  0.77 us (1%)
    all_to_all x1, blocking collectives, per_device_packed(): lax.all_to_all(outgoing, ('dp', 'mp'), split_axis=0, concat_axis=0, tiled...  23.4 us
    unnamed x29, local copies, waits for them, and re-layouts  9.13 us
    pallas_call x5, Pallas kernels, run(): pl.pallas_call(kernel, out_shape=[pltpu.VMEM(o.shape, o.dtype) for o in o...  8.71 us
    ppermute x3, starting transfers between devices, per_device_packed(): lax.ppermute(parts[s], 'dp', [(i, (i + s) % replicas) for i in range(repl...  7.02 us
    all_to_all x1, waiting for transfers between devices, per_device_packed(): lax.all_to_all(back, 'mp', split_axis=0, concat_axis=0, tiled=True)  3.74 us
    all_to_all x1, starting transfers between devices, per_device_packed(): lax.all_to_all(back, 'mp', split_axis=0, concat_axis=0, tiled=True)  3.42 us
  transfers between devices with their start and end apart: 4, of which 1 were waited for; matrix products, arithmetic and copies ran while one was open for 6% of the time, Pallas kernels for 4%

profile of v2, /device:TPU:0, one launch (start us, length us, event | category | flops | bytes accessed | tf_op | source)
XLA Modules:
  0.0 56.2 jit_solution(1680985554022368825)
XLA Ops:
  0.6 1.0 %copy-done.6 = bf16[1,4,72,576]{3,2,1,0:T(8,128)(2,1)S(1)} copy-done((bf16[1,4,72,576]{3,2,1,0:T(8,128)(2,1)S(1)}, bf16[1,4,72,576]{3,2,1,0:T(8,128)(2,1)}, u32[]{:S(2)}) %copy-start.6) | copy-done | bytes 331800
  1.6 0.1 pack.1
  1.8 3.1 %collective-permute-start = (bf16[4,88,128]{2,1,0:T(8,128)(2,1)S(1)}, bf16[4,88,128]{2,1,0:T(8,128)(2,1)S(1)}, u32[]{:S(2)}, u32[]{:S(2)}) collective-permute-start(bf16[4,88,128]{2,1,0:T(8,128)(2,1)S(1)} %get-tuple-element.23), channel_id=1, source_target_pairs={{0,8},{8,16},{16,24},{24,0},{1,9},{9,17},{17,25},{25,1},{2,10},{10... | collective-permute-start | bytes 270344 | tf_op jit(solution)/shard_map/ppermute | solution.py:219
  4.9 2.6 %collective-permute-start.1 = (bf16[4,88,128]{2,1,0:T(8,128)(2,1)S(1)}, bf16[4,88,128]{2,1,0:T(8,128)(2,1)S(1)}, u32[]{:S(2)}, u32[]{:S(2)}) collective-permute-start(bf16[4,88,128]{2,1,0:T(8,128)(2,1)S(1)} %get-tuple-element.24), channel_id=1, source_target_pairs={{0,16},{8,24},{16,0},{24,8},{1,17},{9,25},{17,1},{25,9},{2,18},{10... | collective-permute-start | bytes 270344 | tf_op jit(solution)/shard_map/ppermute | solution.py:219
  7.4 1.3 %collective-permute-start.2 = (bf16[4,88,128]{2,1,0:T(8,128)(2,1)S(1)}, bf16[4,88,128]{2,1,0:T(8,128)(2,1)S(1)}, u32[]{:S(2)}, u32[]{:S(2)}) collective-permute-start(bf16[4,88,128]{2,1,0:T(8,128)(2,1)S(1)} %get-tuple-element.25), channel_id=1, source_target_pairs={{0,24},{8,0},{16,8},{24,16},{1,25},{9,1},{17,9},{25,17},{2,26},{10... | collective-permute-start | bytes 270344 | tf_op jit(solution)/shard_map/ppermute | solution.py:219
  8.8 1.1 %copy-done.1 = bf16[1,576,576]{2,1,0:T(8,128)(2,1)S(1)} copy-done((bf16[1,576,576]{2,1,0:T(8,128)(2,1)S(1)}, bf16[1,576,576]{2,1,0:T(8,128)(2,1)}, u32[]{:S(2)}) %copy-start.1) | copy-done | bytes 663576
  9.9 1.1 %copy-done.3 = bf16[1,576,576]{2,1,0:T(8,128)(2,1)S(1)} copy-done((bf16[1,576,576]{2,1,0:T(8,128)(2,1)S(1)}, bf16[1,576,576]{2,1,0:T(8,128)(2,1)}, u32[]{:S(2)}) %copy-start.3) | copy-done | bytes 663576
  11.0 1.1 %copy-done.5 = bf16[1,576,576]{2,1,0:T(8,128)(2,1)S(1)} copy-done((bf16[1,576,576]{2,1,0:T(8,128)(2,1)S(1)}, bf16[1,576,576]{2,1,0:T(8,128)(2,1)}, u32[]{:S(2)}) %copy-start.5) | copy-done | bytes 663576
  12.1 0.7 %copy-done.9 = s32[4]{0:T(128)S(1)} copy-done((s32[4]{0:T(128)S(1)}, s32[4]{0:T(128)}, u32[]{:S(2)}) %copy-start.9) | copy-done | bytes 40
  12.8 2.0 %prepare.1 = (bf16[576,576]{1,0:T(8,128)(2,1)S(1)}, f32[576,576]{1,0:T(8,128)S(1)}) custom-call(s32[1]{0:T(128)} %bitcast.group_ref, s32[4]{0:T(128)S(1)} %copy-done.9, bf16[576,576]{1,0:T(8,128)(2,1)S(1)} %bitcast.26, bf16[576,576]{1,0:T(8,128)(2,1)S(1)} %bitcast.28, bf16[576,576]{1,0:T(8,128)(2,1)S(1)} %bitcast.30), custom_call_target="tpu_custom_call" | custom-call | flops 764411904 | bytes 3981312 | tf_op jit(solution)/shard_map/prepare/pallas_call | solution.py:179
  14.9 0.0 copy-start
  14.9 0.0 copy-start.2
  14.9 0.0 copy-start.10
  14.9 0.7 %route.1 = bf16[32,88,128]{2,1,0:T(8,128)(2,1)S(1)} custom-call(s32[4]{0:T(128)S(1)} %copy-done.9, s32[4]{0:T(128)S(1)} %copy-done.11, bf16[4,88,128]{2,1,0:T(8,128)(2,1)S(1)} %get-tuple-element.28.refs_0_, bf16[4,88,128]{2,1,0:T(8,128)(2,1)S(1)} %collective-permute-done.refs_1_, bf16[4,88,128]{2,1,0:T(8,128)(2,1)S(1)} %collective-permute-done.1.refs_2_, ...), custom_call_target="tpu_custom_call" | custom-call | bytes 1081344 | tf_op jit(solution)/shard_map/route/pallas_call | solution.py:179
  15.6 23.4 %all_to_all.10.arrived = bf16[32,88,128]{2,1,0:T(8,128)(2,1)S(1)} all-to-all(bf16[32,88,128]{2,1,0:T(8,128)(2,1)S(1)} %route.1), channel_id=1, replica_groups=mesh['dp'=4,'mp'=8] {'dp','mp'}, dimensions={0} | all-to-all | bytes 1441792 | tf_op jit(solution)/shard_map/all_to_all | solution.py:239
  39.0 5.3 %owner_step.1 = (bf16[8,72,144]{2,1,0:T(8,128)(2,1)}, f32[576,576]{1,0:T(8,128)S(1)}, bf16[576,576]{1,0:T(8,128)(2,1)S(1)}, f32[144,576]{1,0:T(8,128)S(1)}, f32[144,576]{1,0:T(8,128)S(1)}) custom-call(s32[1]{0:T(128)} %bitcast.group_ref, s32[1]{0:T(128)} %bitcast.1.me_ref.share_ref, s32[4]{0:T(128)S(1)} %copy-done.10, ...), custom_call_target="tpu_custom_call" | custom-call | flops 1528823808 | bytes 9512960 | tf_op jit(solution)/shard_map/owner_step/pallas_call | solution.py:179
  44.3 3.4 %all-to-all-start.1 = ((bf16[8,72,144]{2,1,0:T(8,128)(2,1)}), bf16[8,72,144]{2,1,0:T(8,128)(2,1)S(1)}, u32[]{:S(2)}, u32[]{:S(2)}) async-start(bf16[8,72,144]{2,1,0:T(8,128)(2,1)} %get-tuple-element.34), calls=%async_computation.1 | async-start | bytes 589824 | tf_op jit(solution)/shard_map/all_to_all | solution.py:255
  47.7 0.7 %copy.15 = f32[1,576,144]{1,2,0:T(8,128)} copy(f32[1,576,144]{1,2,0:T(8,128)S(1)} %bitcast.24) | data formatting | bytes 663552
  48.5 0.7 %copy.16 = f32[1,576,144]{1,2,0:T(8,128)} copy(f32[1,576,144]{1,2,0:T(8,128)S(1)} %bitcast.23) | data formatting | bytes 663552
  49.2 0.9 %copy.17 = bf16[1,576,576]{2,1,0:T(8,128)(2,1)} copy(bf16[1,576,576]{2,1,0:T(8,128)(2,1)S(1)} %bitcast.22) | data formatting | bytes 1327104
  50.1 1.1 %copy.18 = f32[1,576,576]{2,1,0:T(8,128)} copy(f32[1,576,576]{2,1,0:T(8,128)S(1)} %bitcast.21) | data formatting | bytes 2654208
  51.2 3.7 %all-to-all-done.1.returned = bf16[8,72,144]{2,1,0:T(8,128)(2,1)S(1)} async-done(((bf16[8,72,144]{2,1,0:T(8,128)(2,1)}), bf16[8,72,144]{2,1,0:T(8,128)(2,1)S(1)}, u32[]{:S(2)}, u32[]{:S(2)}) %all-to-all-start.1) | async-done | bytes 165920 | tf_op jit(solution)/shard_map/all_to_all | solution.py:255
  54.9 0.6 place.1
  55.5 0.7 %copy.14 = bf16[4,72,144]{2,1,0:T(8,128)(2,1)} copy(bf16[4,72,144]{2,1,0:T(8,128)(2,1)S(1)} %place.1) | data formatting | bytes 165888
  (19 shorter events, 0.0 us)
Async XLA Ops:
  0.6 1.0 %copy-start.6 = (bf16[1,4,72,576]{3,2,1,0:T(8,128)(2,1)S(1)}, bf16[1,4,72,576]{3,2,1,0:T(8,128)(2,1)}, u32[]{:S(2)}) copy-start(bf16[1,4,72,576]{3,2,1,0:T(8,128)(2,1)} %param.9) | copy-start | bytes 995332
  1.8 13.2 %copy-start.11 = (s32[4]{0:T(128)S(1)}, s32[4]{0:T(128)}, u32[]{:S(2)}) copy-start(s32[4]{0:T(128)} %offset_ref.3) | copy-start | bytes 52
  1.8 13.1 %collective-permute-start = (bf16[4,88,128]{2,1,0:T(8,128)(2,1)S(1)}, bf16[4,88,128]{2,1,0:T(8,128)(2,1)S(1)}, u32[]{:S(2)}, u32[]{:S(2)}) collective-permute-start(bf16[4,88,128]{2,1,0:T(8,128)(2,1)S(1)} %get-tuple-element.23), channel_id=1, source_target_pairs={{0,8},{8,16},{16,24},{24,0},{1,9},{9,17},{17,25},{25,1},{2,10},{10... | collective-permute-start | bytes 270344 | tf_op jit(solution)/shard_map/ppermute | solution.py:219
  4.9 10.0 %collective-permute-start.1 = (bf16[4,88,128]{2,1,0:T(8,128)(2,1)S(1)}, bf16[4,88,128]{2,1,0:T(8,128)(2,1)S(1)}, u32[]{:S(2)}, u32[]{:S(2)}) collective-permute-start(bf16[4,88,128]{2,1,0:T(8,128)(2,1)S(1)} %get-tuple-element.24), channel_id=1, source_target_pairs={{0,16},{8,24},{16,0},{24,8},{1,17},{9,25},{17,1},{25,9},{2,18},{10... | collective-permute-start | bytes 270344 | tf_op jit(solution)/shard_map/ppermute | solution.py:219
  7.4 7.5 %collective-permute-start.2 = (bf16[4,88,128]{2,1,0:T(8,128)(2,1)S(1)}, bf16[4,88,128]{2,1,0:T(8,128)(2,1)S(1)}, u32[]{:S(2)}, u32[]{:S(2)}) collective-permute-start(bf16[4,88,128]{2,1,0:T(8,128)(2,1)S(1)} %get-tuple-element.25), channel_id=1, source_target_pairs={{0,24},{8,0},{16,8},{24,16},{1,25},{9,1},{17,9},{25,17},{2,26},{10... | collective-permute-start | bytes 270344 | tf_op jit(solution)/shard_map/ppermute | solution.py:219
  8.8 1.1 %copy-start.1 = (bf16[1,576,576]{2,1,0:T(8,128)(2,1)S(1)}, bf16[1,576,576]{2,1,0:T(8,128)(2,1)}, u32[]{:S(2)}) copy-start(bf16[1,576,576]{2,1,0:T(8,128)(2,1)} %param.14) | copy-start | bytes 1990660
  9.9 1.1 %copy-start.3 = (bf16[1,576,576]{2,1,0:T(8,128)(2,1)S(1)}, bf16[1,576,576]{2,1,0:T(8,128)(2,1)}, u32[]{:S(2)}) copy-start(bf16[1,576,576]{2,1,0:T(8,128)(2,1)} %param.15) | copy-start | bytes 1990660
  11.0 1.1 %copy-start.5 = (bf16[1,576,576]{2,1,0:T(8,128)(2,1)S(1)}, bf16[1,576,576]{2,1,0:T(8,128)(2,1)}, u32[]{:S(2)}) copy-start(bf16[1,576,576]{2,1,0:T(8,128)(2,1)} %param.16) | copy-start | bytes 1990660
  12.1 0.7 %copy-start.9 = (s32[4]{0:T(128)S(1)}, s32[4]{0:T(128)}, u32[]{:S(2)}) copy-start(s32[4]{0:T(128)} %owner_ref.7) | copy-start | bytes 52
  12.8 26.2 %copy-start.4 = (bf16[1,576,576]{2,1,0:T(8,128)(2,1)S(1)}, bf16[1,576,576]{2,1,0:T(8,128)(2,1)}, u32[]{:S(2)}) copy-start(bf16[1,576,576]{2,1,0:T(8,128)(2,1)} %param.15) | copy-start | bytes 1990660
  12.8 26.2 %copy-start.7 = (f32[1,576,144]{1,2,0:T(8,128)S(1)}, f32[1,576,144]{1,2,0:T(8,128)}, u32[]{:S(2)}) copy-start(f32[1,576,144]{1,2,0:T(8,128)} %param.12) | copy-start | bytes 995332
  12.8 26.2 %copy-start.8 = (f32[1,576,144]{1,2,0:T(8,128)S(1)}, f32[1,576,144]{1,2,0:T(8,128)}, u32[]{:S(2)}) copy-start(f32[1,576,144]{1,2,0:T(8,128)} %param.13) | copy-start | bytes 995332
  14.9 24.1 %copy-start = (f32[1,576,576]{2,1,0:T(8,128)S(1)}, f32[1,576,576]{2,1,0:T(8,128)}, u32[]{:S(2)}) copy-start(f32[1,576,576]{2,1,0:T(8,128)} %param.17) | copy-start | bytes 3981316
  14.9 24.1 %copy-start.2 = (bf16[1,576,576]{2,1,0:T(8,128)(2,1)S(1)}, bf16[1,576,576]{2,1,0:T(8,128)(2,1)}, u32[]{:S(2)}) copy-start(bf16[1,576,576]{2,1,0:T(8,128)(2,1)} %param.14) | copy-start | bytes 1990660
  14.9 24.1 %copy-start.10 = (s32[4]{0:T(128)S(1)}, s32[4]{0:T(128)}, u32[]{:S(2)}) copy-start(s32[4]{0:T(128)} %owner_ref.7) | copy-start | bytes 52
  44.3 10.6 %all-to-all-start.1 = ((bf16[8,72,144]{2,1,0:T(8,128)(2,1)}), bf16[8,72,144]{2,1,0:T(8,128)(2,1)S(1)}, u32[]{:S(2)}, u32[]{:S(2)}) async-start(bf16[8,72,144]{2,1,0:T(8,128)(2,1)} %get-tuple-element.34), calls=%async_computation.1 | async-start | bytes 589824 | tf_op jit(solution)/shard_map/all_to_all | solution.py:255

commit v3 on v2

--- a/solution.py
+++ b/solution.py
@@ -10,6 +10,7 @@
 VMEM = pl.BlockSpec(memory_space=pltpu.VMEM)
 SMEM = pl.BlockSpec(memory_space=pltpu.SMEM)
 VMEM_GRANT = 16 * 2**20
+CUT = 2 * LANES
 
 def contract_first(matrix_a, matrix_b):
     return lax.dot_general(
@@ -34,10 +35,13 @@
 
 
 def packed_fits(rows, columns, replicas):
+    width = columns // replicas - LANES
     return (
         columns == replicas * LANES + LANES // 2
         and rows == (2 * replicas + 1) * SUBLANES
-        and rows % SUBLANES == 0
+        and width * replicas == LANES // 2
+        and width % 16 == 0
+        and LANES // width == rows // SUBLANES - 1
     )
 
 
@@ -96,7 +100,9 @@
             out[r * groups + group] = piece
 
 
-def prepare_kernel(group_ref, owner_ref, lbasis, rbasis, moment, lbasis_t, turned_back):
+def prepare_kernel(
+    group_ref, share_ref, owner_ref, lbasis, rbasis, moment, lbasis_t, old_part, back_basis
+):
     _, found = slot_of(owner_ref, group_ref[0])
 
     @pl.when(found == 1)
@@ -104,54 +110,94 @@
         transposed = lbasis[...].T
         lbasis_t[...] = transposed
         turned = matmul(transposed, moment[...]).astype(jnp.bfloat16)
-        turned_back[...] = 0.9 * matmul(turned, rbasis[...])
+        old_part[...] = 0.9 * matmul(turned, rbasis[...])
+        columns = rbasis.shape[0]
+        col_share = columns // (columns // LANES)
+        tail = col_share - LANES
+        first = pl.multiple_of(share_ref[0] * col_share, tail)
+        main = rbasis[pl.ds(first, LANES), :]
+        last = rbasis[pl.ds(pl.multiple_of(first + LANES, tail), tail), :]
+        back_basis[...] = jnp.concatenate([main] + [last] * (LANES // tail), axis=0).T
+
+
+def assemble(arrived, gradient, groups, rows):
+    half = LANES // 2
+    tail = gradient.shape[1] - half
+    for r in range(arrived.shape[0] // groups):
+        start = tail_start(r)
+        for m in range(groups):
+            piece = r * groups + m
+            base = m * rows
+            gradient[base : base + rows, r * LANES : (r + 1) * LANES] = arrived[piece, :rows, :]
+            for g in range(3 if r == 0 else 2):
+                row = base + (start + g) * SUBLANES
+                below = rows + (g % 2) * SUBLANES
+                beside = (g // 2) * half
+                gradient[row : row + SUBLANES, tail:] = arrived[
+                    piece, below : below + SUBLANES, beside : beside + half
+                ]
 
 
 def owner_kernel(
-    group_ref, share_ref, owner_ref, arrived, lbasis, rbasis, lbasis_t, old_part, second, moment,
-    left_t, right_t, back, new_second, new_moment, new_left_t, new_right_t, gradient, turned,
-    unrotated,
+    group_ref, owner_ref, arrived, lbasis, rbasis, lbasis_t, old_part, back_basis, second,
+    back, gradient, new_second, turned,
 ):
     _, found = slot_of(owner_ref, group_ref[0])
-    groups, rows, col_share = back.shape
+    groups = back.shape[0]
     columns = gradient.shape[1]
-    replicas = arrived.shape[0] // groups
-    half = LANES // 2
-    tail = columns - half
+    rows = columns // groups
 
     @pl.when(found == 1)
     def _():
-        for r in range(replicas):
-            start = tail_start(r)
-            count = 3 if r == 0 else 2
-            for m in range(groups):
-                piece = r * groups + m
-                base = m * rows
-                gradient[base : base + rows, r * LANES : (r + 1) * LANES] = arrived[piece, :rows, :]
-                for g in range(count):
-                    row = base + (start + g) * SUBLANES
-                    below = rows + (g % 2) * SUBLANES
-                    beside = (g // 2) * half
-                    gradient[row : row + SUBLANES, tail:] = arrived[
-                        piece, below : below + SUBLANES, beside : beside + half
-                    ]
-        first = pl.multiple_of(share_ref[0] * col_share, 16)
-        own = pl.ds(first, col_share)
+        assemble(arrived, gradient, groups, rows)
         turned[...] = matmul(lbasis_t[...], gradient[...]).astype(jnp.bfloat16)
-        cut = 2 * LANES
-        for low in range(0, columns, cut):
-            cols = slice(low, min(low + cut, columns))
+        total = None
+        for low in range(0, columns, CUT):
+            cols = slice(low, min(low + CUT, columns))
             rotated = matmul(turned[...], rbasis[:, cols])
             fresh = 0.95 * second[:, cols] + 0.05 * rotated * rotated
             new_second[:, cols] = fresh
             rotated_mom = old_part[:, cols] + 0.1 * rotated
             scaled = (rotated_mom / (jnp.sqrt(fresh) + 1e-08)).astype(jnp.bfloat16)
-            unrotated[:, cols] = matmul(lbasis[...], scaled).astype(jnp.bfloat16)
-        result = contract_last(unrotated[...], rbasis[own, :]).astype(jnp.bfloat16)
+            term = matmul(scaled, back_basis[cols, :])
+            total = term if total is None else total + term
+        result = matmul(lbasis[...], total.astype(jnp.bfloat16))
+        lane = lax.broadcasted_iota(jnp.int32, (SUBLANES, LANES), 1)
+        tail_groups = rows // SUBLANES - 1
+        width = LANES // tail_groups
         for m in range(groups):
-            back[m] = result[m * rows : (m + 1) * rows]
+            base = m * rows
+            back[m, :rows, :] = result[base : base + rows, :LANES].astype(jnp.bfloat16)
+            mixed = result[base : base + SUBLANES, LANES:]
+            for g in range(1, tail_groups):
+                row = base + g * SUBLANES
+                mixed = jnp.where(
+                    lane < g * width, mixed, result[row : row + SUBLANES, LANES:]
+                )
+            back[m, rows : rows + SUBLANES, :] = mixed.astype(jnp.bfloat16)
+            back[m, rows + SUBLANES :, :] = result[
+                base + rows - SUBLANES : base + rows, LANES:
+            ].astype(jnp.bfloat16)
+
+    @pl.when(found == 0)
+    def _():
+        new_second[...] = second[...]
+
+
+def factor_kernel(
+    group_ref, share_ref, owner_ref, gradient, left_t, right_t, moment, new_left_t, new_right_t,
+    new_moment,
+):
+    _, found = slot_of(owner_ref, group_ref[0])
+    col_share, columns = left_t.shape
+
+    @pl.when(found == 1)
+    def _():
+        first = pl.multiple_of(share_ref[0] * col_share, 16)
         grad = gradient[...]
-        new_left_t[...] = 0.95 * left_t[...] + 0.05 * contract_last(gradient[own, :], grad)
+        new_left_t[...] = 0.95 * left_t[...] + 0.05 * contract_last(
+            gradient[pl.ds(first, col_share), :], grad
+        )
         picked = lax.broadcasted_iota(jnp.int32, (col_share, columns), 0) + first
         places = lax.broadcasted_iota(jnp.int32, (col_share, columns), 1)
         pick = jnp.where(picked == places, 1.0, 0.0).astype(jnp.bfloat16)
@@ -163,22 +209,30 @@
 
     @pl.when(found == 0)
     def _():
-        new_second[...] = second[...]
-        new_moment[...] = moment[...]
         new_left_t[...] = left_t[...]
         new_right_t[...] = right_t[...]
+        new_moment[...] = moment[...]
 
 
 def place_kernel(owner_ref, offset_ref, returned, update):
-    for b in range(update.shape[0]):
-        update[offset_ref[b]] = returned[owner_ref[b]]
-
-
-def run(name, kernel, scalars, arrays, outs, scratch=(), flops=0):
+    blocks, rows, col_share = update.shape
+    tail_groups = rows // SUBLANES - 1
+    width = col_share - LANES
+    for b in range(blocks):
+        place, slot = offset_ref[b], owner_ref[b]
+        update[place, :, :LANES] = returned[slot, :rows, :]
+        for g in range(tail_groups):
+            update[place, g * SUBLANES : (g + 1) * SUBLANES, LANES:] = returned[
+                slot, rows : rows + SUBLANES, g * width : (g + 1) * width
+            ]
+        update[place, rows - SUBLANES :, LANES:] = returned[slot, rows + SUBLANES :, :width]
+
+
+def run(name, kernel, scalars, arrays, outs, scratch=(), flops=0, keep=True):
     moved = sum(a.size * a.dtype.itemsize for a in list(arrays) + list(outs))
     return pl.pallas_call(
         kernel,
-        out_shape=[pltpu.VMEM(o.shape, o.dtype) for o in outs],
+        out_shape=[pltpu.VMEM(o.shape, o.dtype) for o in outs] if keep else list(outs),
         in_specs=[SMEM] * len(scalars) + [VMEM] * len(arrays),
         out_specs=[VMEM] * len(outs),
         scratch_shapes=[pltpu.VMEM(o.shape, o.dtype) for o in scratch],
@@ -219,15 +273,17 @@
         lax.ppermute(parts[s], "dp", [(i, (i + s) % replicas) for i in range(replicas)])
         for s in range(1, replicas)
     ]
-    lbasis_t, old_part = run(
+    lbasis_t, old_part, back_basis = run(
         "prepare",
         prepare_kernel,
-        [group, owner],
+        [group, share, owner],
         [lbasis, rbasis, moment],
-        [shape(square, bf16), shape(square, f32)],
+        [shape(square, bf16), shape(square, f32), shape((columns, 2 * LANES), bf16)],
         flops=2 * product,
     )
-    parts, lbasis_t, old_part = lax.optimization_barrier((parts, lbasis_t, old_part))
+    parts, lbasis_t, old_part, back_basis = lax.optimization_barrier(
+        (parts, lbasis_t, old_part, back_basis)
+    )
     (outgoing,) = run(
         "route",
         route_kernel,
@@ -237,28 +293,36 @@
         scratch=[packed],
     )
     arrived = lax.all_to_all(outgoing, ("dp", "mp"), split_axis=0, concat_axis=0, tiled=True)
-    back, new_second, new_moment, new_left_t, new_right_t = run(
+    back, gradient, new_second = run(
         "owner_step",
         owner_kernel,
+        [group, owner],
+        [arrived, lbasis, rbasis, lbasis_t, old_part, back_basis, second],
+        [
+            shape((groups, rows + 2 * SUBLANES, LANES), bf16),
+            shape(square, bf16),
+            shape(square, f32),
+        ],
+        scratch=[shape(square, bf16)],
+        flops=3 * product,
+    )
+    returned = lax.all_to_all(back, "mp", split_axis=0, concat_axis=0, tiled=True)
+    new_left_t, new_right_t, new_moment = run(
+        "factors",
+        factor_kernel,
         [group, share, owner],
-        [arrived, lbasis, rbasis, lbasis_t, old_part, second, moment, left_t, right_t],
-        [
-            shape((groups, rows, col_share), bf16),
-            shape(square, f32),
-            shape(square, bf16),
-            shape(left_t.shape, f32),
-            shape(right_t.shape, f32),
-        ],
-        scratch=[shape(square, bf16)] * 3,
-        flops=4 * product,
-    )
-    returned = lax.all_to_all(back, "mp", split_axis=0, concat_axis=0, tiled=True)
+        [gradient, left_t, right_t, moment],
+        [shape(left_t.shape, f32), shape(right_t.shape, f32), shape(square, bf16)],
+        flops=product,
+        keep=False,
+    )
     (update,) = run(
         "place",
         place_kernel,
         [owner, offset],
         [returned],
         [shape((blocks, rows, col_share), bf16)],
+        keep=False,
     )
     return (
         update,

time: 56.6 us -> 53.8 us (0.951)
  waiting for transfers between devices: 3.75 us -> 1.44 us
  local copies, waits for them, and re-layouts: 9.13 us -> 6.84 us
  Pallas kernels: 8.71 us -> 10.8 us
    all_to_all x1, waiting for transfers between devices: 3.74 us -> 1.43 us  [per_device_packed(): lax.all_to_all(back, 'mp', split_axis=0, concat_axis=0, tiled=True)]
    unnamed x29 -> x27, local copies, waits for them, and re-layouts: 9.13 us -> 6.84 us
    pallas_call x5 -> x6, Pallas kernels: 8.71 us -> 10.8 us  [run(): pl.pallas_call(kernel, out_shape=[pltpu.VMEM(o.shape, o.dtype) for o in o...]
  transfers between devices with their start and end apart: 4 -> 4, of which waited for: 1 -> 1; matrix products, arithmetic and copies ran while one was open for 6% -> 2% of each run, Pallas kernels for 4% -> 9%
where the time goes in v3:
time: 53.8 us; the launch traced here: 53.6 us
  blocking collectives  23.3 us (43%)
  Pallas kernels  10.8 us (20%)
  starting transfers between devices  10.4 us (19%)
  local copies, waits for them, and re-layouts  6.84 us (13%)
  waiting for transfers between devices  1.44 us (3%)
  between operations  0.77 us (1%)
    all_to_all x1, blocking collectives, per_device_packed(): lax.all_to_all(outgoing, ('dp', 'mp'), split_axis=0, concat_axis=0, tiled...  23.3 us
    pallas_call x6, Pallas kernels, run(): pl.pallas_call(kernel, out_shape=[pltpu.VMEM(o.shape, o.dtype) for o in o...  10.8 us
    ppermute x3, starting transfers between devices, per_device_packed(): lax.ppermute(parts[s], 'dp', [(i, (i + s) % replicas) for i in range(repl...  7.02 us
    unnamed x27, local copies, waits for them, and re-layouts  6.84 us
    all_to_all x1, starting transfers between devices, per_device_packed(): lax.all_to_all(back, 'mp', split_axis=0, concat_axis=0, tiled=True)  3.39 us
    all_to_all x1, waiting for transfers between devices, per_device_packed(): lax.all_to_all(back, 'mp', split_axis=0, concat_axis=0, tiled=True)  1.43 us
  transfers between devices with their start and end apart: 4, of which 1 were waited for; matrix products, arithmetic and copies ran while one was open for 2% of the time, Pallas kernels for 9%

profile of v3, /device:TPU:0, one launch (start us, length us, event | category | flops | bytes accessed | tf_op | source)
XLA Modules:
  0.0 53.6 jit_solution(15484989607698188178)
XLA Ops:
  0.6 1.0 %copy-done.9 = bf16[1,4,72,576]{3,2,1,0:T(8,128)(2,1)S(1)} copy-done((bf16[1,4,72,576]{3,2,1,0:T(8,128)(2,1)S(1)}, bf16[1,4,72,576]{3,2,1,0:T(8,128)(2,1)}, u32[]{:S(2)}) %copy-start.9) | copy-done | bytes 331800
  1.6 0.1 pack.1
  1.8 3.1 %collective-permute-start = (bf16[4,88,128]{2,1,0:T(8,128)(2,1)S(1)}, bf16[4,88,128]{2,1,0:T(8,128)(2,1)S(1)}, u32[]{:S(2)}, u32[]{:S(2)}) collective-permute-start(bf16[4,88,128]{2,1,0:T(8,128)(2,1)S(1)} %get-tuple-element.26), channel_id=1, source_target_pairs={{0,8},{8,16},{16,24},{24,0},{1,9},{9,17},{17,25},{25,1},{2,10},{10... | collective-permute-start | bytes 270344 | tf_op jit(solution)/shard_map/ppermute | solution.py:273
  4.9 2.6 %collective-permute-start.1 = (bf16[4,88,128]{2,1,0:T(8,128)(2,1)S(1)}, bf16[4,88,128]{2,1,0:T(8,128)(2,1)S(1)}, u32[]{:S(2)}, u32[]{:S(2)}) collective-permute-start(bf16[4,88,128]{2,1,0:T(8,128)(2,1)S(1)} %get-tuple-element.27), channel_id=1, source_target_pairs={{0,16},{8,24},{16,0},{24,8},{1,17},{9,25},{17,1},{25,9},{2,18},{10... | collective-permute-start | bytes 270344 | tf_op jit(solution)/shard_map/ppermute | solution.py:273
  7.4 1.3 %collective-permute-start.2 = (bf16[4,88,128]{2,1,0:T(8,128)(2,1)S(1)}, bf16[4,88,128]{2,1,0:T(8,128)(2,1)S(1)}, u32[]{:S(2)}, u32[]{:S(2)}) collective-permute-start(bf16[4,88,128]{2,1,0:T(8,128)(2,1)S(1)} %get-tuple-element.28), channel_id=1, source_target_pairs={{0,24},{8,0},{16,8},{24,16},{1,25},{9,1},{17,9},{25,17},{2,26},{10... | collective-permute-start | bytes 270344 | tf_op jit(solution)/shard_map/ppermute | solution.py:273
  8.8 1.1 %copy-done.1 = bf16[1,576,576]{2,1,0:T(8,128)(2,1)S(1)} copy-done((bf16[1,576,576]{2,1,0:T(8,128)(2,1)S(1)}, bf16[1,576,576]{2,1,0:T(8,128)(2,1)}, u32[]{:S(2)}) %copy-start.1) | copy-done | bytes 663576
  9.9 1.1 %copy-done.3 = bf16[1,576,576]{2,1,0:T(8,128)(2,1)S(1)} copy-done((bf16[1,576,576]{2,1,0:T(8,128)(2,1)S(1)}, bf16[1,576,576]{2,1,0:T(8,128)(2,1)}, u32[]{:S(2)}) %copy-start.3) | copy-done | bytes 663576
  11.0 1.1 %copy-done.5 = bf16[1,576,576]{2,1,0:T(8,128)(2,1)S(1)} copy-done((bf16[1,576,576]{2,1,0:T(8,128)(2,1)S(1)}, bf16[1,576,576]{2,1,0:T(8,128)(2,1)}, u32[]{:S(2)}) %copy-start.5) | copy-done | bytes 663576
  12.1 0.7 %copy-done.10 = s32[4]{0:T(128)S(1)} copy-done((s32[4]{0:T(128)S(1)}, s32[4]{0:T(128)}, u32[]{:S(2)}) %copy-start.10) | copy-done | bytes 40
  12.8 2.1 %prepare.1 = (bf16[576,576]{1,0:T(8,128)(2,1)S(1)}, f32[576,576]{1,0:T(8,128)S(1)}, bf16[576,256]{1,0:T(8,128)(2,1)S(1)}) custom-call(s32[1]{0:T(128)} %bitcast.group_ref, s32[1]{0:T(128)} %bitcast.1.me_ref.share_ref, s32[4]{0:T(128)S(1)} %copy-done.10, bf16[576,576]{1,0:T(8,128)(2,1)S(1)} %bitcast.23, bf16[576,576]{1,0:T(8,128)(2,1)S(1)} %bitcast.25, ...), custom_call_target="tpu_custom_call" | custom-call | flops 764411904 | bytes 4276224 | tf_op jit(solution)/shard_map/prepare/pallas_call | solution.py:233
  14.9 0.0 copy-start.2
  14.9 0.0 copy-start.11
  14.9 0.7 %route.1 = bf16[32,88,128]{2,1,0:T(8,128)(2,1)S(1)} custom-call(s32[4]{0:T(128)S(1)} %copy-done.10, s32[4]{0:T(128)S(1)} %copy-done.12, bf16[4,88,128]{2,1,0:T(8,128)(2,1)S(1)} %get-tuple-element.32.refs_0_, bf16[4,88,128]{2,1,0:T(8,128)(2,1)S(1)} %collective-permute-done.refs_1_, bf16[4,88,128]{2,1,0:T(8,128)(2,1)S(1)} %collective-permute-done.1.refs_2_, ...), custom_call_target="tpu_custom_call" | custom-call | bytes 1081344 | tf_op jit(solution)/shard_map/route/pallas_call | solution.py:233
  15.6 23.3 %all_to_all.10.arrived = bf16[32,88,128]{2,1,0:T(8,128)(2,1)S(1)} all-to-all(bf16[32,88,128]{2,1,0:T(8,128)(2,1)S(1)} %route.1), channel_id=1, replica_groups=mesh['dp'=4,'mp'=8] {'dp','mp'}, dimensions={0} | all-to-all | bytes 1441792 | tf_op jit(solution)/shard_map/all_to_all | solution.py:295
  39.0 4.0 %owner_step.1 = (bf16[8,88,128]{2,1,0:T(8,128)(2,1)}, bf16[576,576]{1,0:T(8,128)(2,1)S(1)}, f32[576,576]{1,0:T(8,128)S(1)}) custom-call(s32[1]{0:T(128)} %bitcast.group_ref, s32[4]{0:T(128)S(1)} %copy-done.11, bf16[32,88,128]{2,1,0:T(8,128)(2,1)S(1)} %all_to_all.10.arrived, bf16[576,576]{1,0:T(8,128)(2,1)S(1)} %bitcast.24, bf16[576,576]{1,0:T(8,128)(2,1)S(1)} %bitcast.26, ...), custom_call_target="tpu_custom_call" | custom-call | flops 1146617856 | bytes 7831552 | tf_op jit(solution)/shard_map/owner_step/pallas_call | solution.py:233
  43.0 3.4 %all-to-all-start.1 = ((bf16[8,88,128]{2,1,0:T(8,128)(2,1)}), bf16[8,88,128]{2,1,0:T(8,128)(2,1)S(1)}, u32[]{:S(2)}, u32[]{:S(2)}) async-start(bf16[8,88,128]{2,1,0:T(8,128)(2,1)} %get-tuple-element.39), calls=%async_computation.1 | async-start | bytes 360448 | tf_op jit(solution)/shard_map/all_to_all | solution.py:309
  46.4 0.0 copy-start.7
  46.4 1.1 %copy.14 = f32[1,576,576]{2,1,0:T(8,128)} copy(f32[1,576,576]{2,1,0:T(8,128)S(1)} %bitcast.21) | data formatting | bytes 2654208
  47.5 0.4 copy-done.6
  47.9 0.2 copy-done.7
  48.1 0.1 copy-done.8
  48.2 2.7 %factors.1 = (f32[144,576]{1,0:T(8,128)}, f32[144,576]{1,0:T(8,128)}, bf16[576,576]{1,0:T(8,128)(2,1)}) custom-call(s32[1]{0:T(128)} %bitcast.group_ref, s32[1]{0:T(128)} %bitcast.1.me_ref.share_ref, s32[4]{0:T(128)S(1)} %copy-done.11, bf16[576,576]{1,0:T(8,128)(2,1)S(1)} %get-tuple-element.40.gradient, f32[144,576]{1,0:T(8,128)S(1)} %bitcast.29, ...), custom_call_target="tpu_custom_call" | custom-call | flops 382205952 | bytes 3317760 | tf_op jit(solution)/shard_map/factors/pallas_call | solution.py:233
  50.9 1.4 %all-to-all-done.1.returned = bf16[8,88,128]{2,1,0:T(8,128)(2,1)S(1)} async-done(((bf16[8,88,128]{2,1,0:T(8,128)(2,1)}), bf16[8,88,128]{2,1,0:T(8,128)(2,1)S(1)}, u32[]{:S(2)}, u32[]{:S(2)}) %all-to-all-start.1) | async-done | bytes 180256 | tf_op jit(solution)/shard_map/all_to_all | solution.py:309
  52.3 1.3 %place.1 = bf16[4,72,144]{2,1,0:T(8,128)(2,1)} custom-call(s32[4]{0:T(128)S(1)} %copy-done.11, s32[4]{0:T(128)S(1)} %copy-done.12, bf16[8,88,128]{2,1,0:T(8,128)(2,1)S(1)} %all-to-all-done.1.returned), custom_call_target="tpu_custom_call" | custom-call | bytes 263168 | tf_op jit(solution)/shard_map/place/pallas_call | solution.py:233
  (18 shorter events, 0.0 us)
Async XLA Ops:
  0.6 1.0 %copy-start.9 = (bf16[1,4,72,576]{3,2,1,0:T(8,128)(2,1)S(1)}, bf16[1,4,72,576]{3,2,1,0:T(8,128)(2,1)}, u32[]{:S(2)}) copy-start(bf16[1,4,72,576]{3,2,1,0:T(8,128)(2,1)} %param.9) | copy-start | bytes 995332
  1.8 13.2 %copy-start.12 = (s32[4]{0:T(128)S(1)}, s32[4]{0:T(128)}, u32[]{:S(2)}) copy-start(s32[4]{0:T(128)} %offset_ref.3) | copy-start | bytes 52
  1.8 13.1 %collective-permute-start = (bf16[4,88,128]{2,1,0:T(8,128)(2,1)S(1)}, bf16[4,88,128]{2,1,0:T(8,128)(2,1)S(1)}, u32[]{:S(2)}, u32[]{:S(2)}) collective-permute-start(bf16[4,88,128]{2,1,0:T(8,128)(2,1)S(1)} %get-tuple-element.26), channel_id=1, source_target_pairs={{0,8},{8,16},{16,24},{24,0},{1,9},{9,17},{17,25},{25,1},{2,10},{10... | collective-permute-start | bytes 270344 | tf_op jit(solution)/shard_map/ppermute | solution.py:273
  4.9 10.1 %collective-permute-start.1 = (bf16[4,88,128]{2,1,0:T(8,128)(2,1)S(1)}, bf16[4,88,128]{2,1,0:T(8,128)(2,1)S(1)}, u32[]{:S(2)}, u32[]{:S(2)}) collective-permute-start(bf16[4,88,128]{2,1,0:T(8,128)(2,1)S(1)} %get-tuple-element.27), channel_id=1, source_target_pairs={{0,16},{8,24},{16,0},{24,8},{1,17},{9,25},{17,1},{25,9},{2,18},{10... | collective-permute-start | bytes 270344 | tf_op jit(solution)/shard_map/ppermute | solution.py:273
  7.4 7.5 %collective-permute-start.2 = (bf16[4,88,128]{2,1,0:T(8,128)(2,1)S(1)}, bf16[4,88,128]{2,1,0:T(8,128)(2,1)S(1)}, u32[]{:S(2)}, u32[]{:S(2)}) collective-permute-start(bf16[4,88,128]{2,1,0:T(8,128)(2,1)S(1)} %get-tuple-element.28), channel_id=1, source_target_pairs={{0,24},{8,0},{16,8},{24,16},{1,25},{9,1},{17,9},{25,17},{2,26},{10... | collective-permute-start | bytes 270344 | tf_op jit(solution)/shard_map/ppermute | solution.py:273
  8.8 1.1 %copy-start.1 = (bf16[1,576,576]{2,1,0:T(8,128)(2,1)S(1)}, bf16[1,576,576]{2,1,0:T(8,128)(2,1)}, u32[]{:S(2)}) copy-start(bf16[1,576,576]{2,1,0:T(8,128)(2,1)} %param.14) | copy-start | bytes 1990660
  9.9 1.1 %copy-start.3 = (bf16[1,576,576]{2,1,0:T(8,128)(2,1)S(1)}, bf16[1,576,576]{2,1,0:T(8,128)(2,1)}, u32[]{:S(2)}) copy-start(bf16[1,576,576]{2,1,0:T(8,128)(2,1)} %param.15) | copy-start | bytes 1990660
  11.0 1.1 %copy-start.5 = (bf16[1,576,576]{2,1,0:T(8,128)(2,1)S(1)}, bf16[1,576,576]{2,1,0:T(8,128)(2,1)}, u32[]{:S(2)}) copy-start(bf16[1,576,576]{2,1,0:T(8,128)(2,1)} %param.16) | copy-start | bytes 1990660
  12.1 0.7 %copy-start.10 = (s32[4]{0:T(128)S(1)}, s32[4]{0:T(128)}, u32[]{:S(2)}) copy-start(s32[4]{0:T(128)} %owner_ref.9) | copy-start | bytes 52
  12.8 26.2 %copy-start.4 = (bf16[1,576,576]{2,1,0:T(8,128)(2,1)S(1)}, bf16[1,576,576]{2,1,0:T(8,128)(2,1)}, u32[]{:S(2)}) copy-start(bf16[1,576,576]{2,1,0:T(8,128)(2,1)} %param.15) | copy-start | bytes 1990660
  14.9 24.1 %copy-start = (f32[1,576,576]{2,1,0:T(8,128)S(1)}, f32[1,576,576]{2,1,0:T(8,128)}, u32[]{:S(2)}) copy-start(f32[1,576,576]{2,1,0:T(8,128)} %param.17) | copy-start | bytes 3981316
  14.9 24.1 %copy-start.2 = (bf16[1,576,576]{2,1,0:T(8,128)(2,1)S(1)}, bf16[1,576,576]{2,1,0:T(8,128)(2,1)}, u32[]{:S(2)}) copy-start(bf16[1,576,576]{2,1,0:T(8,128)(2,1)} %param.14) | copy-start | bytes 1990660
  14.9 24.1 %copy-start.11 = (s32[4]{0:T(128)S(1)}, s32[4]{0:T(128)}, u32[]{:S(2)}) copy-start(s32[4]{0:T(128)} %owner_ref.9) | copy-start | bytes 52
  43.0 9.4 %all-to-all-start.1 = ((bf16[8,88,128]{2,1,0:T(8,128)(2,1)}), bf16[8,88,128]{2,1,0:T(8,128)(2,1)S(1)}, u32[]{:S(2)}, u32[]{:S(2)}) async-start(bf16[8,88,128]{2,1,0:T(8,128)(2,1)} %get-tuple-element.39), calls=%async_computation.1 | async-start | bytes 360448 | tf_op jit(solution)/shard_map/all_to_all | solution.py:309
  46.4 1.5 %copy-start.6 = (bf16[1,576,576]{2,1,0:T(8,128)(2,1)S(1)}, bf16[1,576,576]{2,1,0:T(8,128)(2,1)}, u32[]{:S(2)}) copy-start(bf16[1,576,576]{2,1,0:T(8,128)(2,1)} %param.16) | copy-start | bytes 1990660
  46.4 1.7 %copy-start.7 = (f32[1,576,144]{1,2,0:T(8,128)S(1)}, f32[1,576,144]{1,2,0:T(8,128)}, u32[]{:S(2)}) copy-start(f32[1,576,144]{1,2,0:T(8,128)} %param.12) | copy-start | bytes 995332
  46.4 1.8 %copy-start.8 = (f32[1,576,144]{1,2,0:T(8,128)S(1)}, f32[1,576,144]{1,2,0:T(8,128)}, u32[]{:S(2)}) copy-start(f32[1,576,144]{1,2,0:T(8,128)} %param.13) | copy-start | bytes 995332

commit v4 on v3

--- a/solution.py
+++ b/solution.py
@@ -9,8 +9,10 @@
 SUBLANES = 8
 VMEM = pl.BlockSpec(memory_space=pltpu.VMEM)
 SMEM = pl.BlockSpec(memory_space=pltpu.SMEM)
+FAR = pl.BlockSpec(memory_space=pltpu.HBM)
 VMEM_GRANT = 16 * 2**20
 CUT = 2 * LANES
+STRIP = 48
 
 def contract_first(matrix_a, matrix_b):
     return lax.dot_general(
@@ -101,15 +103,27 @@
 
 
 def prepare_kernel(
-    group_ref, share_ref, owner_ref, lbasis, rbasis, moment, lbasis_t, old_part, back_basis
+    group_ref, share_ref, owner_ref, lbasis_hbm, rbasis_hbm, moment_hbm,
+    lbasis_t, old_part, back_basis, lbasis, rbasis, moment, sems,
 ):
     _, found = slot_of(owner_ref, group_ref[0])
 
     @pl.when(found == 1)
     def _():
+        copies = [
+            pltpu.make_async_copy(source, target, sems.at[n])
+            for n, (source, target) in enumerate(
+                ((lbasis_hbm, lbasis), (moment_hbm, moment), (rbasis_hbm, rbasis))
+            )
+        ]
+        for copy in copies:
+            copy.start()
+        copies[0].wait()
         transposed = lbasis[...].T
         lbasis_t[...] = transposed
+        copies[1].wait()
         turned = matmul(transposed, moment[...]).astype(jnp.bfloat16)
+        copies[2].wait()
         old_part[...] = 0.9 * matmul(turned, rbasis[...])
         columns = rbasis.shape[0]
         col_share = columns // (columns // LANES)
@@ -140,10 +154,13 @@
 
 def owner_kernel(
     group_ref, owner_ref, arrived, lbasis, rbasis, lbasis_t, old_part, back_basis, second,
-    back, gradient, new_second, turned,
+    gradient, new_second, back_out, turned, back, sems,
 ):
     _, found = slot_of(owner_ref, group_ref[0])
     groups = back.shape[0]
+    copies = [
+        pltpu.make_async_copy(back.at[n], back_out.at[n], sems.at[n]) for n in range(groups)
+    ]
     columns = gradient.shape[1]
     rows = columns // groups
 
@@ -158,7 +175,8 @@
             fresh = 0.95 * second[:, cols] + 0.05 * rotated * rotated
             new_second[:, cols] = fresh
             rotated_mom = old_part[:, cols] + 0.1 * rotated
-            scaled = (rotated_mom / (jnp.sqrt(fresh) + 1e-08)).astype(jnp.bfloat16)
+            spread = fresh * lax.rsqrt(fresh) + 1e-08
+            scaled = (rotated_mom * lax.rsqrt(spread * spread)).astype(jnp.bfloat16)
             term = matmul(scaled, back_basis[cols, :])
             total = term if total is None else total + term
         result = matmul(lbasis[...], total.astype(jnp.bfloat16))
@@ -167,17 +185,21 @@
         width = LANES // tail_groups
         for m in range(groups):
             base = m * rows
-            back[m, :rows, :] = result[base : base + rows, :LANES].astype(jnp.bfloat16)
+            back[groups - 1 - m, :rows, :] = result[base : base + rows, :LANES].astype(jnp.bfloat16)
             mixed = result[base : base + SUBLANES, LANES:]
             for g in range(1, tail_groups):
                 row = base + g * SUBLANES
                 mixed = jnp.where(
                     lane < g * width, mixed, result[row : row + SUBLANES, LANES:]
                 )
-            back[m, rows : rows + SUBLANES, :] = mixed.astype(jnp.bfloat16)
-            back[m, rows + SUBLANES :, :] = result[
+            back[groups - 1 - m, rows : rows + SUBLANES, :] = mixed.astype(jnp.bfloat16)
+            back[groups - 1 - m, rows + SUBLANES :, :] = result[
                 base + rows - SUBLANES : base + rows, LANES:
             ].astype(jnp.bfloat16)
+        for copy in copies:
+            copy.start()
+        for copy in copies:
+            copy.wait()
 
     @pl.when(found == 0)
     def _():
@@ -185,33 +207,63 @@
 
 
 def factor_kernel(
-    group_ref, share_ref, owner_ref, gradient, left_t, right_t, moment, new_left_t, new_right_t,
-    new_moment,
+    group_ref, share_ref, owner_ref, gradient, second, left_hbm, right_hbm, moment_hbm,
+    second_out, left_out, right_out, moment_out,
+    left_t, right_t, moment, new_left_t, new_right_t, new_moment, sems,
 ):
     _, found = slot_of(owner_ref, group_ref[0])
     col_share, columns = left_t.shape
+    pairs = (
+        (moment_hbm, moment),
+        (left_hbm, left_t),
+        (right_hbm, right_t),
+        (second, second_out),
+        (new_moment, moment_out),
+        (new_left_t, left_out),
+        (new_right_t, right_out),
+        (moment, moment_out),
+        (left_t, left_out),
+        (right_t, right_out),
+    )
+    copies = [pltpu.make_async_copy(a, b, sems.at[n]) for n, (a, b) in enumerate(pairs)]
+    for copy in copies[:4]:
+        copy.start()
 
     @pl.when(found == 1)
     def _():
         first = pl.multiple_of(share_ref[0] * col_share, 16)
         grad = gradient[...]
+        copies[0].wait()
+        for low in range(0, columns, STRIP):
+            strip = slice(low, min(low + STRIP, columns))
+            new_moment[strip, :] = (
+                0.9 * moment[strip, :].astype(jnp.float32)
+                + 0.1 * gradient[strip, :].astype(jnp.float32)
+            ).astype(jnp.bfloat16)
+        copies[4].start()
+        copies[1].wait()
         new_left_t[...] = 0.95 * left_t[...] + 0.05 * contract_last(
             gradient[pl.ds(first, col_share), :], grad
         )
+        copies[5].start()
         picked = lax.broadcasted_iota(jnp.int32, (col_share, columns), 0) + first
         places = lax.broadcasted_iota(jnp.int32, (col_share, columns), 1)
         pick = jnp.where(picked == places, 1.0, 0.0).astype(jnp.bfloat16)
         grad_cols_t = contract_last(pick, grad).astype(jnp.bfloat16)
+        copies[2].wait()
         new_right_t[...] = 0.95 * right_t[...] + 0.05 * matmul(grad_cols_t, grad)
-        new_moment[...] = (
-            0.9 * moment[...].astype(jnp.float32) + 0.1 * grad.astype(jnp.float32)
-        ).astype(jnp.bfloat16)
+        copies[6].start()
+        for copy in copies[3:7]:
+            copy.wait()
 
     @pl.when(found == 0)
     def _():
-        new_left_t[...] = left_t[...]
-        new_right_t[...] = right_t[...]
-        new_moment[...] = moment[...]
+        for n in range(3):
+            copies[n].wait()
+            copies[7 + n].start()
+        copies[3].wait()
+        for copy in copies[7:]:
+            copy.wait()
 
 
 def place_kernel(owner_ref, offset_ref, returned, update):
@@ -219,7 +271,7 @@
     tail_groups = rows // SUBLANES - 1
     width = col_share - LANES
     for b in range(blocks):
-        place, slot = offset_ref[b], owner_ref[b]
+        place, slot = offset_ref[b], returned.shape[0] - 1 - owner_ref[b]
         update[place, :, :LANES] = returned[slot, :rows, :]
         for g in range(tail_groups):
             update[place, g * SUBLANES : (g + 1) * SUBLANES, LANES:] = returned[
@@ -228,18 +280,27 @@
         update[place, rows - SUBLANES :, LANES:] = returned[slot, rows + SUBLANES :, :width]
 
 
-def run(name, kernel, scalars, arrays, outs, scratch=(), flops=0, keep=True):
+def run(name, kernel, scalars, arrays, outs, scratch=(), flops=0, sems=0, far=0, far_outs=0):
     moved = sum(a.size * a.dtype.itemsize for a in list(arrays) + list(outs))
+    near = len(arrays) - far
+    near_outs = len(outs) - max(far_outs, 0)
+    near_shape = (lambda o: o) if far_outs < 0 else (lambda o: pltpu.VMEM(o.shape, o.dtype))
     return pl.pallas_call(
         kernel,
-        out_shape=[pltpu.VMEM(o.shape, o.dtype) for o in outs] if keep else list(outs),
-        in_specs=[SMEM] * len(scalars) + [VMEM] * len(arrays),
-        out_specs=[VMEM] * len(outs),
-        scratch_shapes=[pltpu.VMEM(o.shape, o.dtype) for o in scratch],
+        out_shape=[near_shape(o) for o in outs[:near_outs]]
+        + [pltpu.HBM(o.shape, o.dtype) for o in outs[near_outs:]],
+        in_specs=[SMEM] * len(scalars) + [VMEM] * near + [FAR] * far,
+        out_specs=[VMEM] * near_outs + [FAR] * max(far_outs, 0),
+        scratch_shapes=[pltpu.VMEM(o.shape, o.dtype) for o in scratch]
+        + [pltpu.SemaphoreType.DMA((sems,))] * (sems > 0),
         compiler_params=pltpu.CompilerParams(vmem_limit_bytes=VMEM_GRANT),
         cost_estimate=pl.CostEstimate(flops=flops, bytes_accessed=moved, transcendentals=0),
         name=name,
-    )(*scalars, *(pltpu.with_memory_space_constraint(a, pltpu.VMEM) for a in arrays))
+    )(
+        *scalars,
+        *(pltpu.with_memory_space_constraint(a, pltpu.VMEM) for a in arrays[:near]),
+        *(pltpu.with_memory_space_constraint(a, pltpu.HBM) for a in arrays[near:]),
+    )
 
 
 def per_device_packed(
@@ -279,6 +340,9 @@
         [group, share, owner],
         [lbasis, rbasis, moment],
         [shape(square, bf16), shape(square, f32), shape((columns, 2 * LANES), bf16)],
+        scratch=[shape(square, bf16)] * 3,
+        sems=3,
+        far=3,
         flops=2 * product,
     )
     parts, lbasis_t, old_part, back_basis = lax.optimization_barrier(
@@ -293,28 +357,38 @@
         scratch=[packed],
     )
     arrived = lax.all_to_all(outgoing, ("dp", "mp"), split_axis=0, concat_axis=0, tiled=True)
-    back, gradient, new_second = run(
+    chunks = shape((groups, rows + 2 * SUBLANES, LANES), bf16)
+    gradient, new_second, back = run(
         "owner_step",
         owner_kernel,
         [group, owner],
         [arrived, lbasis, rbasis, lbasis_t, old_part, back_basis, second],
-        [
-            shape((groups, rows + 2 * SUBLANES, LANES), bf16),
-            shape(square, bf16),
-            shape(square, f32),
-        ],
-        scratch=[shape(square, bf16)],
+        [shape(square, bf16), shape(square, f32), chunks],
+        scratch=[shape(square, bf16), chunks],
+        sems=groups,
+        far_outs=1,
         flops=3 * product,
     )
-    returned = lax.all_to_all(back, "mp", split_axis=0, concat_axis=0, tiled=True)
-    new_left_t, new_right_t, new_moment = run(
+    returned = lax.all_to_all(
+        back,
+        "mp",
+        split_axis=0,
+        concat_axis=0,
+        tiled=True,
+        axis_index_groups=[list(range(groups))[::-1]],
+    )
+    factor_t = shape(left_t.shape, f32)
+    new_second, new_left_t, new_right_t, new_moment = run(
         "factors",
         factor_kernel,
         [group, share, owner],
-        [gradient, left_t, right_t, moment],
-        [shape(left_t.shape, f32), shape(right_t.shape, f32), shape(square, bf16)],
+        [gradient, new_second, left_t, right_t, moment],
+        [shape(square, f32), factor_t, factor_t, shape(square, bf16)],
+        scratch=[factor_t, factor_t, shape(square, bf16)] * 2,
+        sems=10,
+        far=3,
+        far_outs=4,
         flops=product,
-        keep=False,
     )
     (update,) = run(
         "place",
@@ -322,7 +396,7 @@
         [owner, offset],
         [returned],
         [shape((blocks, rows, col_share), bf16)],
-        keep=False,
+        far_outs=-1,
     )
     return (
         update,

time: 53.8 us -> 53.6 us (level); the launches traced: 53.6 us -> 52.6 us
  local copies, waits for them, and re-layouts: 6.84 us -> 1.66 us
  starting transfers between devices: 10.4 us -> 15.2 us
  Pallas kernels: 10.8 us -> 6.78 us
  waiting for transfers between devices: 1.44 us -> 3.67 us
  blocking collectives: 23.3 us -> 24.6 us
    unnamed x27 -> x14, local copies, waits for them, and re-layouts: 6.84 us -> 1.66 us
    all_to_all x1, starting transfers between devices: 3.39 us -> 8.17 us  [per_device_packed(): lax.all_to_all(back, 'mp', split_axis=0, concat_axis=0, tiled=True, axis_...]
    pallas_call x6, Pallas kernels: 10.8 us -> 6.78 us  [run(): pl.pallas_call(kernel, out_shape=[near_shape(o) for o in outs[:near_outs]...]
    ppermute x3, waiting for transfers between devices: 0.01 us -> 3.63 us  [per_device_packed(): lax.ppermute(parts[s], 'dp', [(i, (i + s) % replicas) for i in range(repl...]
    all_to_all x1, waiting for transfers between devices: 1.43 us -> 0.04 us  [per_device_packed(): lax.all_to_all(back, 'mp', split_axis=0, concat_axis=0, tiled=True, axis_...]
    all_to_all x1, blocking collectives: 23.3 us -> 24.6 us  [per_device_packed(): lax.all_to_all(outgoing, ('dp', 'mp'), split_axis=0, concat_axis=0, tiled...]
  transfers between devices with their start and end apart: 4 -> 4, of which waited for: 1 -> 3; matrix products, arithmetic and copies ran while one was open for 2% -> 0% of each run, Pallas kernels for 9% -> 7%
where the time goes in v4:
time: 53.6 us; the launch traced here: 52.6 us
  blocking collectives  24.6 us (46%)
  starting transfers between devices  15.2 us (28%)
  Pallas kernels  6.78 us (13%)
  waiting for transfers between devices  3.67 us (7%)
  local copies, waits for them, and re-layouts  1.66 us (3%)
  between operations  0.72 us (1%)
    all_to_all x1, blocking collectives, per_device_packed(): lax.all_to_all(outgoing, ('dp', 'mp'), split_axis=0, concat_axis=0, tiled...  24.6 us
    all_to_all x1, starting transfers between devices, per_device_packed(): lax.all_to_all(back, 'mp', split_axis=0, concat_axis=0, tiled=True, axis_...  8.17 us
    ppermute x3, starting transfers between devices, per_device_packed(): lax.ppermute(parts[s], 'dp', [(i, (i + s) % replicas) for i in range(repl...  7.02 us
    pallas_call x6, Pallas kernels, run(): pl.pallas_call(kernel, out_shape=[near_shape(o) for o in outs[:near_outs]...  6.78 us
    ppermute x3, waiting for transfers between devices, per_device_packed(): lax.ppermute(parts[s], 'dp', [(i, (i + s) % replicas) for i in range(repl...  3.63 us
    unnamed x14, local copies, waits for them, and re-layouts  1.66 us
  transfers between devices with their start and end apart: 4, of which 3 were waited for; matrix products, arithmetic and copies ran while one was open for 0% of the time, Pallas kernels for 7%

profile of v4, /device:TPU:0, one launch (start us, length us, event | category | flops | bytes accessed | tf_op | source)
XLA Modules:
  0.0 52.6 jit_solution(17723224032228322703)
XLA Ops:
  0.6 0.0 copy-start.3
  0.6 1.0 %copy-done.3 = bf16[1,4,72,576]{3,2,1,0:T(8,128)(2,1)S(1)} copy-done((bf16[1,4,72,576]{3,2,1,0:T(8,128)(2,1)S(1)}, bf16[1,4,72,576]{3,2,1,0:T(8,128)(2,1)}, u32[]{:S(2)}) %copy-start.3) | copy-done | bytes 331800
  1.6 0.1 pack.1
  1.8 3.1 %collective-permute-start = (bf16[4,88,128]{2,1,0:T(8,128)(2,1)S(1)}, bf16[4,88,128]{2,1,0:T(8,128)(2,1)S(1)}, u32[]{:S(2)}, u32[]{:S(2)}) collective-permute-start(bf16[4,88,128]{2,1,0:T(8,128)(2,1)S(1)} %get-tuple-element.27), channel_id=1, source_target_pairs={{0,8},{8,16},{16,24},{24,0},{1,9},{9,17},{17,25},{25,1},{2,10},{10... | collective-permute-start | bytes 270344 | tf_op jit(solution)/shard_map/ppermute | solution.py:334
  4.9 2.6 %collective-permute-start.1 = (bf16[4,88,128]{2,1,0:T(8,128)(2,1)S(1)}, bf16[4,88,128]{2,1,0:T(8,128)(2,1)S(1)}, u32[]{:S(2)}, u32[]{:S(2)}) collective-permute-start(bf16[4,88,128]{2,1,0:T(8,128)(2,1)S(1)} %get-tuple-element.28), channel_id=1, source_target_pairs={{0,16},{8,24},{16,0},{24,8},{1,17},{9,25},{17,1},{25,9},{2,18},{10... | collective-permute-start | bytes 270344 | tf_op jit(solution)/shard_map/ppermute | solution.py:334
  7.4 1.3 %collective-permute-start.2 = (bf16[4,88,128]{2,1,0:T(8,128)(2,1)S(1)}, bf16[4,88,128]{2,1,0:T(8,128)(2,1)S(1)}, u32[]{:S(2)}, u32[]{:S(2)}) collective-permute-start(bf16[4,88,128]{2,1,0:T(8,128)(2,1)S(1)} %get-tuple-element.29), channel_id=1, source_target_pairs={{0,24},{8,0},{16,8},{24,16},{1,25},{9,1},{17,9},{25,17},{2,26},{10... | collective-permute-start | bytes 270344 | tf_op jit(solution)/shard_map/ppermute | solution.py:334
  8.8 0.7 %copy-done.4 = s32[4]{0:T(128)S(1)} copy-done((s32[4]{0:T(128)S(1)}, s32[4]{0:T(128)}, u32[]{:S(2)}) %copy-start.4) | copy-done | bytes 40
  9.5 0.6 %prepare.1 = (bf16[576,576]{1,0:T(8,128)(2,1)S(1)}, f32[576,576]{1,0:T(8,128)S(1)}, bf16[576,256]{1,0:T(8,128)(2,1)S(1)}) custom-call(s32[1]{0:T(128)} %bitcast.group_ref, s32[1]{0:T(128)} %bitcast.1.me_ref.share_ref, s32[4]{0:T(128)S(1)} %copy-done.4, bf16[576,576]{1,0:T(8,128)(2,1)} %bitcast.22, bf16[576,576]{1,0:T(8,128)(2,1)} %bitcast.24, ...), custom_call_target="tpu_custom_call" | custom-call | flops 764411904 | bytes 4276224 | tf_op jit(solution)/shard_map/prepare/pallas_call | solution.py:288
  10.0 0.0 copy-start
  10.1 0.0 copy-start.1
  10.1 0.0 copy-start.5
  10.1 0.1 collective-permute-done.refs_1_
  10.2 3.3 %collective-permute-done.1.refs_2_ = bf16[4,88,128]{2,1,0:T(8,128)(2,1)S(1)} collective-permute-done((bf16[4,88,128]{2,1,0:T(8,128)(2,1)S(1)}, bf16[4,88,128]{2,1,0:T(8,128)(2,1)S(1)}, u32[]{:S(2)}, u32[]{:S(2)}) %collective-permute-start.1) | collective-permute-done | bytes 90144 | tf_op jit(solution)/shard_map/ppermute | solution.py:334
  13.5 0.2 collective-permute-done.2.refs_3_
  13.7 0.0 copy-done.6
  13.7 0.7 %route.1 = bf16[32,88,128]{2,1,0:T(8,128)(2,1)S(1)} custom-call(s32[4]{0:T(128)S(1)} %copy-done.4, s32[4]{0:T(128)S(1)} %copy-done.6, bf16[4,88,128]{2,1,0:T(8,128)(2,1)S(1)} %get-tuple-element.33.refs_0_, bf16[4,88,128]{2,1,0:T(8,128)(2,1)S(1)} %collective-permute-done.refs_1_, bf16[4,88,128]{2,1,0:T(8,128)(2,1)S(1)} %collective-permute-done.1.refs_2_, ...), custom_call_target="tpu_custom_call" | custom-call | bytes 1081344 | tf_op jit(solution)/shard_map/route/pallas_call | solution.py:288
  14.4 24.6 %all_to_all.10.arrived = bf16[32,88,128]{2,1,0:T(8,128)(2,1)S(1)} all-to-all(bf16[32,88,128]{2,1,0:T(8,128)(2,1)S(1)} %route.1), channel_id=1, replica_groups=mesh['dp'=4,'mp'=8] {'dp','mp'}, dimensions={0} | all-to-all | bytes 1441792 | tf_op jit(solution)/shard_map/all_to_all | solution.py:359
  39.0 0.0 copy-done.2
  39.0 0.0 copy-done
  39.0 0.7 %owner_step.1 = (bf16[576,576]{1,0:T(8,128)(2,1)S(1)}, f32[576,576]{1,0:T(8,128)S(1)}, bf16[8,88,128]{2,1,0:T(8,128)(2,1)}) custom-call(s32[1]{0:T(128)} %bitcast.group_ref, s32[4]{0:T(128)S(1)} %copy-done.5, bf16[32,88,128]{2,1,0:T(8,128)(2,1)S(1)} %all_to_all.10.arrived, bf16[576,576]{1,0:T(8,128)(2,1)S(1)} %bitcast.23, bf16[576,576]{1,0:T(8,128)(2,1)S(1)} %bitcast.25, ...), custom_call_target="tpu_custom_call" | custom-call | flops 1146617856 | bytes 7831552 | tf_op jit(solution)/shard_map/owner_step/pallas_call | solution.py:288
  39.7 8.2 %all-to-all-start.1 = ((bf16[8,88,128]{2,1,0:T(8,128)(2,1)}), bf16[8,88,128]{2,1,0:T(8,128)(2,1)S(1)}, u32[]{:S(2)}, u32[]{:S(2)}) async-start(bf16[8,88,128]{2,1,0:T(8,128)(2,1)} %get-tuple-element.40), calls=%async_computation.1 | async-start | bytes 360448 | tf_op jit(solution)/shard_map/all_to_all | solution.py:372
  47.9 3.3 %factors.1 = (f32[576,576]{1,0:T(8,128)}, f32[144,576]{1,0:T(8,128)}, f32[144,576]{1,0:T(8,128)}, bf16[576,576]{1,0:T(8,128)(2,1)}) custom-call(s32[1]{0:T(128)} %bitcast.group_ref, s32[1]{0:T(128)} %bitcast.1.me_ref.share_ref, s32[4]{0:T(128)S(1)} %copy-done.5, bf16[576,576]{1,0:T(8,128)(2,1)S(1)} %get-tuple-element.41.gradient, ...), custom_call_target="tpu_custom_call" | custom-call | flops 382205952 | bytes 5971968 | tf_op jit(solution)/shard_map/factors/pallas_call | solution.py:288
  51.3 0.0 all-to-all-done.1.returned
  51.3 1.3 %place.1 = bf16[4,72,144]{2,1,0:T(8,128)(2,1)} custom-call(s32[4]{0:T(128)S(1)} %copy-done.5, s32[4]{0:T(128)S(1)} %copy-done.6, bf16[8,88,128]{2,1,0:T(8,128)(2,1)S(1)} %all-to-all-done.1.returned), custom_call_target="tpu_custom_call" | custom-call | bytes 263168 | tf_op jit(solution)/shard_map/place/pallas_call | solution.py:288
  (5 shorter events, 0.0 us)
Async XLA Ops:
  0.6 1.0 %copy-start.3 = (bf16[1,4,72,576]{3,2,1,0:T(8,128)(2,1)S(1)}, bf16[1,4,72,576]{3,2,1,0:T(8,128)(2,1)}, u32[]{:S(2)}) copy-start(bf16[1,4,72,576]{3,2,1,0:T(8,128)(2,1)} %param.9) | copy-start | bytes 995332
  1.8 11.9 %copy-start.6 = (s32[4]{0:T(128)S(1)}, s32[4]{0:T(128)}, u32[]{:S(2)}) copy-start(s32[4]{0:T(128)} %offset_ref.3) | copy-start | bytes 52
  1.8 8.4 %collective-permute-start = (bf16[4,88,128]{2,1,0:T(8,128)(2,1)S(1)}, bf16[4,88,128]{2,1,0:T(8,128)(2,1)S(1)}, u32[]{:S(2)}, u32[]{:S(2)}) collective-permute-start(bf16[4,88,128]{2,1,0:T(8,128)(2,1)S(1)} %get-tuple-element.27), channel_id=1, source_target_pairs={{0,8},{8,16},{16,24},{24,0},{1,9},{9,17},{17,25},{25,1},{2,10},{10... | collective-permute-start | bytes 270344 | tf_op jit(solution)/shard_map/ppermute | solution.py:334
  4.9 8.6 %collective-permute-start.1 = (bf16[4,88,128]{2,1,0:T(8,128)(2,1)S(1)}, bf16[4,88,128]{2,1,0:T(8,128)(2,1)S(1)}, u32[]{:S(2)}, u32[]{:S(2)}) collective-permute-start(bf16[4,88,128]{2,1,0:T(8,128)(2,1)S(1)} %get-tuple-element.28), channel_id=1, source_target_pairs={{0,16},{8,24},{16,0},{24,8},{1,17},{9,25},{17,1},{25,9},{2,18},{10... | collective-permute-start | bytes 270344 | tf_op jit(solution)/shard_map/ppermute | solution.py:334
  7.4 6.3 %collective-permute-start.2 = (bf16[4,88,128]{2,1,0:T(8,128)(2,1)S(1)}, bf16[4,88,128]{2,1,0:T(8,128)(2,1)S(1)}, u32[]{:S(2)}, u32[]{:S(2)}) collective-permute-start(bf16[4,88,128]{2,1,0:T(8,128)(2,1)S(1)} %get-tuple-element.29), channel_id=1, source_target_pairs={{0,24},{8,0},{16,8},{24,16},{1,25},{9,1},{17,9},{25,17},{2,26},{10... | collective-permute-start | bytes 270344 | tf_op jit(solution)/shard_map/ppermute | solution.py:334
  8.8 0.7 %copy-start.4 = (s32[4]{0:T(128)S(1)}, s32[4]{0:T(128)}, u32[]{:S(2)}) copy-start(s32[4]{0:T(128)} %owner_ref.9) | copy-start | bytes 52
  9.5 29.5 %copy-start.2 = (bf16[1,576,576]{2,1,0:T(8,128)(2,1)S(1)}, bf16[1,576,576]{2,1,0:T(8,128)(2,1)}, u32[]{:S(2)}) copy-start(bf16[1,576,576]{2,1,0:T(8,128)(2,1)} %param.15) | copy-start | bytes 1990660
  10.0 28.9 %copy-start = (f32[1,576,576]{2,1,0:T(8,128)S(1)}, f32[1,576,576]{2,1,0:T(8,128)}, u32[]{:S(2)}) copy-start(f32[1,576,576]{2,1,0:T(8,128)} %param.17) | copy-start | bytes 3981316
  10.1 28.9 %copy-start.1 = (bf16[1,576,576]{2,1,0:T(8,128)(2,1)S(1)}, bf16[1,576,576]{2,1,0:T(8,128)(2,1)}, u32[]{:S(2)}) copy-start(bf16[1,576,576]{2,1,0:T(8,128)(2,1)} %param.14) | copy-start | bytes 1990660
  10.1 28.9 %copy-start.5 = (s32[4]{0:T(128)S(1)}, s32[4]{0:T(128)}, u32[]{:S(2)}) copy-start(s32[4]{0:T(128)} %owner_ref.9) | copy-start | bytes 52
  39.7 11.6 %all-to-all-start.1 = ((bf16[8,88,128]{2,1,0:T(8,128)(2,1)}), bf16[8,88,128]{2,1,0:T(8,128)(2,1)S(1)}, u32[]{:S(2)}, u32[]{:S(2)}) async-start(bf16[8,88,128]{2,1,0:T(8,128)(2,1)} %get-tuple-element.40), calls=%async_computation.1 | async-start | bytes 360448 | tf_op jit(solution)/shard_map/all_to_all | solution.py:372

commit v5 on v4

--- a/solution.py
+++ b/solution.py
@@ -47,32 +47,39 @@
     )
 
 
-def pack_kernel(me_ref, grad_ref, *outs):
+def pack_kernel(me_ref, grad_hbm, *refs):
+    outs, last, sems = refs[:-2], refs[-2], refs[-1]
     replicas = len(outs)
-    blocks, rows, columns = grad_ref.shape
+    blocks, rows, columns = grad_hbm.shape
     half = LANES // 2
+    copies = [pltpu.make_async_copy(grad_hbm.at[:, :, columns - half :], last, sems.at[replicas])]
     for step in range(replicas):
         share = lax.rem(me_ref[0] + step, replicas)
         col = pl.multiple_of(share * LANES, LANES)
+        copies.append(
+            pltpu.make_async_copy(
+                grad_hbm.at[:, :, pl.ds(col, LANES)], outs[step].at[:, :rows, :], sems.at[step]
+            )
+        )
+    for copy in copies:
+        copy.start()
+    copies[0].wait()
+    for step in range(replicas):
+        share = lax.rem(me_ref[0] + step, replicas)
         start = tail_start(share)
         row = pl.multiple_of(start * SUBLANES, SUBLANES)
+        row_next = pl.multiple_of(row + SUBLANES, SUBLANES)
         row_third = pl.multiple_of(
             jnp.minimum(start + 2, rows // SUBLANES - 1) * SUBLANES, SUBLANES
         )
         out = outs[step]
         for b in range(blocks):
-            out[b, :rows, :] = grad_ref[b, :, pl.ds(col, LANES)]
-            out[b, rows : rows + SUBLANES, :half] = grad_ref[
-                b, pl.ds(row, SUBLANES), columns - half :
-            ]
-            row_next = pl.multiple_of(row + SUBLANES, SUBLANES)
-            out[b, rows + SUBLANES :, :half] = grad_ref[
-                b, pl.ds(row_next, SUBLANES), columns - half :
-            ]
-            out[b, rows : rows + SUBLANES, half:] = grad_ref[
-                b, pl.ds(row_third, SUBLANES), columns - half :
-            ]
+            out[b, rows : rows + SUBLANES, :half] = last[b, pl.ds(row, SUBLANES), :]
+            out[b, rows + SUBLANES :, :half] = last[b, pl.ds(row_next, SUBLANES), :]
+            out[b, rows : rows + SUBLANES, half:] = last[b, pl.ds(row_third, SUBLANES), :]
             out[b, rows + SUBLANES :, half:] = jnp.zeros((SUBLANES, half), out.dtype)
+    for copy in copies[1:]:
+        copy.wait()
 
 
 def slot_of(owner_ref, group):
@@ -154,13 +161,25 @@
 
 def owner_kernel(
     group_ref, owner_ref, arrived, lbasis, rbasis, lbasis_t, old_part, back_basis, second,
-    gradient, new_second, back_out, turned, back, sems,
+    moment_hbm, left_hbm, right_hbm,
+    gradient, moment, left_t, right_t, second_out, back_out,
+    turned, back, new_second, sems,
 ):
     _, found = slot_of(owner_ref, group_ref[0])
     groups = back.shape[0]
     copies = [
         pltpu.make_async_copy(back.at[n], back_out.at[n], sems.at[n]) for n in range(groups)
     ]
+    loads = [
+        pltpu.make_async_copy(source, target, sems.at[groups + n])
+        for n, (source, target) in enumerate(
+            ((moment_hbm, moment), (left_hbm, left_t), (right_hbm, right_t))
+        )
+    ]
+    fresh_copy = pltpu.make_async_copy(new_second, second_out, sems.at[groups + 3])
+    kept_copy = pltpu.make_async_copy(second, second_out, sems.at[groups + 4])
+    for load in loads:
+        load.start()
     columns = gradient.shape[1]
     rows = columns // groups
 
@@ -179,6 +198,7 @@
             scaled = (rotated_mom * lax.rsqrt(spread * spread)).astype(jnp.bfloat16)
             term = matmul(scaled, back_basis[cols, :])
             total = term if total is None else total + term
+        fresh_copy.start()
         result = matmul(lbasis[...], total.astype(jnp.bfloat16))
         lane = lax.broadcasted_iota(jnp.int32, (SUBLANES, LANES), 1)
         tail_groups = rows // SUBLANES - 1
@@ -198,99 +218,102 @@
             ].astype(jnp.bfloat16)
         for copy in copies:
             copy.start()
-        for copy in copies:
+        for copy in copies + [fresh_copy]:
             copy.wait()
 
     @pl.when(found == 0)
     def _():
-        new_second[...] = second[...]
+        kept_copy.start()
+        kept_copy.wait()
+
+    for load in loads:
+        load.wait()
 
 
 def factor_kernel(
-    group_ref, share_ref, owner_ref, gradient, second, left_hbm, right_hbm, moment_hbm,
-    second_out, left_out, right_out, moment_out,
-    left_t, right_t, moment, new_left_t, new_right_t, new_moment, sems,
+    group_ref, share_ref, owner_ref, gradient, moment, left_t, right_t,
+    moment_out, left_out, right_out, new_moment, new_left_t, new_right_t, sems,
 ):
     _, found = slot_of(owner_ref, group_ref[0])
     col_share, columns = left_t.shape
-    pairs = (
-        (moment_hbm, moment),
-        (left_hbm, left_t),
-        (right_hbm, right_t),
-        (second, second_out),
-        (new_moment, moment_out),
-        (new_left_t, left_out),
-        (new_right_t, right_out),
-        (moment, moment_out),
-        (left_t, left_out),
-        (right_t, right_out),
-    )
-    copies = [pltpu.make_async_copy(a, b, sems.at[n]) for n, (a, b) in enumerate(pairs)]
-    for copy in copies[:4]:
-        copy.start()
+    outs = (moment_out, left_out, right_out)
+    fresh, kept = (
+        [pltpu.make_async_copy(a, b, sems.at[n]) for n, (a, b) in enumerate(zip(sources, outs))]
+        for sources in ((new_moment, new_left_t, new_right_t), (moment, left_t, right_t))
+    )
 
     @pl.when(found == 1)
     def _():
-        first = pl.multiple_of(share_ref[0] * col_share, 16)
-        grad = gradient[...]
-        copies[0].wait()
         for low in range(0, columns, STRIP):
             strip = slice(low, min(low + STRIP, columns))
             new_moment[strip, :] = (
                 0.9 * moment[strip, :].astype(jnp.float32)
                 + 0.1 * gradient[strip, :].astype(jnp.float32)
             ).astype(jnp.bfloat16)
-        copies[4].start()
-        copies[1].wait()
+        fresh[0].start()
+        first = pl.multiple_of(share_ref[0] * col_share, 16)
+        grad = gradient[...]
         new_left_t[...] = 0.95 * left_t[...] + 0.05 * contract_last(
             gradient[pl.ds(first, col_share), :], grad
         )
-        copies[5].start()
         picked = lax.broadcasted_iota(jnp.int32, (col_share, columns), 0) + first
         places = lax.broadcasted_iota(jnp.int32, (col_share, columns), 1)
         pick = jnp.where(picked == places, 1.0, 0.0).astype(jnp.bfloat16)
         grad_cols_t = contract_last(pick, grad).astype(jnp.bfloat16)
-        copies[2].wait()
         new_right_t[...] = 0.95 * right_t[...] + 0.05 * matmul(grad_cols_t, grad)
-        copies[6].start()
-        for copy in copies[3:7]:
+        for copy in fresh[1:]:
+            copy.start()
+        for copy in fresh:
             copy.wait()
 
     @pl.when(found == 0)
     def _():
-        for n in range(3):
-            copies[n].wait()
-            copies[7 + n].start()
-        copies[3].wait()
-        for copy in copies[7:]:
+        for copy in kept:
+            copy.start()
+        for copy in kept:
             copy.wait()
 
 
-def place_kernel(owner_ref, offset_ref, returned, update):
+def place_kernel(owner_ref, offset_ref, returned, update, tails, sems):
     blocks, rows, col_share = update.shape
     tail_groups = rows // SUBLANES - 1
     width = col_share - LANES
+    copies = []
     for b in range(blocks):
         place, slot = offset_ref[b], returned.shape[0] - 1 - owner_ref[b]
-        update[place, :, :LANES] = returned[slot, :rows, :]
+        copies.append(
+            pltpu.make_async_copy(
+                returned.at[slot, :rows], update.at[place, :, :LANES], sems.at[b]
+            )
+        )
+        copies[-1].start()
+    for b in range(blocks):
+        place, slot = offset_ref[b], returned.shape[0] - 1 - owner_ref[b]
         for g in range(tail_groups):
-            update[place, g * SUBLANES : (g + 1) * SUBLANES, LANES:] = returned[
+            tails[b, g * SUBLANES : (g + 1) * SUBLANES, :] = returned[
                 slot, rows : rows + SUBLANES, g * width : (g + 1) * width
             ]
-        update[place, rows - SUBLANES :, LANES:] = returned[slot, rows + SUBLANES :, :width]
+        tails[b, rows - SUBLANES :, :] = returned[slot, rows + SUBLANES :, :width]
+        copies.append(
+            pltpu.make_async_copy(
+                tails.at[b], update.at[place, :, LANES:], sems.at[blocks + b]
+            )
+        )
+        copies[-1].start()
+    for copy in copies:
+        copy.wait()
 
 
 def run(name, kernel, scalars, arrays, outs, scratch=(), flops=0, sems=0, far=0, far_outs=0):
     moved = sum(a.size * a.dtype.itemsize for a in list(arrays) + list(outs))
     near = len(arrays) - far
-    near_outs = len(outs) - max(far_outs, 0)
-    near_shape = (lambda o: o) if far_outs < 0 else (lambda o: pltpu.VMEM(o.shape, o.dtype))
+    near_outs = len(outs) - far_outs
     return pl.pallas_call(
         kernel,
-        out_shape=[near_shape(o) for o in outs[:near_outs]]
+        out_shape=[pltpu.VMEM(o.shape, o.dtype) for o in outs[:near_outs]]
         + [pltpu.HBM(o.shape, o.dtype) for o in outs[near_outs:]],
         in_specs=[SMEM] * len(scalars) + [VMEM] * near + [FAR] * far,
-        out_specs=[VMEM] * near_outs + [FAR] * max(far_outs, 0),
+        out_specs=[VMEM] * near_outs + [FAR] * far_outs,
         scratch_shapes=[pltpu.VMEM(o.shape, o.dtype) for o in scratch]
         + [pltpu.SemaphoreType.DMA((sems,))] * (sems > 0),
         compiler_params=pltpu.CompilerParams(vmem_limit_bytes=VMEM_GRANT),
@@ -329,7 +352,16 @@
     left_t, right_t = left_factor[0].T, right_factor[0].T
     product = 2 * columns**3
 
-    parts = run("pack", pack_kernel, [share], [pieces], [packed] * replicas)
+    parts = run(
+        "pack",
+        pack_kernel,
+        [share],
+        [pieces],
+        [packed] * replicas,
+        scratch=[shape((blocks, rows, LANES // 2), bf16)],
+        sems=replicas + 1,
+        far=1,
+    )
     parts = [parts[0]] + [
         lax.ppermute(parts[s], "dp", [(i, (i + s) % replicas) for i in range(replicas)])
         for s in range(1, replicas)
@@ -358,15 +390,20 @@
     )
     arrived = lax.all_to_all(outgoing, ("dp", "mp"), split_axis=0, concat_axis=0, tiled=True)
     chunks = shape((groups, rows + 2 * SUBLANES, LANES), bf16)
-    gradient, new_second, back = run(
+    factor_t = shape(left_t.shape, f32)
+    gradient, moment, left_t, right_t, new_second, back = run(
         "owner_step",
         owner_kernel,
         [group, owner],
-        [arrived, lbasis, rbasis, lbasis_t, old_part, back_basis, second],
-        [shape(square, bf16), shape(square, f32), chunks],
-        scratch=[shape(square, bf16), chunks],
-        sems=groups,
-        far_outs=1,
+        [
+            arrived, lbasis, rbasis, lbasis_t, old_part, back_basis, second, moment, left_t,
+            right_t,
+        ],
+        [shape(square, bf16)] * 2 + [factor_t] * 2 + [shape(square, f32), chunks],
+        scratch=[shape(square, bf16), chunks, shape(square, f32)],
+        sems=groups + 5,
+        far=3,
+        far_outs=2,
         flops=3 * product,
     )
     returned = lax.all_to_all(
@@ -377,17 +414,15 @@
         tiled=True,
         axis_index_groups=[list(range(groups))[::-1]],
     )
-    factor_t = shape(left_t.shape, f32)
-    new_second, new_left_t, new_right_t, new_moment = run(
+    new_moment, new_left_t, new_right_t = run(
         "factors",
         factor_kernel,
         [group, share, owner],
-        [gradient, new_second, left_t, right_t, moment],
-        [shape(square, f32), factor_t, factor_t, shape(square, bf16)],
-        scratch=[factor_t, factor_t, shape(square, bf16)] * 2,
-        sems=10,
-        far=3,
-        far_outs=4,
+        [gradient, moment, left_t, right_t],
+        [shape(square, bf16), factor_t, factor_t],
+        scratch=[shape(square, bf16), factor_t, factor_t],
+        sems=3,
+        far_outs=3,
         flops=product,
     )
     (update,) = run(
@@ -396,7 +431,9 @@
         [owner, offset],
         [returned],
         [shape((blocks, rows, col_share), bf16)],
-        far_outs=-1,
+        scratch=[shape((blocks, rows, col_share - LANES), bf16)],
+        sems=2 * blocks,
+        far_outs=1,
     )
     return (
         update,

time: 53.6 us -> 53.3 us (level); the launches traced: 52.6 us -> 53 us
  waiting for transfers between devices: 3.67 us -> 5.34 us
  starting transfers between devices: 15.2 us -> 13.8 us
  Pallas kernels: 6.78 us -> 7.88 us
  local copies, waits for them, and re-layouts: 1.66 us -> 0.68 us
    all_to_all x1, waiting for transfers between devices: 0.04 us -> 1.71 us  [per_device_packed(): lax.all_to_all(back, 'mp', split_axis=0, concat_axis=0, tiled=True, axis_...]
    all_to_all x1, starting transfers between devices: 8.17 us -> 6.73 us  [per_device_packed(): lax.all_to_all(back, 'mp', split_axis=0, concat_axis=0, tiled=True, axis_...]
    pallas_call x6, Pallas kernels: 6.78 us -> 7.88 us  [run(): pl.pallas_call(kernel, out_shape=[pltpu.VMEM(o.shape, o.dtype) for o in o...]
    unnamed x14 -> x12, local copies, waits for them, and re-layouts: 1.66 us -> 0.68 us
  transfers between devices with their start and end apart: 4 -> 4, of which waited for: 3 -> 4; matrix products, arithmetic and copies ran while one was open for 0% -> 0% of each run, Pallas kernels for 7% -> 4%
where the time goes in v5:
time: 53.3 us; the launch traced here: 53 us
  blocking collectives  24.6 us (46%)
  starting transfers between devices  13.8 us (26%)
  Pallas kernels  7.88 us (15%)
  waiting for transfers between devices  5.34 us (10%)
  between operations  0.72 us (1%)
  local copies, waits for them, and re-layouts  0.68 us (1%)
    all_to_all x1, blocking collectives, per_device_packed(): lax.all_to_all(outgoing, ('dp', 'mp'), split_axis=0, concat_axis=0, tiled...  24.6 us
    pallas_call x6, Pallas kernels, run(): pl.pallas_call(kernel, out_shape=[pltpu.VMEM(o.shape, o.dtype) for o in o...  7.88 us
    ppermute x3, starting transfers between devices, per_device_packed(): lax.ppermute(parts[s], 'dp', [(i, (i + s) % replicas) for i in range(repl...  7.04 us
    all_to_all x1, starting transfers between devices, per_device_packed(): lax.all_to_all(back, 'mp', split_axis=0, concat_axis=0, tiled=True, axis_...  6.73 us
    ppermute x3, waiting for transfers between devices, per_device_packed(): lax.ppermute(parts[s], 'dp', [(i, (i + s) % replicas) for i in range(repl...  3.63 us
    all_to_all x1, waiting for transfers between devices, per_device_packed(): lax.all_to_all(back, 'mp', split_axis=0, concat_axis=0, tiled=True, axis_...  1.71 us
  transfers between devices with their start and end apart: 4, of which 4 were waited for; matrix products, arithmetic and copies ran while one was open for 0% of the time, Pallas kernels for 4%

profile of v5, /device:TPU:0, one launch (start us, length us, event | category | flops | bytes accessed | tf_op | source)
XLA Modules:
  0.0 53.0 jit_solution(14964072433304603307)
XLA Ops:
  0.6 1.1 %pack.1 = (bf16[4,88,128]{2,1,0:T(8,128)(2,1)S(1)}, bf16[4,88,128]{2,1,0:T(8,128)(2,1)S(1)}, bf16[4,88,128]{2,1,0:T(8,128)(2,1)S(1)}, bf16[4,88,128]{2,1,0:T(8,128)(2,1)S(1)}) custom-call(s32[1]{0:T(128)} %bitcast.1.me_ref.share_ref, bf16[4,72,576]{2,1,0:T(8,128)(2,1)} %bitcast.28), custom_call_target="tpu_custom_call" | custom-call | bytes 692224 | tf_op jit(solution)/shard_map/pack/pallas_call | solution.py:311
  1.7 0.0 copy-start.5
  1.8 3.1 %collective-permute-start = (bf16[4,88,128]{2,1,0:T(8,128)(2,1)S(1)}, bf16[4,88,128]{2,1,0:T(8,128)(2,1)S(1)}, u32[]{:S(2)}, u32[]{:S(2)}) collective-permute-start(bf16[4,88,128]{2,1,0:T(8,128)(2,1)S(1)} %get-tuple-element.29), channel_id=1, source_target_pairs={{0,8},{8,16},{16,24},{24,0},{1,9},{9,17},{17,25},{25,1},{2,10},{10... | collective-permute-start | bytes 270344 | tf_op jit(solution)/shard_map/ppermute | solution.py:366
  4.9 2.6 %collective-permute-start.1 = (bf16[4,88,128]{2,1,0:T(8,128)(2,1)S(1)}, bf16[4,88,128]{2,1,0:T(8,128)(2,1)S(1)}, u32[]{:S(2)}, u32[]{:S(2)}) collective-permute-start(bf16[4,88,128]{2,1,0:T(8,128)(2,1)S(1)} %get-tuple-element.30), channel_id=1, source_target_pairs={{0,16},{8,24},{16,0},{24,8},{1,17},{9,25},{17,1},{25,9},{2,18},{10... | collective-permute-start | bytes 270344 | tf_op jit(solution)/shard_map/ppermute | solution.py:366
  7.4 1.3 %collective-permute-start.2 = (bf16[4,88,128]{2,1,0:T(8,128)(2,1)S(1)}, bf16[4,88,128]{2,1,0:T(8,128)(2,1)S(1)}, u32[]{:S(2)}, u32[]{:S(2)}) collective-permute-start(bf16[4,88,128]{2,1,0:T(8,128)(2,1)S(1)} %get-tuple-element.31), channel_id=1, source_target_pairs={{0,24},{8,0},{16,8},{24,16},{1,25},{9,1},{17,9},{25,17},{2,26},{10... | collective-permute-start | bytes 270344 | tf_op jit(solution)/shard_map/ppermute | solution.py:366
  8.8 0.7 %copy-done.3 = s32[4]{0:T(128)S(1)} copy-done((s32[4]{0:T(128)S(1)}, s32[4]{0:T(128)}, u32[]{:S(2)}) %copy-start.3) | copy-done | bytes 40
  9.5 0.6 %prepare.1 = (bf16[576,576]{1,0:T(8,128)(2,1)S(1)}, f32[576,576]{1,0:T(8,128)S(1)}, bf16[576,256]{1,0:T(8,128)(2,1)S(1)}) custom-call(s32[1]{0:T(128)} %bitcast.group_ref, s32[1]{0:T(128)} %bitcast.1.me_ref.share_ref, s32[4]{0:T(128)S(1)} %copy-done.3, bf16[576,576]{1,0:T(8,128)(2,1)} %bitcast.22, bf16[576,576]{1,0:T(8,128)(2,1)} %bitcast.24, ...), custom_call_target="tpu_custom_call" | custom-call | flops 764411904 | bytes 4276224 | tf_op jit(solution)/shard_map/prepare/pallas_call | solution.py:311
  10.0 0.0 copy-start
  10.0 0.0 copy-start.1
  10.1 0.0 copy-start.4
  10.1 0.1 collective-permute-done.refs_1_
  10.2 3.3 %collective-permute-done.1.refs_2_ = bf16[4,88,128]{2,1,0:T(8,128)(2,1)S(1)} collective-permute-done((bf16[4,88,128]{2,1,0:T(8,128)(2,1)S(1)}, bf16[4,88,128]{2,1,0:T(8,128)(2,1)S(1)}, u32[]{:S(2)}, u32[]{:S(2)}) %collective-permute-start.1) | collective-permute-done | bytes 90144 | tf_op jit(solution)/shard_map/ppermute | solution.py:366
  13.5 0.2 collective-permute-done.2.refs_3_
  13.7 0.0 copy-done.5
  13.7 0.7 %route.1 = bf16[32,88,128]{2,1,0:T(8,128)(2,1)S(1)} custom-call(s32[4]{0:T(128)S(1)} %copy-done.3, s32[4]{0:T(128)S(1)} %copy-done.5, bf16[4,88,128]{2,1,0:T(8,128)(2,1)S(1)} %get-tuple-element.35.refs_0_, bf16[4,88,128]{2,1,0:T(8,128)(2,1)S(1)} %collective-permute-done.refs_1_, bf16[4,88,128]{2,1,0:T(8,128)(2,1)S(1)} %collective-permute-done.1.refs_2_, ...), custom_call_target="tpu_custom_call" | custom-call | bytes 1081344 | tf_op jit(solution)/shard_map/route/pallas_call | solution.py:311
  14.4 24.6 %all_to_all.10.arrived = bf16[32,88,128]{2,1,0:T(8,128)(2,1)S(1)} all-to-all(bf16[32,88,128]{2,1,0:T(8,128)(2,1)S(1)} %route.1), channel_id=1, replica_groups=mesh['dp'=4,'mp'=8] {'dp','mp'}, dimensions={0} | all-to-all | bytes 1441792 | tf_op jit(solution)/shard_map/all_to_all | solution.py:391
  39.0 0.0 copy-done.2
  39.0 0.0 copy-done
  39.0 0.0 copy-done.1
  39.0 2.5 %owner_step.1 = (bf16[576,576]{1,0:T(8,128)(2,1)S(1)}, bf16[576,576]{1,0:T(8,128)(2,1)S(1)}, f32[144,576]{1,0:T(8,128)S(1)}, f32[144,576]{1,0:T(8,128)S(1)}, f32...) custom-call(s32[1]{0:T(128)} %bitcast.group_ref, s32[4]{0:T(128)S(1)} %copy-done.4, ...), custom_call_target="tpu_custom_call" | custom-call | flops 1146617856 | bytes 10485760 | tf_op jit(solution)/shard_map/owner_step/pallas_call | solution.py:311
  41.5 6.7 %all-to-all-start.1 = ((bf16[8,88,128]{2,1,0:T(8,128)(2,1)}), bf16[8,88,128]{2,1,0:T(8,128)(2,1)S(1)}, u32[]{:S(2)}, u32[]{:S(2)}) async-start(bf16[8,88,128]{2,1,0:T(8,128)(2,1)} %get-tuple-element.42), calls=%async_computation.1 | async-start | bytes 360448 | tf_op jit(solution)/shard_map/all_to_all | solution.py:409
  48.3 1.7 %factors.1 = (bf16[576,576]{1,0:T(8,128)(2,1)}, f32[144,576]{1,0:T(8,128)}, f32[144,576]{1,0:T(8,128)}) custom-call(s32[1]{0:T(128)} %bitcast.group_ref, s32[1]{0:T(128)} %bitcast.1.me_ref.share_ref, s32[4]{0:T(128)S(1)} %copy-done.4, bf16[576,576]{1,0:T(8,128)(2,1)S(1)} %get-tuple-element.43.gradient, bf16[576,576]{1,0:T(8,128)(2,1)S(1)} %get-tuple-element.44.moment, ...), custom_call_target="tpu_custom_call" | custom-call | flops 382205952 | bytes 3317760 | tf_op jit(solution)/shard_map/factors/pallas_call | solution.py:311
  50.0 1.7 %all-to-all-done.1.returned = bf16[8,88,128]{2,1,0:T(8,128)(2,1)S(1)} async-done(((bf16[8,88,128]{2,1,0:T(8,128)(2,1)}), bf16[8,88,128]{2,1,0:T(8,128)(2,1)S(1)}, u32[]{:S(2)}, u32[]{:S(2)}) %all-to-all-start.1) | async-done | bytes 180256 | tf_op jit(solution)/shard_map/all_to_all | solution.py:409
  51.7 1.3 %place.1 = bf16[4,72,144]{2,1,0:T(8,128)(2,1)} custom-call(s32[4]{0:T(128)S(1)} %copy-done.4, s32[4]{0:T(128)S(1)} %copy-done.5, bf16[8,88,128]{2,1,0:T(8,128)(2,1)S(1)} %all-to-all-done.1.returned), custom_call_target="tpu_custom_call" | custom-call | bytes 263168 | tf_op jit(solution)/shard_map/place/pallas_call | solution.py:311
  (3 shorter events, 0.0 us)
Async XLA Ops:
  1.7 12.0 %copy-start.5 = (s32[4]{0:T(128)S(1)}, s32[4]{0:T(128)}, u32[]{:S(2)}) copy-start(s32[4]{0:T(128)} %offset_ref.3) | copy-start | bytes 52
  1.8 8.4 %collective-permute-start = (bf16[4,88,128]{2,1,0:T(8,128)(2,1)S(1)}, bf16[4,88,128]{2,1,0:T(8,128)(2,1)S(1)}, u32[]{:S(2)}, u32[]{:S(2)}) collective-permute-start(bf16[4,88,128]{2,1,0:T(8,128)(2,1)S(1)} %get-tuple-element.29), channel_id=1, source_target_pairs={{0,8},{8,16},{16,24},{24,0},{1,9},{9,17},{17,25},{25,1},{2,10},{10... | collective-permute-start | bytes 270344 | tf_op jit(solution)/shard_map/ppermute | solution.py:366
  4.9 8.6 %collective-permute-start.1 = (bf16[4,88,128]{2,1,0:T(8,128)(2,1)S(1)}, bf16[4,88,128]{2,1,0:T(8,128)(2,1)S(1)}, u32[]{:S(2)}, u32[]{:S(2)}) collective-permute-start(bf16[4,88,128]{2,1,0:T(8,128)(2,1)S(1)} %get-tuple-element.30), channel_id=1, source_target_pairs={{0,16},{8,24},{16,0},{24,8},{1,17},{9,25},{17,1},{25,9},{2,18},{10... | collective-permute-start | bytes 270344 | tf_op jit(solution)/shard_map/ppermute | solution.py:366
  7.4 6.3 %collective-permute-start.2 = (bf16[4,88,128]{2,1,0:T(8,128)(2,1)S(1)}, bf16[4,88,128]{2,1,0:T(8,128)(2,1)S(1)}, u32[]{:S(2)}, u32[]{:S(2)}) collective-permute-start(bf16[4,88,128]{2,1,0:T(8,128)(2,1)S(1)} %get-tuple-element.31), channel_id=1, source_target_pairs={{0,24},{8,0},{16,8},{24,16},{1,25},{9,1},{17,9},{25,17},{2,26},{10... | collective-permute-start | bytes 270344 | tf_op jit(solution)/shard_map/ppermute | solution.py:366
  8.8 0.7 %copy-start.3 = (s32[4]{0:T(128)S(1)}, s32[4]{0:T(128)}, u32[]{:S(2)}) copy-start(s32[4]{0:T(128)} %owner_ref.9) | copy-start | bytes 52
  9.4 29.5 %copy-start.2 = (bf16[1,576,576]{2,1,0:T(8,128)(2,1)S(1)}, bf16[1,576,576]{2,1,0:T(8,128)(2,1)}, u32[]{:S(2)}) copy-start(bf16[1,576,576]{2,1,0:T(8,128)(2,1)} %param.15) | copy-start | bytes 1990660
  10.0 28.9 %copy-start = (f32[1,576,576]{2,1,0:T(8,128)S(1)}, f32[1,576,576]{2,1,0:T(8,128)}, u32[]{:S(2)}) copy-start(f32[1,576,576]{2,1,0:T(8,128)} %param.17) | copy-start | bytes 3981316
  10.0 28.9 %copy-start.1 = (bf16[1,576,576]{2,1,0:T(8,128)(2,1)S(1)}, bf16[1,576,576]{2,1,0:T(8,128)(2,1)}, u32[]{:S(2)}) copy-start(bf16[1,576,576]{2,1,0:T(8,128)(2,1)} %param.14) | copy-start | bytes 1990660
  10.1 28.9 %copy-start.4 = (s32[4]{0:T(128)S(1)}, s32[4]{0:T(128)}, u32[]{:S(2)}) copy-start(s32[4]{0:T(128)} %owner_ref.9) | copy-start | bytes 52
  41.5 10.1 %all-to-all-start.1 = ((bf16[8,88,128]{2,1,0:T(8,128)(2,1)}), bf16[8,88,128]{2,1,0:T(8,128)(2,1)S(1)}, u32[]{:S(2)}, u32[]{:S(2)}) async-start(bf16[8,88,128]{2,1,0:T(8,128)(2,1)} %get-tuple-element.42), calls=%async_computation.1 | async-start | bytes 360448 | tf_op jit(solution)/shard_map/all_to_all | solution.py:409

commit v6 on v5

--- a/solution.py
+++ b/solution.py
@@ -82,17 +82,26 @@
         copy.wait()
 
 
-def slot_of(owner_ref, group):
+SHARE, GROUP, FOUND, SLOTS = 0, 1, 2, 3
+
+
+def table_kernel(share_ref, group_ref, owner_ref, offset_ref, table):
+    blocks = owner_ref.shape[0]
+    groups = table.shape[0] - SLOTS - blocks
+    table[SHARE] = share_ref[0]
+    table[GROUP] = group_ref[0]
     found = jnp.int32(0)
-    block = jnp.int32(0)
-    for b in range(owner_ref.shape[0]):
-        hit = owner_ref[b] == group
-        block = jnp.where(hit, b, block)
-        found = jnp.where(hit, 1, found)
-    return block, found
-
-
-def route_kernel(owner_ref, offset_ref, *refs):
+    for b in range(blocks):
+        found = jnp.where(owner_ref[b] == group_ref[0], 1, found)
+    table[FOUND] = found
+    for group in range(groups):
+        table[SLOTS + group] = jnp.int32(0)
+    for b in range(blocks):
+        table[SLOTS + owner_ref[b]] = offset_ref[b]
+        table[SLOTS + groups + offset_ref[b]] = groups - 1 - owner_ref[b]
+
+
+def route_kernel(table, *refs):
     parts, out, summed = refs[:-2], refs[-2], refs[-1]
     replicas = len(parts)
     groups = out.shape[0] // replicas
@@ -103,17 +112,16 @@
             total = total + part[b].astype(jnp.float32)
         summed[b] = total.astype(jnp.bfloat16)
     for group in range(groups):
-        block, _ = slot_of(owner_ref, group)
-        piece = summed[offset_ref[block]]
+        piece = summed[table[SLOTS + group]]
         for r in range(replicas):
             out[r * groups + group] = piece
 
 
 def prepare_kernel(
-    group_ref, share_ref, owner_ref, lbasis_hbm, rbasis_hbm, moment_hbm,
+    table, lbasis_hbm, rbasis_hbm, moment_hbm,
     lbasis_t, old_part, back_basis, lbasis, rbasis, moment, sems,
 ):
-    _, found = slot_of(owner_ref, group_ref[0])
+    found = table[FOUND]
 
     @pl.when(found == 1)
     def _():
@@ -135,7 +143,7 @@
         columns = rbasis.shape[0]
         col_share = columns // (columns // LANES)
         tail = col_share - LANES
-        first = pl.multiple_of(share_ref[0] * col_share, tail)
+        first = pl.multiple_of(table[SHARE] * col_share, tail)
         main = rbasis[pl.ds(first, LANES), :]
         last = rbasis[pl.ds(pl.multiple_of(first + LANES, tail), tail), :]
         back_basis[...] = jnp.concatenate([main] + [last] * (LANES // tail), axis=0).T
@@ -160,12 +168,12 @@
 
 
 def owner_kernel(
-    group_ref, owner_ref, arrived, lbasis, rbasis, lbasis_t, old_part, back_basis, second,
+    table, arrived, lbasis, rbasis, lbasis_t, old_part, back_basis, second,
     moment_hbm, left_hbm, right_hbm,
     gradient, moment, left_t, right_t, second_out, back_out,
     turned, back, new_second, sems,
 ):
-    _, found = slot_of(owner_ref, group_ref[0])
+    found = table[FOUND]
     groups = back.shape[0]
     copies = [
         pltpu.make_async_copy(back.at[n], back_out.at[n], sems.at[n]) for n in range(groups)
@@ -231,10 +239,10 @@
 
 
 def factor_kernel(
-    group_ref, share_ref, owner_ref, gradient, moment, left_t, right_t,
+    table, gradient, moment, left_t, right_t,
     moment_out, left_out, right_out, new_moment, new_left_t, new_right_t, sems,
 ):
-    _, found = slot_of(owner_ref, group_ref[0])
+    found = table[FOUND]
     col_share, columns = left_t.shape
     outs = (moment_out, left_out, right_out)
     fresh, kept = (
@@ -251,7 +259,7 @@
                 + 0.1 * gradient[strip, :].astype(jnp.float32)
             ).astype(jnp.bfloat16)
         fresh[0].start()
-        first = pl.multiple_of(share_ref[0] * col_share, 16)
+        first = pl.multiple_of(table[SHARE] * col_share, 16)
         grad = gradient[...]
         new_left_t[...] = 0.95 * left_t[...] + 0.05 * contract_last(
             gradient[pl.ds(first, col_share), :], grad
@@ -274,29 +282,30 @@
             copy.wait()
 
 
-def place_kernel(owner_ref, offset_ref, returned, update, tails, sems):
+def place_kernel(table, returned, update, tails, sems):
     blocks, rows, col_share = update.shape
+    groups = returned.shape[0]
     tail_groups = rows // SUBLANES - 1
     width = col_share - LANES
     copies = []
-    for b in range(blocks):
-        place, slot = offset_ref[b], returned.shape[0] - 1 - owner_ref[b]
+    for place in range(blocks):
+        slot = table[SLOTS + groups + place]
         copies.append(
             pltpu.make_async_copy(
-                returned.at[slot, :rows], update.at[place, :, :LANES], sems.at[b]
+                returned.at[slot, :rows], update.at[place, :, :LANES], sems.at[place]
             )
         )
         copies[-1].start()
-    for b in range(blocks):
-        place, slot = offset_ref[b], returned.shape[0] - 1 - owner_ref[b]
+    for place in range(blocks):
+        slot = table[SLOTS + groups + place]
         for g in range(tail_groups):
-            tails[b, g * SUBLANES : (g + 1) * SUBLANES, :] = returned[
+            tails[place, g * SUBLANES : (g + 1) * SUBLANES, :] = returned[
                 slot, rows : rows + SUBLANES, g * width : (g + 1) * width
             ]
-        tails[b, rows - SUBLANES :, :] = returned[slot, rows + SUBLANES :, :width]
+        tails[place, rows - SUBLANES :, :] = returned[slot, rows + SUBLANES :, :width]
         copies.append(
             pltpu.make_async_copy(
-                tails.at[b], update.at[place, :, LANES:], sems.at[blocks + b]
+                tails.at[place], update.at[place, :, LANES:], sems.at[blocks + place]
             )
         )
         copies[-1].start()
@@ -366,10 +375,17 @@
         lax.ppermute(parts[s], "dp", [(i, (i + s) % replicas) for i in range(replicas)])
         for s in range(1, replicas)
     ]
+    table = pl.pallas_call(
+        table_kernel,
+        out_shape=pltpu.SMEM((SLOTS + groups + blocks,), jnp.int32),
+        in_specs=[SMEM] * 4,
+        out_specs=SMEM,
+        name="table",
+    )(share, group, owner, offset)
     lbasis_t, old_part, back_basis = run(
         "prepare",
         prepare_kernel,
-        [group, share, owner],
+        [table],
         [lbasis, rbasis, moment],
         [shape(square, bf16), shape(square, f32), shape((columns, 2 * LANES), bf16)],
         scratch=[shape(square, bf16)] * 3,
@@ -383,7 +399,7 @@
     (outgoing,) = run(
         "route",
         route_kernel,
-        [owner, offset],
+        [table],
         parts,
         [shape((replicas * groups,) + packed.shape[1:], bf16)],
         scratch=[packed],
@@ -394,7 +410,7 @@
     gradient, moment, left_t, right_t, new_second, back = run(
         "owner_step",
         owner_kernel,
-        [group, owner],
+        [table],
         [
             arrived, lbasis, rbasis, lbasis_t, old_part, back_basis, second, moment, left_t,
             right_t,
@@ -417,7 +433,7 @@
     new_moment, new_left_t, new_right_t = run(
         "factors",
         factor_kernel,
-        [group, share, owner],
+        [table],
         [gradient, moment, left_t, right_t],
         [shape(square, bf16), factor_t, factor_t],
         scratch=[shape(square, bf16), factor_t, factor_t],
@@ -428,7 +444,7 @@
     (update,) = run(
         "place",
         place_kernel,
-        [owner, offset],
+        [table],
         [returned],
         [shape((blocks, rows, col_share), bf16)],
         scratch=[shape((blocks, rows, col_share - LANES), bf16)],

time: 53.3 us -> 50.9 us (0.955)
  Pallas kernels: 7.88 us -> 12.1 us
  waiting for transfers between devices: 5.34 us -> 2.08 us
  starting transfers between devices: 13.8 us -> 11 us
  local copies, waits for them, and re-layouts: 0.68 us -> 0.02 us
    pallas_call x6, Pallas kernels: 7.88 us -> 11.4 us  [run(): pl.pallas_call(kernel, out_shape=[pltpu.VMEM(o.shape, o.dtype) for o in o...]
    ppermute x3, waiting for transfers between devices: 3.63 us -> 0.8 us  [per_device_packed(): lax.ppermute(parts[s], 'dp', [(i, (i + s) % replicas) for i in range(repl...]
    all_to_all x1, starting transfers between devices: 6.73 us -> 3.94 us  [per_device_packed(): lax.all_to_all(back, 'mp', split_axis=0, concat_axis=0, tiled=True, axis_...]
    pallas_call x0 -> x1, Pallas kernels: none -> 0.69 us  [per_device_packed(): pl.pallas_call(table_kernel, out_shape=pltpu.SMEM((SLOTS + groups + block...]
    unnamed x12 -> x6, local copies, waits for them, and re-layouts: 0.68 us -> 0.02 us
  transfers between devices with their start and end apart: 4 -> 4, of which waited for: 4 -> 3; matrix products, arithmetic and copies ran while one was open for 0% -> 0% of each run, Pallas kernels for 4% -> 13%
where the time goes in v6:
time: 50.9 us; the launch traced here: 50.5 us
  blocking collectives  24.6 us (48%)
  Pallas kernels  12.1 us (24%)
  starting transfers between devices  11 us (22%)
  waiting for transfers between devices  2.08 us (4%)
  between operations  0.72 us (1%)
    all_to_all x1, blocking collectives, per_device_packed(): lax.all_to_all(outgoing, ('dp', 'mp'), split_axis=0, concat_axis=0, tiled...  24.6 us
    pallas_call x6, Pallas kernels, run(): pl.pallas_call(kernel, out_shape=[pltpu.VMEM(o.shape, o.dtype) for o in o...  11.4 us
    ppermute x3, starting transfers between devices, per_device_packed(): lax.ppermute(parts[s], 'dp', [(i, (i + s) % replicas) for i in range(repl...  7.04 us
    all_to_all x1, starting transfers between devices, per_device_packed(): lax.all_to_all(back, 'mp', split_axis=0, concat_axis=0, tiled=True, axis_...  3.94 us
    all_to_all x1, waiting for transfers between devices, per_device_packed(): lax.all_to_all(back, 'mp', split_axis=0, concat_axis=0, tiled=True, axis_...  1.28 us
  transfers between devices with their start and end apart: 4, of which 3 were waited for; matrix products, arithmetic and copies ran while one was open for 0% of the time, Pallas kernels for 13%

profile of v6, /device:TPU:0, one launch (start us, length us, event | category | flops | bytes accessed | tf_op | source)
XLA Modules:
  0.0 50.5 jit_solution(15685156944089527924)
XLA Ops:
  0.6 1.1 %pack.1 = (bf16[4,88,128]{2,1,0:T(8,128)(2,1)S(1)}, bf16[4,88,128]{2,1,0:T(8,128)(2,1)S(1)}, bf16[4,88,128]{2,1,0:T(8,128)(2,1)S(1)}, bf16[4,88,128]{2,1,0:T(8,128)(2,1)S(1)}) custom-call(s32[1]{0:T(128)} %bitcast.share_ref.me_ref, bf16[4,72,576]{2,1,0:T(8,128)(2,1)} %bitcast.28), custom_call_target="tpu_custom_call" | custom-call | bytes 692224 | tf_op jit(solution)/shard_map/pack/pallas_call | solution.py:320
  1.7 3.1 %collective-permute-start = (bf16[4,88,128]{2,1,0:T(8,128)(2,1)S(1)}, bf16[4,88,128]{2,1,0:T(8,128)(2,1)S(1)}, u32[]{:S(2)}, u32[]{:S(2)}) collective-permute-start(bf16[4,88,128]{2,1,0:T(8,128)(2,1)S(1)} %get-tuple-element.29), channel_id=1, source_target_pairs={{0,8},{8,16},{16,24},{24,0},{1,9},{9,17},{17,25},{25,1},{2,10},{10... | collective-permute-start | bytes 270344 | tf_op jit(solution)/shard_map/ppermute | solution.py:375
  4.8 2.6 %collective-permute-start.1 = (bf16[4,88,128]{2,1,0:T(8,128)(2,1)S(1)}, bf16[4,88,128]{2,1,0:T(8,128)(2,1)S(1)}, u32[]{:S(2)}, u32[]{:S(2)}) collective-permute-start(bf16[4,88,128]{2,1,0:T(8,128)(2,1)S(1)} %get-tuple-element.30), channel_id=1, source_target_pairs={{0,16},{8,24},{16,0},{24,8},{1,17},{9,25},{17,1},{25,9},{2,18},{10... | collective-permute-start | bytes 270344 | tf_op jit(solution)/shard_map/ppermute | solution.py:375
  7.4 1.3 %collective-permute-start.2 = (bf16[4,88,128]{2,1,0:T(8,128)(2,1)S(1)}, bf16[4,88,128]{2,1,0:T(8,128)(2,1)S(1)}, u32[]{:S(2)}, u32[]{:S(2)}) collective-permute-start(bf16[4,88,128]{2,1,0:T(8,128)(2,1)S(1)} %get-tuple-element.31), channel_id=1, source_target_pairs={{0,24},{8,0},{16,8},{24,16},{1,25},{9,1},{17,9},{25,17},{2,26},{10... | collective-permute-start | bytes 270344 | tf_op jit(solution)/shard_map/ppermute | solution.py:375
  8.8 0.7 %table.1 = s32[15]{0:T(128)S(4)} custom-call(s32[1]{0:T(128)} %bitcast.share_ref.me_ref, s32[1]{0:T(128)} %bitcast.1.group_ref, s32[4]{0:T(128)} %owner_ref.1, s32[4]{0:T(128)} %offset_ref.1), custom_call_target="tpu_custom_call" | custom-call | tf_op jit(solution)/shard_map/table/pallas_call | solution.py:378
  9.5 0.0 copy-start.2
  9.5 3.4 %prepare.1 = (bf16[576,576]{1,0:T(8,128)(2,1)S(1)}, f32[576,576]{1,0:T(8,128)S(1)}, bf16[576,256]{1,0:T(8,128)(2,1)S(1)}) custom-call(s32[15]{0:T(128)S(4)} %table.1, bf16[576,576]{1,0:T(8,128)(2,1)} %bitcast.22, bf16[576,576]{1,0:T(8,128)(2,1)} %bitcast.24, bf16[576,576]{1,0:T(8,128)(2,1)} %bitcast.26), custom_call_target="tpu_custom_call" | custom-call | flops 764411904 | bytes 4276224 | tf_op jit(solution)/shard_map/prepare/pallas_call | solution.py:320
  12.9 0.0 copy-start
  12.9 0.0 copy-start.1
  12.9 0.0 collective-permute-done.refs_1_
  12.9 0.6 %collective-permute-done.1.refs_2_ = bf16[4,88,128]{2,1,0:T(8,128)(2,1)S(1)} collective-permute-done((bf16[4,88,128]{2,1,0:T(8,128)(2,1)S(1)}, bf16[4,88,128]{2,1,0:T(8,128)(2,1)S(1)}, u32[]{:S(2)}, u32[]{:S(2)}) %collective-permute-start.1) | collective-permute-done | bytes 90144 | tf_op jit(solution)/shard_map/ppermute | solution.py:375
  13.5 0.2 collective-permute-done.2.refs_3_
  13.7 0.1 route.1
  13.8 24.6 %all_to_all.10.arrived = bf16[32,88,128]{2,1,0:T(8,128)(2,1)S(1)} all-to-all(bf16[32,88,128]{2,1,0:T(8,128)(2,1)S(1)} %route.1), channel_id=1, replica_groups=mesh['dp'=4,'mp'=8] {'dp','mp'}, dimensions={0} | all-to-all | bytes 1441792 | tf_op jit(solution)/shard_map/all_to_all | solution.py:407
  38.4 0.0 copy-done.2
  38.4 0.0 copy-done
  38.4 0.0 copy-done.1
  38.4 3.7 %owner_step.1 = (bf16[576,576]{1,0:T(8,128)(2,1)S(1)}, bf16[576,576]{1,0:T(8,128)(2,1)S(1)}, f32[144,576]{1,0:T(8,128)S(1)}, f32[144,576]{1,0:T(8,128)S(1)}, f32...) custom-call(s32[15]{0:T(128)S(4)} %table.1, bf16[32,88,128]{2,1,0:T(8,128)(2,1)S(1)} %all_to_all.10.arrived, ...), custom_call_target="tpu_custom_call" | custom-call | flops 1146617856 | bytes 10485760 | tf_op jit(solution)/shard_map/owner_step/pallas_call | solution.py:320
  42.2 3.9 %all-to-all-start.1 = ((bf16[8,88,128]{2,1,0:T(8,128)(2,1)}), bf16[8,88,128]{2,1,0:T(8,128)(2,1)S(1)}, u32[]{:S(2)}, u32[]{:S(2)}) async-start(bf16[8,88,128]{2,1,0:T(8,128)(2,1)} %get-tuple-element.42), calls=%async_computation.1 | async-start | bytes 360448 | tf_op jit(solution)/shard_map/all_to_all | solution.py:425
  46.1 2.3 %factors.1 = (bf16[576,576]{1,0:T(8,128)(2,1)}, f32[144,576]{1,0:T(8,128)}, f32[144,576]{1,0:T(8,128)}) custom-call(s32[15]{0:T(128)S(4)} %table.1, bf16[576,576]{1,0:T(8,128)(2,1)S(1)} %get-tuple-element.43.gradient, bf16[576,576]{1,0:T(8,128)(2,1)S(1)} %get-tuple-element.44.moment, f32[144,576]{1,0:T(8,128)S(1)} %get-tuple-element.45.left_t, ...), custom_call_target="tpu_custom_call" | custom-call | flops 382205952 | bytes 3317760 | tf_op jit(solution)/shard_map/factors/pallas_call | solution.py:320
  48.4 1.3 %all-to-all-done.1.returned = bf16[8,88,128]{2,1,0:T(8,128)(2,1)S(1)} async-done(((bf16[8,88,128]{2,1,0:T(8,128)(2,1)}), bf16[8,88,128]{2,1,0:T(8,128)(2,1)S(1)}, u32[]{:S(2)}, u32[]{:S(2)}) %all-to-all-start.1) | async-done | bytes 180256 | tf_op jit(solution)/shard_map/all_to_all | solution.py:425
  49.7 0.8 %place.1 = bf16[4,72,144]{2,1,0:T(8,128)(2,1)} custom-call(s32[15]{0:T(128)S(4)} %table.1, bf16[8,88,128]{2,1,0:T(8,128)(2,1)S(1)} %all-to-all-done.1.returned), custom_call_target="tpu_custom_call" | custom-call | bytes 263168 | tf_op jit(solution)/shard_map/place/pallas_call | solution.py:320
Async XLA Ops:
  1.7 11.1 %collective-permute-start = (bf16[4,88,128]{2,1,0:T(8,128)(2,1)S(1)}, bf16[4,88,128]{2,1,0:T(8,128)(2,1)S(1)}, u32[]{:S(2)}, u32[]{:S(2)}) collective-permute-start(bf16[4,88,128]{2,1,0:T(8,128)(2,1)S(1)} %get-tuple-element.29), channel_id=1, source_target_pairs={{0,8},{8,16},{16,24},{24,0},{1,9},{9,17},{17,25},{25,1},{2,10},{10... | collective-permute-start | bytes 270344 | tf_op jit(solution)/shard_map/ppermute | solution.py:375
  4.8 8.6 %collective-permute-start.1 = (bf16[4,88,128]{2,1,0:T(8,128)(2,1)S(1)}, bf16[4,88,128]{2,1,0:T(8,128)(2,1)S(1)}, u32[]{:S(2)}, u32[]{:S(2)}) collective-permute-start(bf16[4,88,128]{2,1,0:T(8,128)(2,1)S(1)} %get-tuple-element.30), channel_id=1, source_target_pairs={{0,16},{8,24},{16,0},{24,8},{1,17},{9,25},{17,1},{25,9},{2,18},{10... | collective-permute-start | bytes 270344 | tf_op jit(solution)/shard_map/ppermute | solution.py:375
  7.4 6.3 %collective-permute-start.2 = (bf16[4,88,128]{2,1,0:T(8,128)(2,1)S(1)}, bf16[4,88,128]{2,1,0:T(8,128)(2,1)S(1)}, u32[]{:S(2)}, u32[]{:S(2)}) collective-permute-start(bf16[4,88,128]{2,1,0:T(8,128)(2,1)S(1)} %get-tuple-element.31), channel_id=1, source_target_pairs={{0,24},{8,0},{16,8},{24,16},{1,25},{9,1},{17,9},{25,17},{2,26},{10... | collective-permute-start | bytes 270344 | tf_op jit(solution)/shard_map/ppermute | solution.py:375
  9.5 28.9 %copy-start.2 = (bf16[1,576,576]{2,1,0:T(8,128)(2,1)S(1)}, bf16[1,576,576]{2,1,0:T(8,128)(2,1)}, u32[]{:S(2)}) copy-start(bf16[1,576,576]{2,1,0:T(8,128)(2,1)} %param.15) | copy-start | bytes 1990660
  12.9 25.6 %copy-start = (f32[1,576,576]{2,1,0:T(8,128)S(1)}, f32[1,576,576]{2,1,0:T(8,128)}, u32[]{:S(2)}) copy-start(f32[1,576,576]{2,1,0:T(8,128)} %param.17) | copy-start | bytes 3981316
  12.9 25.6 %copy-start.1 = (bf16[1,576,576]{2,1,0:T(8,128)(2,1)S(1)}, bf16[1,576,576]{2,1,0:T(8,128)(2,1)}, u32[]{:S(2)}) copy-start(bf16[1,576,576]{2,1,0:T(8,128)(2,1)} %param.14) | copy-start | bytes 1990660
  42.2 7.5 %all-to-all-start.1 = ((bf16[8,88,128]{2,1,0:T(8,128)(2,1)}), bf16[8,88,128]{2,1,0:T(8,128)(2,1)S(1)}, u32[]{:S(2)}, u32[]{:S(2)}) async-start(bf16[8,88,128]{2,1,0:T(8,128)(2,1)} %get-tuple-element.42), calls=%async_computation.1 | async-start | bytes 360448 | tf_op jit(solution)/shard_map/all_to_all | solution.py:425

commit v7 on v6

--- a/solution.py
+++ b/solution.py
@@ -169,25 +169,13 @@
 
 def owner_kernel(
     table, arrived, lbasis, rbasis, lbasis_t, old_part, back_basis, second,
-    moment_hbm, left_hbm, right_hbm,
-    gradient, moment, left_t, right_t, second_out, back_out,
-    turned, back, new_second, sems,
+    gradient, new_second, back_out, turned, scaled, back, sems,
 ):
     found = table[FOUND]
     groups = back.shape[0]
     copies = [
         pltpu.make_async_copy(back.at[n], back_out.at[n], sems.at[n]) for n in range(groups)
     ]
-    loads = [
-        pltpu.make_async_copy(source, target, sems.at[groups + n])
-        for n, (source, target) in enumerate(
-            ((moment_hbm, moment), (left_hbm, left_t), (right_hbm, right_t))
-        )
-    ]
-    fresh_copy = pltpu.make_async_copy(new_second, second_out, sems.at[groups + 3])
-    kept_copy = pltpu.make_async_copy(second, second_out, sems.at[groups + 4])
-    for load in loads:
-        load.start()
     columns = gradient.shape[1]
     rows = columns // groups
 
@@ -195,7 +183,6 @@
     def _():
         assemble(arrived, gradient, groups, rows)
         turned[...] = matmul(lbasis_t[...], gradient[...]).astype(jnp.bfloat16)
-        total = None
         for low in range(0, columns, CUT):
             cols = slice(low, min(low + CUT, columns))
             rotated = matmul(turned[...], rbasis[:, cols])
@@ -203,10 +190,8 @@
             new_second[:, cols] = fresh
             rotated_mom = old_part[:, cols] + 0.1 * rotated
             spread = fresh * lax.rsqrt(fresh) + 1e-08
-            scaled = (rotated_mom * lax.rsqrt(spread * spread)).astype(jnp.bfloat16)
-            term = matmul(scaled, back_basis[cols, :])
-            total = term if total is None else total + term
-        fresh_copy.start()
+            scaled[:, cols] = (rotated_mom * lax.rsqrt(spread * spread)).astype(jnp.bfloat16)
+        total = matmul(scaled[...], back_basis[...])
         result = matmul(lbasis[...], total.astype(jnp.bfloat16))
         lane = lax.broadcasted_iota(jnp.int32, (SUBLANES, LANES), 1)
         tail_groups = rows // SUBLANES - 1
@@ -226,60 +211,72 @@
             ].astype(jnp.bfloat16)
         for copy in copies:
             copy.start()
-        for copy in copies + [fresh_copy]:
+        for copy in copies:
             copy.wait()
 
     @pl.when(found == 0)
     def _():
-        kept_copy.start()
-        kept_copy.wait()
-
-    for load in loads:
-        load.wait()
+        new_second[...] = second[...]
 
 
 def factor_kernel(
-    table, gradient, moment, left_t, right_t,
-    moment_out, left_out, right_out, new_moment, new_left_t, new_right_t, sems,
+    table, gradient, second, moment_hbm, left_hbm, right_hbm,
+    second_out, moment_out, left_out, right_out,
+    moment, left_t, right_t, new_moment, new_left_t, new_right_t, sems,
 ):
     found = table[FOUND]
     col_share, columns = left_t.shape
+    held = (moment, left_t, right_t)
     outs = (moment_out, left_out, right_out)
-    fresh, kept = (
-        [pltpu.make_async_copy(a, b, sems.at[n]) for n, (a, b) in enumerate(zip(sources, outs))]
-        for sources in ((new_moment, new_left_t, new_right_t), (moment, left_t, right_t))
-    )
+
+    def copies_of(first, sources, targets):
+        return [
+            pltpu.make_async_copy(a, b, sems.at[first + n])
+            for n, (a, b) in enumerate(zip(sources, targets))
+        ]
+
+    loads = copies_of(0, (left_hbm, right_hbm, moment_hbm), (left_t, right_t, moment))
+    fresh = copies_of(3, (new_left_t, new_right_t, new_moment), (left_out, right_out, moment_out))
+    kept = copies_of(6, held, outs)
+    second_copy = pltpu.make_async_copy(second, second_out, sems.at[9])
+    for copy in loads + [second_copy]:
+        copy.start()
 
     @pl.when(found == 1)
     def _():
+        first = pl.multiple_of(table[SHARE] * col_share, 16)
+        grad = gradient[...]
+        left_term = 0.05 * contract_last(gradient[pl.ds(first, col_share), :], grad)
+        picked = lax.broadcasted_iota(jnp.int32, (col_share, columns), 0) + first
+        places = lax.broadcasted_iota(jnp.int32, (col_share, columns), 1)
+        pick = jnp.where(picked == places, 1.0, 0.0).astype(jnp.bfloat16)
+        grad_cols_t = contract_last(pick, grad).astype(jnp.bfloat16)
+        right_term = 0.05 * matmul(grad_cols_t, grad)
+        for copy in loads:
+            copy.wait()
+        new_left_t[...] = 0.95 * left_t[...] + left_term
+        new_right_t[...] = 0.95 * right_t[...] + right_term
         for low in range(0, columns, STRIP):
             strip = slice(low, min(low + STRIP, columns))
             new_moment[strip, :] = (
                 0.9 * moment[strip, :].astype(jnp.float32)
                 + 0.1 * gradient[strip, :].astype(jnp.float32)
             ).astype(jnp.bfloat16)
-        fresh[0].start()
-        first = pl.multiple_of(table[SHARE] * col_share, 16)
-        grad = gradient[...]
-        new_left_t[...] = 0.95 * left_t[...] + 0.05 * contract_last(
-            gradient[pl.ds(first, col_share), :], grad
-        )
-        picked = lax.broadcasted_iota(jnp.int32, (col_share, columns), 0) + first
-        places = lax.broadcasted_iota(jnp.int32, (col_share, columns), 1)
-        pick = jnp.where(picked == places, 1.0, 0.0).astype(jnp.bfloat16)
-        grad_cols_t = contract_last(pick, grad).astype(jnp.bfloat16)
-        new_right_t[...] = 0.95 * right_t[...] + 0.05 * matmul(grad_cols_t, grad)
-        for copy in fresh[1:]:
+        for copy in fresh:
             copy.start()
         for copy in fresh:
             copy.wait()
 
     @pl.when(found == 0)
     def _():
+        for copy in loads:
+            copy.wait()
         for copy in kept:
             copy.start()
         for copy in kept:
             copy.wait()
+
+    second_copy.wait()
 
 
 def place_kernel(table, returned, update, tails, sems):
@@ -407,19 +404,15 @@
     arrived = lax.all_to_all(outgoing, ("dp", "mp"), split_axis=0, concat_axis=0, tiled=True)
     chunks = shape((groups, rows + 2 * SUBLANES, LANES), bf16)
     factor_t = shape(left_t.shape, f32)
-    gradient, moment, left_t, right_t, new_second, back = run(
+    gradient, new_second, back = run(
         "owner_step",
         owner_kernel,
         [table],
-        [
-            arrived, lbasis, rbasis, lbasis_t, old_part, back_basis, second, moment, left_t,
-            right_t,
-        ],
-        [shape(square, bf16)] * 2 + [factor_t] * 2 + [shape(square, f32), chunks],
-        scratch=[shape(square, bf16), chunks, shape(square, f32)],
-        sems=groups + 5,
-        far=3,
-        far_outs=2,
+        [arrived, lbasis, rbasis, lbasis_t, old_part, back_basis, second],
+        [shape(square, bf16), shape(square, f32), chunks],
+        scratch=[shape(square, bf16)] * 2 + [chunks],
+        sems=groups,
+        far_outs=1,
         flops=3 * product,
     )
     returned = lax.all_to_all(
@@ -430,15 +423,16 @@
         tiled=True,
         axis_index_groups=[list(range(groups))[::-1]],
     )
-    new_moment, new_left_t, new_right_t = run(
+    new_second, new_moment, new_left_t, new_right_t = run(
         "factors",
         factor_kernel,
         [table],
-        [gradient, moment, left_t, right_t],
-        [shape(square, bf16), factor_t, factor_t],
-        scratch=[shape(square, bf16), factor_t, factor_t],
-        sems=3,
-        far_outs=3,
+        [gradient, new_second, moment, left_t, right_t],
+        [shape(square, f32), shape(square, bf16), factor_t, factor_t],
+        scratch=[shape(square, bf16), factor_t, factor_t] * 2,
+        sems=10,
+        far=3,
+        far_outs=4,
         flops=product,
     )
     (update,) = run(

time: 50.9 us -> 51.2 us (level)
  Pallas kernels: 12.1 us -> 5.98 us
  starting transfers between devices: 11 us -> 15.1 us
  waiting for transfers between devices: 2.08 us -> 4.45 us
    pallas_call x6, Pallas kernels: 11.4 us -> 5.29 us  [run(): pl.pallas_call(kernel, out_shape=[pltpu.VMEM(o.shape, o.dtype) for o in o...]
    all_to_all x1, starting transfers between devices: 3.94 us -> 8.04 us  [per_device_packed(): lax.all_to_all(back, 'mp', split_axis=0, concat_axis=0, tiled=True, axis_...]
    ppermute x3, waiting for transfers between devices: 0.8 us -> 4.13 us  [per_device_packed(): lax.ppermute(parts[s], 'dp', [(i, (i + s) % replicas) for i in range(repl...]
    all_to_all x1, waiting for transfers between devices: 1.28 us -> 0.32 us  [per_device_packed(): lax.all_to_all(back, 'mp', split_axis=0, concat_axis=0, tiled=True, axis_...]
  transfers between devices with their start and end apart: 4 -> 4, of which waited for: 3 -> 4; matrix products, arithmetic and copies ran while one was open for 0% -> 0% of each run, Pallas kernels for 13% -> 7%
where the time goes in v7:
time: 51.2 us; the launch traced here: 50.8 us
  blocking collectives  24.6 us (48%)
  starting transfers between devices  15.1 us (29%)
  Pallas kernels  5.98 us (12%)
  waiting for transfers between devices  4.45 us (9%)
  between operations  0.71 us (1%)
    all_to_all x1, blocking collectives, per_device_packed(): lax.all_to_all(outgoing, ('dp', 'mp'), split_axis=0, concat_axis=0, tiled...  24.6 us
    all_to_all x1, starting transfers between devices, per_device_packed(): lax.all_to_all(back, 'mp', split_axis=0, concat_axis=0, tiled=True, axis_...  8.04 us
    ppermute x3, starting transfers between devices, per_device_packed(): lax.ppermute(parts[s], 'dp', [(i, (i + s) % replicas) for i in range(repl...  7.04 us
    pallas_call x6, Pallas kernels, run(): pl.pallas_call(kernel, out_shape=[pltpu.VMEM(o.shape, o.dtype) for o in o...  5.29 us
    ppermute x3, waiting for transfers between devices, per_device_packed(): lax.ppermute(parts[s], 'dp', [(i, (i + s) % replicas) for i in range(repl...  4.13 us
  transfers between devices with their start and end apart: 4, of which 4 were waited for; matrix products, arithmetic and copies ran while one was open for 0% of the time, Pallas kernels for 7%

profile of v7, /device:TPU:0, one launch (start us, length us, event | category | flops | bytes accessed | tf_op | source)
XLA Modules:
  0.0 50.8 jit_solution(10147204173232801618)
XLA Ops:
  0.6 1.1 %pack.1 = (bf16[4,88,128]{2,1,0:T(8,128)(2,1)S(1)}, bf16[4,88,128]{2,1,0:T(8,128)(2,1)S(1)}, bf16[4,88,128]{2,1,0:T(8,128)(2,1)S(1)}, bf16[4,88,128]{2,1,0:T(8,128)(2,1)S(1)}) custom-call(s32[1]{0:T(128)} %bitcast.share_ref.me_ref, bf16[4,72,576]{2,1,0:T(8,128)(2,1)} %bitcast.28), custom_call_target="tpu_custom_call" | custom-call | bytes 692224 | tf_op jit(solution)/shard_map/pack/pallas_call | solution.py:317
  1.7 3.1 %collective-permute-start = (bf16[4,88,128]{2,1,0:T(8,128)(2,1)S(1)}, bf16[4,88,128]{2,1,0:T(8,128)(2,1)S(1)}, u32[]{:S(2)}, u32[]{:S(2)}) collective-permute-start(bf16[4,88,128]{2,1,0:T(8,128)(2,1)S(1)} %get-tuple-element.27), channel_id=1, source_target_pairs={{0,8},{8,16},{16,24},{24,0},{1,9},{9,17},{17,25},{25,1},{2,10},{10... | collective-permute-start | bytes 270344 | tf_op jit(solution)/shard_map/ppermute | solution.py:372
  4.8 2.6 %collective-permute-start.1 = (bf16[4,88,128]{2,1,0:T(8,128)(2,1)S(1)}, bf16[4,88,128]{2,1,0:T(8,128)(2,1)S(1)}, u32[]{:S(2)}, u32[]{:S(2)}) collective-permute-start(bf16[4,88,128]{2,1,0:T(8,128)(2,1)S(1)} %get-tuple-element.28), channel_id=1, source_target_pairs={{0,16},{8,24},{16,0},{24,8},{1,17},{9,25},{17,1},{25,9},{2,18},{10... | collective-permute-start | bytes 270344 | tf_op jit(solution)/shard_map/ppermute | solution.py:372
  7.4 1.3 %collective-permute-start.2 = (bf16[4,88,128]{2,1,0:T(8,128)(2,1)S(1)}, bf16[4,88,128]{2,1,0:T(8,128)(2,1)S(1)}, u32[]{:S(2)}, u32[]{:S(2)}) collective-permute-start(bf16[4,88,128]{2,1,0:T(8,128)(2,1)S(1)} %get-tuple-element.29), channel_id=1, source_target_pairs={{0,24},{8,0},{16,8},{24,16},{1,25},{9,1},{17,9},{25,17},{2,26},{10... | collective-permute-start | bytes 270344 | tf_op jit(solution)/shard_map/ppermute | solution.py:372
  8.8 0.7 %table.1 = s32[15]{0:T(128)S(4)} custom-call(s32[1]{0:T(128)} %bitcast.share_ref.me_ref, s32[1]{0:T(128)} %bitcast.1.group_ref, s32[4]{0:T(128)} %owner_ref.1, s32[4]{0:T(128)} %offset_ref.1), custom_call_target="tpu_custom_call" | custom-call | tf_op jit(solution)/shard_map/table/pallas_call | solution.py:375
  9.5 0.0 copy-start.2
  9.5 0.0 copy-start
  9.5 0.0 copy-start.1
  9.6 0.6 %collective-permute-done.refs_1_ = bf16[4,88,128]{2,1,0:T(8,128)(2,1)S(1)} collective-permute-done((bf16[4,88,128]{2,1,0:T(8,128)(2,1)S(1)}, bf16[4,88,128]{2,1,0:T(8,128)(2,1)S(1)}, u32[]{:S(2)}, u32[]{:S(2)}) %collective-permute-start) | collective-permute-done | bytes 90144 | tf_op jit(solution)/shard_map/ppermute | solution.py:372
  10.2 3.3 %collective-permute-done.1.refs_2_ = bf16[4,88,128]{2,1,0:T(8,128)(2,1)S(1)} collective-permute-done((bf16[4,88,128]{2,1,0:T(8,128)(2,1)S(1)}, bf16[4,88,128]{2,1,0:T(8,128)(2,1)S(1)}, u32[]{:S(2)}, u32[]{:S(2)}) %collective-permute-start.1) | collective-permute-done | bytes 90144 | tf_op jit(solution)/shard_map/ppermute | solution.py:372
  13.5 0.2 collective-permute-done.2.refs_3_
  13.7 0.1 route.1
  13.8 24.6 %all_to_all.10.arrived = bf16[32,88,128]{2,1,0:T(8,128)(2,1)S(1)} all-to-all(bf16[32,88,128]{2,1,0:T(8,128)(2,1)S(1)} %route.1), channel_id=1, replica_groups=mesh['dp'=4,'mp'=8] {'dp','mp'}, dimensions={0} | all-to-all | bytes 1441792 | tf_op jit(solution)/shard_map/all_to_all | solution.py:404
  38.4 0.0 copy-done.2
  38.4 0.0 copy-done
  38.4 0.0 copy-done.1
  38.4 0.2 owner_step.1
  38.6 8.0 %all-to-all-start.1 = ((bf16[8,88,128]{2,1,0:T(8,128)(2,1)}), bf16[8,88,128]{2,1,0:T(8,128)(2,1)S(1)}, u32[]{:S(2)}, u32[]{:S(2)}) async-start(bf16[8,88,128]{2,1,0:T(8,128)(2,1)} %get-tuple-element.40), calls=%async_computation.1 | async-start | bytes 360448 | tf_op jit(solution)/shard_map/all_to_all | solution.py:418
  46.7 3.1 %factors.1 = (f32[576,576]{1,0:T(8,128)}, bf16[576,576]{1,0:T(8,128)(2,1)}, f32[144,576]{1,0:T(8,128)}, f32[144,576]{1,0:T(8,128)}) custom-call(s32[15]{0:T(128)S(4)} %table.1, bf16[576,576]{1,0:T(8,128)(2,1)S(1)} %get-tuple-element.41.gradient, f32[576,576]{1,0:T(8,128)S(1)} %get-tuple-element.42.second, bf16[576,576]{1,0:T(8,128)(2,1)} %bitcast.27, ...), custom_call_target="tpu_custom_call" | custom-call | flops 382205952 | bytes 5971968 | tf_op jit(solution)/shard_map/factors/pallas_call | solution.py:317
  49.7 0.3 all-to-all-done.1.returned
  50.1 0.8 %place.1 = bf16[4,72,144]{2,1,0:T(8,128)(2,1)} custom-call(s32[15]{0:T(128)S(4)} %table.1, bf16[8,88,128]{2,1,0:T(8,128)(2,1)S(1)} %all-to-all-done.1.returned), custom_call_target="tpu_custom_call" | custom-call | bytes 263168 | tf_op jit(solution)/shard_map/place/pallas_call | solution.py:317
  (1 shorter events, 0.0 us)
Async XLA Ops:
  1.7 8.4 %collective-permute-start = (bf16[4,88,128]{2,1,0:T(8,128)(2,1)S(1)}, bf16[4,88,128]{2,1,0:T(8,128)(2,1)S(1)}, u32[]{:S(2)}, u32[]{:S(2)}) collective-permute-start(bf16[4,88,128]{2,1,0:T(8,128)(2,1)S(1)} %get-tuple-element.27), channel_id=1, source_target_pairs={{0,8},{8,16},{16,24},{24,0},{1,9},{9,17},{17,25},{25,1},{2,10},{10... | collective-permute-start | bytes 270344 | tf_op jit(solution)/shard_map/ppermute | solution.py:372
  4.8 8.6 %collective-permute-start.1 = (bf16[4,88,128]{2,1,0:T(8,128)(2,1)S(1)}, bf16[4,88,128]{2,1,0:T(8,128)(2,1)S(1)}, u32[]{:S(2)}, u32[]{:S(2)}) collective-permute-start(bf16[4,88,128]{2,1,0:T(8,128)(2,1)S(1)} %get-tuple-element.28), channel_id=1, source_target_pairs={{0,16},{8,24},{16,0},{24,8},{1,17},{9,25},{17,1},{25,9},{2,18},{10... | collective-permute-start | bytes 270344 | tf_op jit(solution)/shard_map/ppermute | solution.py:372
  7.4 6.3 %collective-permute-start.2 = (bf16[4,88,128]{2,1,0:T(8,128)(2,1)S(1)}, bf16[4,88,128]{2,1,0:T(8,128)(2,1)S(1)}, u32[]{:S(2)}, u32[]{:S(2)}) collective-permute-start(bf16[4,88,128]{2,1,0:T(8,128)(2,1)S(1)} %get-tuple-element.29), channel_id=1, source_target_pairs={{0,24},{8,0},{16,8},{24,16},{1,25},{9,1},{17,9},{25,17},{2,26},{10... | collective-permute-start | bytes 270344 | tf_op jit(solution)/shard_map/ppermute | solution.py:372
  9.5 28.9 %copy-start.2 = (bf16[1,576,576]{2,1,0:T(8,128)(2,1)S(1)}, bf16[1,576,576]{2,1,0:T(8,128)(2,1)}, u32[]{:S(2)}) copy-start(bf16[1,576,576]{2,1,0:T(8,128)(2,1)} %param.15) | copy-start | bytes 1990660
  9.5 28.9 %copy-start = (f32[1,576,576]{2,1,0:T(8,128)S(1)}, f32[1,576,576]{2,1,0:T(8,128)}, u32[]{:S(2)}) copy-start(f32[1,576,576]{2,1,0:T(8,128)} %param.17) | copy-start | bytes 3981316
  9.5 28.9 %copy-start.1 = (bf16[1,576,576]{2,1,0:T(8,128)(2,1)S(1)}, bf16[1,576,576]{2,1,0:T(8,128)(2,1)}, u32[]{:S(2)}) copy-start(bf16[1,576,576]{2,1,0:T(8,128)(2,1)} %param.14) | copy-start | bytes 1990660
  38.6 11.4 %all-to-all-start.1 = ((bf16[8,88,128]{2,1,0:T(8,128)(2,1)}), bf16[8,88,128]{2,1,0:T(8,128)(2,1)S(1)}, u32[]{:S(2)}, u32[]{:S(2)}) async-start(bf16[8,88,128]{2,1,0:T(8,128)(2,1)} %get-tuple-element.40), calls=%async_computation.1 | async-start | bytes 360448 | tf_op jit(solution)/shard_map/all_to_all | solution.py:418

commit v8 on v7

--- a/solution.py
+++ b/solution.py
@@ -47,37 +47,50 @@
     )
 
 
+def tail_places(blocks, rows):
+    for b in range(blocks):
+        for g in range(3):
+            place = 3 * b + g
+            yield b, g, blocks * rows + place // 2 * SUBLANES, place % 2 * (LANES // 2)
+
+
+def chunk_rows(blocks, rows):
+    return blocks * rows + -(-3 * blocks // 2) * SUBLANES
+
+
 def pack_kernel(me_ref, grad_hbm, *refs):
     outs, last, sems = refs[:-2], refs[-2], refs[-1]
     replicas = len(outs)
     blocks, rows, columns = grad_hbm.shape
     half = LANES // 2
-    copies = [pltpu.make_async_copy(grad_hbm.at[:, :, columns - half :], last, sems.at[replicas])]
+    shares = [lax.rem(me_ref[0] + step, replicas) for step in range(replicas)]
+    copies = [
+        pltpu.make_async_copy(
+            grad_hbm.at[:, :, columns - half :], last, sems.at[replicas * blocks]
+        )
+    ]
     for step in range(replicas):
-        share = lax.rem(me_ref[0] + step, replicas)
-        col = pl.multiple_of(share * LANES, LANES)
-        copies.append(
-            pltpu.make_async_copy(
-                grad_hbm.at[:, :, pl.ds(col, LANES)], outs[step].at[:, :rows, :], sems.at[step]
+        col = pl.multiple_of(shares[step] * LANES, LANES)
+        for b in range(blocks):
+            copies.append(
+                pltpu.make_async_copy(
+                    grad_hbm.at[b, :, pl.ds(col, LANES)],
+                    outs[step].at[b * rows : (b + 1) * rows, :],
+                    sems.at[step * blocks + b],
+                )
             )
-        )
     for copy in copies:
         copy.start()
     copies[0].wait()
     for step in range(replicas):
-        share = lax.rem(me_ref[0] + step, replicas)
-        start = tail_start(share)
-        row = pl.multiple_of(start * SUBLANES, SUBLANES)
-        row_next = pl.multiple_of(row + SUBLANES, SUBLANES)
-        row_third = pl.multiple_of(
-            jnp.minimum(start + 2, rows // SUBLANES - 1) * SUBLANES, SUBLANES
-        )
-        out = outs[step]
-        for b in range(blocks):
-            out[b, rows : rows + SUBLANES, :half] = last[b, pl.ds(row, SUBLANES), :]
-            out[b, rows + SUBLANES :, :half] = last[b, pl.ds(row_next, SUBLANES), :]
-            out[b, rows : rows + SUBLANES, half:] = last[b, pl.ds(row_third, SUBLANES), :]
-            out[b, rows + SUBLANES :, half:] = jnp.zeros((SUBLANES, half), out.dtype)
+        start = tail_start(shares[step])
+        for b, g, row, lane in tail_places(blocks, rows):
+            source = pl.multiple_of(
+                jnp.minimum(start + g, rows // SUBLANES - 1) * SUBLANES, SUBLANES
+            )
+            outs[step][row : row + SUBLANES, lane : lane + half] = last[
+                b, pl.ds(source, SUBLANES), :
+            ]
     for copy in copies[1:]:
         copy.wait()
 
@@ -106,11 +119,24 @@
     replicas = len(parts)
     groups = out.shape[0] // replicas
     blocks = summed.shape[0]
+    rows = summed.shape[1] - 2 * SUBLANES
+    half = LANES // 2
+
+    def add(*index):
+        total = parts[0][index].astype(jnp.float32)
+        for part in parts[1:]:
+            total = total + part[index].astype(jnp.float32)
+        return total.astype(jnp.bfloat16)
+
     for b in range(blocks):
-        total = parts[0][b].astype(jnp.float32)
-        for part in parts[1:]:
-            total = total + part[b].astype(jnp.float32)
-        summed[b] = total.astype(jnp.bfloat16)
+        summed[b, :rows, :] = add(slice(b * rows, (b + 1) * rows), slice(None))
+        summed[b, rows + SUBLANES :, half:] = jnp.zeros((SUBLANES, half), jnp.bfloat16)
+    for b, g, row, lane in tail_places(blocks, rows):
+        below = rows + (g % 2) * SUBLANES
+        beside = (g // 2) * half
+        summed[b, below : below + SUBLANES, beside : beside + half] = add(
+            slice(row, row + SUBLANES), slice(lane, lane + half)
+        )
     for group in range(groups):
         piece = summed[table[SLOTS + group]]
         for r in range(replicas):
@@ -353,6 +379,7 @@
     bf16, f32 = jnp.bfloat16, jnp.float32
     shape = jax.ShapeDtypeStruct
     packed = shape((blocks, rows + 2 * SUBLANES, LANES), bf16)
+    sent = shape((chunk_rows(blocks, rows), LANES), bf16)
     square = (columns, columns)
     lbasis, rbasis, moment, second = left_basis[0], right_basis[0], momentum[0], second_moment[0]
     left_t, right_t = left_factor[0].T, right_factor[0].T
@@ -363,9 +390,9 @@
         pack_kernel,
         [share],
         [pieces],
-        [packed] * replicas,
+        [sent] * replicas,
         scratch=[shape((blocks, rows, LANES // 2), bf16)],
-        sems=replicas + 1,
+        sems=replicas * blocks + 1,
         far=1,
     )
     parts = [parts[0]] + [

time: 51.2 us -> 50.3 us (0.982)
  starting transfers between devices: 15.1 us -> 14.1 us
    all_to_all x1, starting transfers between devices: 8.04 us -> 7.09 us  [per_device_packed(): lax.all_to_all(back, 'mp', split_axis=0, concat_axis=0, tiled=True, axis_...]
  transfers between devices with their start and end apart: 4 -> 4, of which waited for: 4 -> 4; matrix products, arithmetic and copies ran while one was open for 0% -> 0% of each run, Pallas kernels for 7% -> 8%
where the time goes in v8:
time: 50.3 us; the launch traced here: 50 us
  blocking collectives  24.5 us (49%)
  starting transfers between devices  14.1 us (28%)
  Pallas kernels  6.08 us (12%)
  waiting for transfers between devices  4.56 us (9%)
  between operations  0.71 us (1%)
    all_to_all x1, blocking collectives, per_device_packed(): lax.all_to_all(outgoing, ('dp', 'mp'), split_axis=0, concat_axis=0, tiled...  24.5 us
    all_to_all x1, starting transfers between devices, per_device_packed(): lax.all_to_all(back, 'mp', split_axis=0, concat_axis=0, tiled=True, axis_...  7.09 us
    ppermute x3, starting transfers between devices, per_device_packed(): lax.ppermute(parts[s], 'dp', [(i, (i + s) % replicas) for i in range(repl...  7.04 us
    pallas_call x6, Pallas kernels, run(): pl.pallas_call(kernel, out_shape=[pltpu.VMEM(o.shape, o.dtype) for o in o...  5.39 us
    ppermute x3, waiting for transfers between devices, per_device_packed(): lax.ppermute(parts[s], 'dp', [(i, (i + s) % replicas) for i in range(repl...  3.86 us
  transfers between devices with their start and end apart: 4, of which 4 were waited for; matrix products, arithmetic and copies ran while one was open for 0% of the time, Pallas kernels for 8%

profile of v8, /device:TPU:0, one launch (start us, length us, event | category | flops | bytes accessed | tf_op | source)
XLA Modules:
  0.0 50.0 jit_solution(7246555281689233939)
XLA Ops:
  0.6 1.2 %pack.1 = (bf16[336,128]{1,0:T(8,128)(2,1)S(1)}, bf16[336,128]{1,0:T(8,128)(2,1)S(1)}, bf16[336,128]{1,0:T(8,128)(2,1)S(1)}, bf16[336,128]{1,0:T(8,128)(2,1)S(1)}) custom-call(s32[1]{0:T(128)} %bitcast.share_ref.me_ref, bf16[4,72,576]{2,1,0:T(8,128)(2,1)} %bitcast.28), custom_call_target="tpu_custom_call" | custom-call | bytes 675840 | tf_op jit(solution)/shard_map/pack/pallas_call | solution.py:343
  1.8 3.1 %collective-permute-start = (bf16[336,128]{1,0:T(8,128)(2,1)S(1)}, bf16[336,128]{1,0:T(8,128)(2,1)S(1)}, u32[]{:S(2)}, u32[]{:S(2)}) collective-permute-start(bf16[336,128]{1,0:T(8,128)(2,1)S(1)} %get-tuple-element.27), channel_id=1, source_target_pairs={{0,8},{8,16},{16,24},{24,0},{1,9},{9,17},{17,25},{25,1},{2,10},{10... | collective-permute-start | bytes 258056 | tf_op jit(solution)/shard_map/ppermute | solution.py:399
  4.9 2.6 %collective-permute-start.1 = (bf16[336,128]{1,0:T(8,128)(2,1)S(1)}, bf16[336,128]{1,0:T(8,128)(2,1)S(1)}, u32[]{:S(2)}, u32[]{:S(2)}) collective-permute-start(bf16[336,128]{1,0:T(8,128)(2,1)S(1)} %get-tuple-element.28), channel_id=1, source_target_pairs={{0,16},{8,24},{16,0},{24,8},{1,17},{9,25},{17,1},{25,9},{2,18},{10... | collective-permute-start | bytes 258056 | tf_op jit(solution)/shard_map/ppermute | solution.py:399
  7.5 1.3 %collective-permute-start.2 = (bf16[336,128]{1,0:T(8,128)(2,1)S(1)}, bf16[336,128]{1,0:T(8,128)(2,1)S(1)}, u32[]{:S(2)}, u32[]{:S(2)}) collective-permute-start(bf16[336,128]{1,0:T(8,128)(2,1)S(1)} %get-tuple-element.29), channel_id=1, source_target_pairs={{0,24},{8,0},{16,8},{24,16},{1,25},{9,1},{17,9},{25,17},{2,26},{10... | collective-permute-start | bytes 258056 | tf_op jit(solution)/shard_map/ppermute | solution.py:399
  8.8 0.7 %table.1 = s32[15]{0:T(128)S(4)} custom-call(s32[1]{0:T(128)} %bitcast.share_ref.me_ref, s32[1]{0:T(128)} %bitcast.1.group_ref, s32[4]{0:T(128)} %owner_ref.1, s32[4]{0:T(128)} %offset_ref.1), custom_call_target="tpu_custom_call" | custom-call | tf_op jit(solution)/shard_map/table/pallas_call | solution.py:402
  9.5 0.0 copy-start.2
  9.6 0.0 copy-start
  9.6 0.0 copy-start.1
  9.6 0.4 collective-permute-done.refs_1_
  10.1 3.2 %collective-permute-done.1.refs_2_ = bf16[336,128]{1,0:T(8,128)(2,1)S(1)} collective-permute-done((bf16[336,128]{1,0:T(8,128)(2,1)S(1)}, bf16[336,128]{1,0:T(8,128)(2,1)S(1)}, u32[]{:S(2)}, u32[]{:S(2)}) %collective-permute-start.1) | collective-permute-done | bytes 86048 | tf_op jit(solution)/shard_map/ppermute | solution.py:399
  13.2 0.2 collective-permute-done.2.refs_3_
  13.5 0.2 route.1
  13.7 24.5 %all_to_all.10.arrived = bf16[32,88,128]{2,1,0:T(8,128)(2,1)S(1)} all-to-all(bf16[32,88,128]{2,1,0:T(8,128)(2,1)S(1)} %route.1), channel_id=1, replica_groups=mesh['dp'=4,'mp'=8] {'dp','mp'}, dimensions={0} | all-to-all | bytes 1441792 | tf_op jit(solution)/shard_map/all_to_all | solution.py:431
  38.2 0.0 copy-done.2
  38.2 0.0 copy-done
  38.2 0.0 copy-done.1
  38.2 0.2 owner_step.1
  38.4 7.1 %all-to-all-start.1 = ((bf16[8,88,128]{2,1,0:T(8,128)(2,1)}), bf16[8,88,128]{2,1,0:T(8,128)(2,1)S(1)}, u32[]{:S(2)}, u32[]{:S(2)}) async-start(bf16[8,88,128]{2,1,0:T(8,128)(2,1)} %get-tuple-element.40), calls=%async_computation.1 | async-start | bytes 360448 | tf_op jit(solution)/shard_map/all_to_all | solution.py:445
  45.5 3.1 %factors.1 = (f32[576,576]{1,0:T(8,128)}, bf16[576,576]{1,0:T(8,128)(2,1)}, f32[144,576]{1,0:T(8,128)}, f32[144,576]{1,0:T(8,128)}) custom-call(s32[15]{0:T(128)S(4)} %table.1, bf16[576,576]{1,0:T(8,128)(2,1)S(1)} %get-tuple-element.41.gradient, f32[576,576]{1,0:T(8,128)S(1)} %get-tuple-element.42.second, bf16[576,576]{1,0:T(8,128)(2,1)} %bitcast.27, ...), custom_call_target="tpu_custom_call" | custom-call | flops 382205952 | bytes 5971968 | tf_op jit(solution)/shard_map/factors/pallas_call | solution.py:343
  48.6 0.7 %all-to-all-done.1.returned = bf16[8,88,128]{2,1,0:T(8,128)(2,1)S(1)} async-done(((bf16[8,88,128]{2,1,0:T(8,128)(2,1)}), bf16[8,88,128]{2,1,0:T(8,128)(2,1)S(1)}, u32[]{:S(2)}, u32[]{:S(2)}) %all-to-all-start.1) | async-done | bytes 180256 | tf_op jit(solution)/shard_map/all_to_all | solution.py:445
  49.3 0.8 %place.1 = bf16[4,72,144]{2,1,0:T(8,128)(2,1)} custom-call(s32[15]{0:T(128)S(4)} %table.1, bf16[8,88,128]{2,1,0:T(8,128)(2,1)S(1)} %all-to-all-done.1.returned), custom_call_target="tpu_custom_call" | custom-call | bytes 263168 | tf_op jit(solution)/shard_map/place/pallas_call | solution.py:343
  (1 shorter events, 0.0 us)
Async XLA Ops:
  1.8 8.3 %collective-permute-start = (bf16[336,128]{1,0:T(8,128)(2,1)S(1)}, bf16[336,128]{1,0:T(8,128)(2,1)S(1)}, u32[]{:S(2)}, u32[]{:S(2)}) collective-permute-start(bf16[336,128]{1,0:T(8,128)(2,1)S(1)} %get-tuple-element.27), channel_id=1, source_target_pairs={{0,8},{8,16},{16,24},{24,0},{1,9},{9,17},{17,25},{25,1},{2,10},{10... | collective-permute-start | bytes 258056 | tf_op jit(solution)/shard_map/ppermute | solution.py:399
  4.9 8.3 %collective-permute-start.1 = (bf16[336,128]{1,0:T(8,128)(2,1)S(1)}, bf16[336,128]{1,0:T(8,128)(2,1)S(1)}, u32[]{:S(2)}, u32[]{:S(2)}) collective-permute-start(bf16[336,128]{1,0:T(8,128)(2,1)S(1)} %get-tuple-element.28), channel_id=1, source_target_pairs={{0,16},{8,24},{16,0},{24,8},{1,17},{9,25},{17,1},{25,9},{2,18},{10... | collective-permute-start | bytes 258056 | tf_op jit(solution)/shard_map/ppermute | solution.py:399
  7.5 6.0 %collective-permute-start.2 = (bf16[336,128]{1,0:T(8,128)(2,1)S(1)}, bf16[336,128]{1,0:T(8,128)(2,1)S(1)}, u32[]{:S(2)}, u32[]{:S(2)}) collective-permute-start(bf16[336,128]{1,0:T(8,128)(2,1)S(1)} %get-tuple-element.29), channel_id=1, source_target_pairs={{0,24},{8,0},{16,8},{24,16},{1,25},{9,1},{17,9},{25,17},{2,26},{10... | collective-permute-start | bytes 258056 | tf_op jit(solution)/shard_map/ppermute | solution.py:399
  9.5 28.7 %copy-start.2 = (bf16[1,576,576]{2,1,0:T(8,128)(2,1)S(1)}, bf16[1,576,576]{2,1,0:T(8,128)(2,1)}, u32[]{:S(2)}) copy-start(bf16[1,576,576]{2,1,0:T(8,128)(2,1)} %param.15) | copy-start | bytes 1990660
  9.6 28.6 %copy-start = (f32[1,576,576]{2,1,0:T(8,128)S(1)}, f32[1,576,576]{2,1,0:T(8,128)}, u32[]{:S(2)}) copy-start(f32[1,576,576]{2,1,0:T(8,128)} %param.17) | copy-start | bytes 3981316
  9.6 28.6 %copy-start.1 = (bf16[1,576,576]{2,1,0:T(8,128)(2,1)S(1)}, bf16[1,576,576]{2,1,0:T(8,128)(2,1)}, u32[]{:S(2)}) copy-start(bf16[1,576,576]{2,1,0:T(8,128)(2,1)} %param.14) | copy-start | bytes 1990660
  38.4 10.9 %all-to-all-start.1 = ((bf16[8,88,128]{2,1,0:T(8,128)(2,1)}), bf16[8,88,128]{2,1,0:T(8,128)(2,1)S(1)}, u32[]{:S(2)}, u32[]{:S(2)}) async-start(bf16[8,88,128]{2,1,0:T(8,128)(2,1)} %get-tuple-element.40), calls=%async_computation.1 | async-start | bytes 360448 | tf_op jit(solution)/shard_map/all_to_all | solution.py:445

commit v9 on v8

--- a/solution.py
+++ b/solution.py
@@ -140,7 +140,7 @@
     for group in range(groups):
         piece = summed[table[SLOTS + group]]
         for r in range(replicas):
-            out[r * groups + group] = piece
+            out[(replicas - r) * groups - 1 - group] = piece
 
 
 def prepare_kernel(
@@ -181,7 +181,7 @@
     for r in range(arrived.shape[0] // groups):
         start = tail_start(r)
         for m in range(groups):
-            piece = r * groups + m
+            piece = arrived.shape[0] - 1 - (r * groups + m)
             base = m * rows
             gradient[base : base + rows, r * LANES : (r + 1) * LANES] = arrived[piece, :rows, :]
             for g in range(3 if r == 0 else 2):
@@ -428,7 +428,14 @@
         [shape((replicas * groups,) + packed.shape[1:], bf16)],
         scratch=[packed],
     )
-    arrived = lax.all_to_all(outgoing, ("dp", "mp"), split_axis=0, concat_axis=0, tiled=True)
+    arrived = lax.all_to_all(
+        outgoing,
+        ("dp", "mp"),
+        split_axis=0,
+        concat_axis=0,
+        tiled=True,
+        axis_index_groups=[list(range(replicas * groups))[::-1]],
+    )
     chunks = shape((groups, rows + 2 * SUBLANES, LANES), bf16)
     factor_t = shape(left_t.shape, f32)
     gradient, new_second, back = run(

time: 50.3 us -> 50.6 us (level)
  Pallas kernels: 6.08 us -> 12.7 us
  waiting for transfers between devices: 4.56 us -> 0.73 us
  starting transfers between devices: 14.1 us -> 11.7 us
    pallas_call x6, Pallas kernels: 5.39 us -> 12 us  [run(): pl.pallas_call(kernel, out_shape=[pltpu.VMEM(o.shape, o.dtype) for o in o...]
    ppermute x3, waiting for transfers between devices: 3.86 us -> 0.54 us  [per_device_packed(): lax.ppermute(parts[s], 'dp', [(i, (i + s) % replicas) for i in range(repl...]
    all_to_all x1, starting transfers between devices: 7.09 us -> 4.66 us  [per_device_packed(): lax.all_to_all(back, 'mp', split_axis=0, concat_axis=0, tiled=True, axis_...]
    all_to_all x1, waiting for transfers between devices: 0.7 us -> 0.18 us  [per_device_packed(): lax.all_to_all(back, 'mp', split_axis=0, concat_axis=0, tiled=True, axis_...]
  transfers between devices with their start and end apart: 4 -> 4, of which waited for: 4 -> 3; matrix products, arithmetic and copies ran while one was open for 0% -> 0% of each run, Pallas kernels for 8% -> 14%
where the time goes in v9:
time: 50.6 us; the launch traced here: 50.4 us
  blocking collectives  24.5 us (48%)
  Pallas kernels  12.7 us (25%)
  starting transfers between devices  11.7 us (23%)
  waiting for transfers between devices  0.73 us (1%)
  between operations  0.72 us (1%)
    all_to_all x1, blocking collectives, per_device_packed(): lax.all_to_all(outgoing, ('dp', 'mp'), split_axis=0, concat_axis=0, tiled...  24.5 us
    pallas_call x6, Pallas kernels, run(): pl.pallas_call(kernel, out_shape=[pltpu.VMEM(o.shape, o.dtype) for o in o...  12 us
    ppermute x3, starting transfers between devices, per_device_packed(): lax.ppermute(parts[s], 'dp', [(i, (i + s) % replicas) for i in range(repl...  7.04 us
    all_to_all x1, starting transfers between devices, per_device_packed(): lax.all_to_all(back, 'mp', split_axis=0, concat_axis=0, tiled=True, axis_...  4.66 us
  transfers between devices with their start and end apart: 4, of which 3 were waited for; matrix products, arithmetic and copies ran while one was open for 0% of the time, Pallas kernels for 14%

profile of v9, /device:TPU:0, one launch (start us, length us, event | category | flops | bytes accessed | tf_op | source)
XLA Modules:
  0.0 50.4 jit_solution(17827698663913558960)
XLA Ops:
  0.6 1.2 %pack.1 = (bf16[336,128]{1,0:T(8,128)(2,1)S(1)}, bf16[336,128]{1,0:T(8,128)(2,1)S(1)}, bf16[336,128]{1,0:T(8,128)(2,1)S(1)}, bf16[336,128]{1,0:T(8,128)(2,1)S(1)}) custom-call(s32[1]{0:T(128)} %bitcast.share_ref.me_ref, bf16[4,72,576]{2,1,0:T(8,128)(2,1)} %bitcast.28), custom_call_target="tpu_custom_call" | custom-call | bytes 675840 | tf_op jit(solution)/shard_map/pack/pallas_call | solution.py:343
  1.8 3.1 %collective-permute-start = (bf16[336,128]{1,0:T(8,128)(2,1)S(1)}, bf16[336,128]{1,0:T(8,128)(2,1)S(1)}, u32[]{:S(2)}, u32[]{:S(2)}) collective-permute-start(bf16[336,128]{1,0:T(8,128)(2,1)S(1)} %get-tuple-element.27), channel_id=1, source_target_pairs={{0,8},{8,16},{16,24},{24,0},{1,9},{9,17},{17,25},{25,1},{2,10},{10... | collective-permute-start | bytes 258056 | tf_op jit(solution)/shard_map/ppermute | solution.py:399
  4.9 2.6 %collective-permute-start.1 = (bf16[336,128]{1,0:T(8,128)(2,1)S(1)}, bf16[336,128]{1,0:T(8,128)(2,1)S(1)}, u32[]{:S(2)}, u32[]{:S(2)}) collective-permute-start(bf16[336,128]{1,0:T(8,128)(2,1)S(1)} %get-tuple-element.28), channel_id=1, source_target_pairs={{0,16},{8,24},{16,0},{24,8},{1,17},{9,25},{17,1},{25,9},{2,18},{10... | collective-permute-start | bytes 258056 | tf_op jit(solution)/shard_map/ppermute | solution.py:399
  7.5 1.3 %collective-permute-start.2 = (bf16[336,128]{1,0:T(8,128)(2,1)S(1)}, bf16[336,128]{1,0:T(8,128)(2,1)S(1)}, u32[]{:S(2)}, u32[]{:S(2)}) collective-permute-start(bf16[336,128]{1,0:T(8,128)(2,1)S(1)} %get-tuple-element.29), channel_id=1, source_target_pairs={{0,24},{8,0},{16,8},{24,16},{1,25},{9,1},{17,9},{25,17},{2,26},{10... | collective-permute-start | bytes 258056 | tf_op jit(solution)/shard_map/ppermute | solution.py:399
  8.8 0.7 %table.1 = s32[15]{0:T(128)S(4)} custom-call(s32[1]{0:T(128)} %bitcast.share_ref.me_ref, s32[1]{0:T(128)} %bitcast.1.group_ref, s32[4]{0:T(128)} %owner_ref.1, s32[4]{0:T(128)} %offset_ref.1), custom_call_target="tpu_custom_call" | custom-call | tf_op jit(solution)/shard_map/table/pallas_call | solution.py:402
  9.5 0.0 copy-start.2
  9.6 3.4 %prepare.1 = (bf16[576,576]{1,0:T(8,128)(2,1)S(1)}, f32[576,576]{1,0:T(8,128)S(1)}, bf16[576,256]{1,0:T(8,128)(2,1)S(1)}) custom-call(s32[15]{0:T(128)S(4)} %table.1, bf16[576,576]{1,0:T(8,128)(2,1)} %bitcast.22, bf16[576,576]{1,0:T(8,128)(2,1)} %bitcast.24, bf16[576,576]{1,0:T(8,128)(2,1)} %bitcast.26), custom_call_target="tpu_custom_call" | custom-call | flops 764411904 | bytes 4276224 | tf_op jit(solution)/shard_map/prepare/pallas_call | solution.py:343
  12.9 0.0 copy-start
  12.9 0.0 copy-start.1
  12.9 0.0 collective-permute-done.refs_1_
  12.9 0.3 collective-permute-done.1.refs_2_
  13.2 0.2 collective-permute-done.2.refs_3_
  13.5 0.2 route.1
  13.7 24.5 %all_to_all.10.arrived = bf16[32,88,128]{2,1,0:T(8,128)(2,1)S(1)} all-to-all(bf16[32,88,128]{2,1,0:T(8,128)(2,1)S(1)} %route.1), channel_id=1, replica_groups={{31,30,29,28,27,26,25,24,23,22,21,20,19,18,17,16,15,14,13,12,11,10,9,8,..., dimensions={0} | all-to-all | bytes 1441792 | tf_op jit(solution)/shard_map/all_to_all | solution.py:431
  38.2 0.0 copy-done.2
  38.2 0.0 copy-done
  38.2 0.0 copy-done.1
  38.2 3.3 %owner_step.1 = (bf16[576,576]{1,0:T(8,128)(2,1)S(1)}, f32[576,576]{1,0:T(8,128)S(1)}, bf16[8,88,128]{2,1,0:T(8,128)(2,1)}) custom-call(s32[15]{0:T(128)S(4)} %table.1, bf16[32,88,128]{2,1,0:T(8,128)(2,1)S(1)} %all_to_all.10.arrived, bf16[576,576]{1,0:T(8,128)(2,1)S(1)} %bitcast.23, bf16[576,576]{1,0:T(8,128)(2,1)S(1)} %bitcast.25, ...), custom_call_target="tpu_custom_call" | custom-call | flops 1146617856 | bytes 7831552 | tf_op jit(solution)/shard_map/owner_step/pallas_call | solution.py:343
  41.6 4.7 %all-to-all-start.1 = ((bf16[8,88,128]{2,1,0:T(8,128)(2,1)}), bf16[8,88,128]{2,1,0:T(8,128)(2,1)S(1)}, u32[]{:S(2)}, u32[]{:S(2)}) async-start(bf16[8,88,128]{2,1,0:T(8,128)(2,1)} %get-tuple-element.40), calls=%async_computation.1 | async-start | bytes 360448 | tf_op jit(solution)/shard_map/all_to_all | solution.py:452
  46.2 3.2 %factors.1 = (f32[576,576]{1,0:T(8,128)}, bf16[576,576]{1,0:T(8,128)(2,1)}, f32[144,576]{1,0:T(8,128)}, f32[144,576]{1,0:T(8,128)}) custom-call(s32[15]{0:T(128)S(4)} %table.1, bf16[576,576]{1,0:T(8,128)(2,1)S(1)} %get-tuple-element.41.gradient, f32[576,576]{1,0:T(8,128)S(1)} %get-tuple-element.42.second, bf16[576,576]{1,0:T(8,128)(2,1)} %bitcast.27, ...), custom_call_target="tpu_custom_call" | custom-call | flops 382205952 | bytes 5971968 | tf_op jit(solution)/shard_map/factors/pallas_call | solution.py:343
  49.4 0.2 all-to-all-done.1.returned
  49.6 0.8 %place.1 = bf16[4,72,144]{2,1,0:T(8,128)(2,1)} custom-call(s32[15]{0:T(128)S(4)} %table.1, bf16[8,88,128]{2,1,0:T(8,128)(2,1)S(1)} %all-to-all-done.1.returned), custom_call_target="tpu_custom_call" | custom-call | bytes 263168 | tf_op jit(solution)/shard_map/place/pallas_call | solution.py:343
Async XLA Ops:
  1.8 11.1 %collective-permute-start = (bf16[336,128]{1,0:T(8,128)(2,1)S(1)}, bf16[336,128]{1,0:T(8,128)(2,1)S(1)}, u32[]{:S(2)}, u32[]{:S(2)}) collective-permute-start(bf16[336,128]{1,0:T(8,128)(2,1)S(1)} %get-tuple-element.27), channel_id=1, source_target_pairs={{0,8},{8,16},{16,24},{24,0},{1,9},{9,17},{17,25},{25,1},{2,10},{10... | collective-permute-start | bytes 258056 | tf_op jit(solution)/shard_map/ppermute | solution.py:399
  4.9 8.3 %collective-permute-start.1 = (bf16[336,128]{1,0:T(8,128)(2,1)S(1)}, bf16[336,128]{1,0:T(8,128)(2,1)S(1)}, u32[]{:S(2)}, u32[]{:S(2)}) collective-permute-start(bf16[336,128]{1,0:T(8,128)(2,1)S(1)} %get-tuple-element.28), channel_id=1, source_target_pairs={{0,16},{8,24},{16,0},{24,8},{1,17},{9,25},{17,1},{25,9},{2,18},{10... | collective-permute-start | bytes 258056 | tf_op jit(solution)/shard_map/ppermute | solution.py:399
  7.5 6.0 %collective-permute-start.2 = (bf16[336,128]{1,0:T(8,128)(2,1)S(1)}, bf16[336,128]{1,0:T(8,128)(2,1)S(1)}, u32[]{:S(2)}, u32[]{:S(2)}) collective-permute-start(bf16[336,128]{1,0:T(8,128)(2,1)S(1)} %get-tuple-element.29), channel_id=1, source_target_pairs={{0,24},{8,0},{16,8},{24,16},{1,25},{9,1},{17,9},{25,17},{2,26},{10... | collective-permute-start | bytes 258056 | tf_op jit(solution)/shard_map/ppermute | solution.py:399
  9.5 28.7 %copy-start.2 = (bf16[1,576,576]{2,1,0:T(8,128)(2,1)S(1)}, bf16[1,576,576]{2,1,0:T(8,128)(2,1)}, u32[]{:S(2)}) copy-start(bf16[1,576,576]{2,1,0:T(8,128)(2,1)} %param.15) | copy-start | bytes 1990660
  12.9 25.3 %copy-start = (f32[1,576,576]{2,1,0:T(8,128)S(1)}, f32[1,576,576]{2,1,0:T(8,128)}, u32[]{:S(2)}) copy-start(f32[1,576,576]{2,1,0:T(8,128)} %param.17) | copy-start | bytes 3981316
  12.9 25.3 %copy-start.1 = (bf16[1,576,576]{2,1,0:T(8,128)(2,1)S(1)}, bf16[1,576,576]{2,1,0:T(8,128)(2,1)}, u32[]{:S(2)}) copy-start(bf16[1,576,576]{2,1,0:T(8,128)(2,1)} %param.14) | copy-start | bytes 1990660
  41.6 8.1 %all-to-all-start.1 = ((bf16[8,88,128]{2,1,0:T(8,128)(2,1)}), bf16[8,88,128]{2,1,0:T(8,128)(2,1)S(1)}, u32[]{:S(2)}, u32[]{:S(2)}) async-start(bf16[8,88,128]{2,1,0:T(8,128)(2,1)} %get-tuple-element.40), calls=%async_computation.1 | async-start | bytes 360448 | tf_op jit(solution)/shard_map/all_to_all | solution.py:452

commit v10 on v8

--- a/solution.py
+++ b/solution.py
@@ -1,3 +1,5 @@
+from functools import partial
+
 import jax
 import jax.numpy as jnp
 from jax import lax
@@ -58,39 +60,37 @@
     return blocks * rows + -(-3 * blocks // 2) * SUBLANES
 
 
-def pack_kernel(me_ref, grad_hbm, *refs):
+def pack_kernel(me_ref, grad_hbm, *refs, steps):
     outs, last, sems = refs[:-2], refs[-2], refs[-1]
-    replicas = len(outs)
     blocks, rows, columns = grad_hbm.shape
     half = LANES // 2
-    shares = [lax.rem(me_ref[0] + step, replicas) for step in range(replicas)]
+    replicas = columns // LANES
+    shares = [lax.rem(me_ref[0] + step, replicas) for step in steps]
     copies = [
         pltpu.make_async_copy(
-            grad_hbm.at[:, :, columns - half :], last, sems.at[replicas * blocks]
+            grad_hbm.at[:, :, columns - half :], last, sems.at[len(outs) * blocks]
         )
     ]
-    for step in range(replicas):
-        col = pl.multiple_of(shares[step] * LANES, LANES)
+    for n, out in enumerate(outs):
+        col = pl.multiple_of(shares[n] * LANES, LANES)
         for b in range(blocks):
             copies.append(
                 pltpu.make_async_copy(
                     grad_hbm.at[b, :, pl.ds(col, LANES)],
-                    outs[step].at[b * rows : (b + 1) * rows, :],
-                    sems.at[step * blocks + b],
+                    out.at[b * rows : (b + 1) * rows, :],
+                    sems.at[n * blocks + b],
                 )
             )
     for copy in copies:
         copy.start()
     copies[0].wait()
-    for step in range(replicas):
-        start = tail_start(shares[step])
+    for n, out in enumerate(outs):
+        start = tail_start(shares[n])
         for b, g, row, lane in tail_places(blocks, rows):
             source = pl.multiple_of(
                 jnp.minimum(start + g, rows // SUBLANES - 1) * SUBLANES, SUBLANES
             )
-            outs[step][row : row + SUBLANES, lane : lane + half] = last[
-                b, pl.ds(source, SUBLANES), :
-            ]
+            out[row : row + SUBLANES, lane : lane + half] = last[b, pl.ds(source, SUBLANES), :]
     for copy in copies[1:]:
         copy.wait()
 
@@ -385,20 +385,28 @@
     left_t, right_t = left_factor[0].T, right_factor[0].T
     product = 2 * columns**3
 
-    parts = run(
-        "pack",
-        pack_kernel,
-        [share],
-        [pieces],
-        [sent] * replicas,
-        scratch=[shape((blocks, rows, LANES // 2), bf16)],
-        sems=replicas * blocks + 1,
-        far=1,
-    )
-    parts = [parts[0]] + [
-        lax.ppermute(parts[s], "dp", [(i, (i + s) % replicas) for i in range(replicas)])
-        for s in range(1, replicas)
-    ]
+    middle = replicas // 2
+    others = [step for step in range(1, replicas) if step != middle]
+
+    def pack(name, steps):
+        return run(
+            name,
+            partial(pack_kernel, steps=steps),
+            [share],
+            [pieces],
+            [sent] * len(steps),
+            scratch=[shape((blocks, rows, LANES // 2), bf16)],
+            sems=len(steps) * blocks + 1,
+            far=1,
+        )
+
+    def send(chunk, step):
+        return lax.ppermute(chunk, "dp", [(i, (i + step) % replicas) for i in range(replicas)])
+
+    first_sent = pack("pack_first", [middle])
+    own, *rest = pack("pack_rest", [0] + others)
+    parts = [own, send(first_sent[0], middle)]
+    parts += [send(chunk, step) for chunk, step in zip(rest, others)]
     table = pl.pallas_call(
         table_kernel,
         out_shape=pltpu.SMEM((SLOTS + groups + blocks,), jnp.int32),

time: 50.3 us -> 51 us (1.014)
  starting transfers between devices: 14.1 us -> 16.1 us
  waiting for transfers between devices: 4.56 us -> 2.84 us
  Pallas kernels: 6.08 us -> 7.04 us
    ppermute x3, waiting for transfers between devices: 3.86 us -> 2.52 us  [send(): lax.ppermute(chunk, 'dp', [(i, (i + step) % replicas) for i in range(repl...]
    ppermute x3, starting transfers between devices: 7.04 us -> 8.01 us  [send(): lax.ppermute(chunk, 'dp', [(i, (i + step) % replicas) for i in range(repl...]
    pallas_call x6 -> x7, Pallas kernels: 5.39 us -> 6.35 us  [run(): pl.pallas_call(kernel, out_shape=[pltpu.VMEM(o.shape, o.dtype) for o in o...]
    all_to_all x1, starting transfers between devices: 7.09 us -> 8.05 us  [per_device_packed(): lax.all_to_all(back, 'mp', split_axis=0, concat_axis=0, tiled=True, axis_...]
  transfers between devices with their start and end apart: 4 -> 4, of which waited for: 4 -> 3; matrix products, arithmetic and copies ran while one was open for 0% -> 0% of each run, Pallas kernels for 8% -> 10%
where the time goes in v10:
time: 51 us; the launch traced here: 50.9 us
  blocking collectives  24.2 us (47%)
  starting transfers between devices  16.1 us (32%)
  Pallas kernels  7.04 us (14%)
  waiting for transfers between devices  2.84 us (6%)
  between operations  0.73 us (1%)
    all_to_all x1, blocking collectives, per_device_packed(): lax.all_to_all(outgoing, ('dp', 'mp'), split_axis=0, concat_axis=0, tiled...  24.2 us
    all_to_all x1, starting transfers between devices, per_device_packed(): lax.all_to_all(back, 'mp', split_axis=0, concat_axis=0, tiled=True, axis_...  8.05 us
    ppermute x3, starting transfers between devices, send(): lax.ppermute(chunk, 'dp', [(i, (i + step) % replicas) for i in range(repl...  8.01 us
    pallas_call x7, Pallas kernels, run(): pl.pallas_call(kernel, out_shape=[pltpu.VMEM(o.shape, o.dtype) for o in o...  6.35 us
    ppermute x3, waiting for transfers between devices, send(): lax.ppermute(chunk, 'dp', [(i, (i + step) % replicas) for i in range(repl...  2.52 us
  transfers between devices with their start and end apart: 4, of which 3 were waited for; matrix products, arithmetic and copies ran while one was open for 0% of the time, Pallas kernels for 10%

profile of v10, /device:TPU:0, one launch (start us, length us, event | category | flops | bytes accessed | tf_op | source)
XLA Modules:
  0.0 50.9 jit_solution(11365545007413095439)
XLA Ops:
  0.6 1.0 %pack_first.1 = bf16[336,128]{1,0:T(8,128)(2,1)S(1)} custom-call(s32[1]{0:T(128)} %bitcast.share_ref.me_ref, bf16[4,72,576]{2,1,0:T(8,128)(2,1)} %bitcast.26), custom_call_target="tpu_custom_call" | custom-call | bytes 417792 | tf_op jit(solution)/shard_map/pack_first/pallas_call | solution.py:343
  1.7 4.1 %collective-permute-start = (bf16[336,128]{1,0:T(8,128)(2,1)S(1)}, bf16[336,128]{1,0:T(8,128)(2,1)S(1)}, u32[]{:S(2)}, u32[]{:S(2)}) collective-permute-start(bf16[336,128]{1,0:T(8,128)(2,1)S(1)} %pack_first.1), channel_id=1, source_target_pairs={{0,16},{8,24},{16,0},{24,8},{1,17},{9,25},{17,1},{25,9},{2,18},{10... | collective-permute-start | bytes 258056 | tf_op jit(solution)/shard_map/ppermute | solution.py:404
  5.8 1.1 %pack_rest.1 = (bf16[336,128]{1,0:T(8,128)(2,1)S(1)}, bf16[336,128]{1,0:T(8,128)(2,1)S(1)}, bf16[336,128]{1,0:T(8,128)(2,1)S(1)}) custom-call(s32[1]{0:T(128)} %bitcast.share_ref.me_ref, bf16[4,72,576]{2,1,0:T(8,128)(2,1)} %bitcast.27), custom_call_target="tpu_custom_call" | custom-call | bytes 589824 | tf_op jit(solution)/shard_map/pack_rest/pallas_call | solution.py:343
  6.9 1.6 %collective-permute-start.1 = (bf16[336,128]{1,0:T(8,128)(2,1)S(1)}, bf16[336,128]{1,0:T(8,128)(2,1)S(1)}, u32[]{:S(2)}, u32[]{:S(2)}) collective-permute-start(bf16[336,128]{1,0:T(8,128)(2,1)S(1)} %get-tuple-element.26), channel_id=1, source_target_pairs={{0,8},{8,16},{16,24},{24,0},{1,9},{9,17},{17,25},{25,1},{2,10},{10... | collective-permute-start | bytes 258056 | tf_op jit(solution)/shard_map/ppermute | solution.py:404
  8.5 2.2 %collective-permute-start.2 = (bf16[336,128]{1,0:T(8,128)(2,1)S(1)}, bf16[336,128]{1,0:T(8,128)(2,1)S(1)}, u32[]{:S(2)}, u32[]{:S(2)}) collective-permute-start(bf16[336,128]{1,0:T(8,128)(2,1)S(1)} %get-tuple-element.27), channel_id=1, source_target_pairs={{0,24},{8,0},{16,8},{24,16},{1,25},{9,1},{17,9},{25,17},{2,26},{10... | collective-permute-start | bytes 258056 | tf_op jit(solution)/shard_map/ppermute | solution.py:404
  10.8 0.7 %table.1 = s32[15]{0:T(128)S(4)} custom-call(s32[1]{0:T(128)} %bitcast.share_ref.me_ref, s32[1]{0:T(128)} %bitcast.1.group_ref, s32[4]{0:T(128)} %owner_ref.1, s32[4]{0:T(128)} %offset_ref.1), custom_call_target="tpu_custom_call" | custom-call | tf_op jit(solution)/shard_map/table/pallas_call | solution.py:410
  11.5 0.0 copy-start.2
  11.5 0.0 copy-start
  11.5 0.0 copy-start.1
  11.6 0.0 collective-permute-done.refs_1_
  11.6 2.1 %collective-permute-done.1.refs_2_ = bf16[336,128]{1,0:T(8,128)(2,1)S(1)} collective-permute-done((bf16[336,128]{1,0:T(8,128)(2,1)S(1)}, bf16[336,128]{1,0:T(8,128)(2,1)S(1)}, u32[]{:S(2)}, u32[]{:S(2)}) %collective-permute-start.1) | collective-permute-done | bytes 86048 | tf_op jit(solution)/shard_map/ppermute | solution.py:404
  13.7 0.4 collective-permute-done.2.refs_3_
  14.1 0.2 route.1
  14.3 24.2 %all_to_all.10.arrived = bf16[32,88,128]{2,1,0:T(8,128)(2,1)S(1)} all-to-all(bf16[32,88,128]{2,1,0:T(8,128)(2,1)S(1)} %route.1), channel_id=1, replica_groups=mesh['dp'=4,'mp'=8] {'dp','mp'}, dimensions={0} | all-to-all | bytes 1441792 | tf_op jit(solution)/shard_map/all_to_all | solution.py:439
  38.5 0.0 copy-done.2
  38.5 0.0 copy-done
  38.5 0.0 copy-done.1
  38.5 0.2 owner_step.1
  38.7 8.0 %all-to-all-start.1 = ((bf16[8,88,128]{2,1,0:T(8,128)(2,1)}), bf16[8,88,128]{2,1,0:T(8,128)(2,1)S(1)}, u32[]{:S(2)}, u32[]{:S(2)}) async-start(bf16[8,88,128]{2,1,0:T(8,128)(2,1)} %get-tuple-element.38), calls=%async_computation.1 | async-start | bytes 360448 | tf_op jit(solution)/shard_map/all_to_all | solution.py:453
  46.7 3.1 %factors.1 = (f32[576,576]{1,0:T(8,128)}, bf16[576,576]{1,0:T(8,128)(2,1)}, f32[144,576]{1,0:T(8,128)}, f32[144,576]{1,0:T(8,128)}) custom-call(s32[15]{0:T(128)S(4)} %table.1, bf16[576,576]{1,0:T(8,128)(2,1)S(1)} %get-tuple-element.39.gradient, f32[576,576]{1,0:T(8,128)S(1)} %get-tuple-element.40.second, bf16[576,576]{1,0:T(8,128)(2,1)} %bitcast.29, ...), custom_call_target="tpu_custom_call" | custom-call | flops 382205952 | bytes 5971968 | tf_op jit(solution)/shard_map/factors/pallas_call | solution.py:343
  49.8 0.3 all-to-all-done.1.returned
  50.1 0.8 %place.1 = bf16[4,72,144]{2,1,0:T(8,128)(2,1)} custom-call(s32[15]{0:T(128)S(4)} %table.1, bf16[8,88,128]{2,1,0:T(8,128)(2,1)S(1)} %all-to-all-done.1.returned), custom_call_target="tpu_custom_call" | custom-call | bytes 263168 | tf_op jit(solution)/shard_map/place/pallas_call | solution.py:343
  (1 shorter events, 0.0 us)
Async XLA Ops:
  1.7 9.9 %collective-permute-start = (bf16[336,128]{1,0:T(8,128)(2,1)S(1)}, bf16[336,128]{1,0:T(8,128)(2,1)S(1)}, u32[]{:S(2)}, u32[]{:S(2)}) collective-permute-start(bf16[336,128]{1,0:T(8,128)(2,1)S(1)} %pack_first.1), channel_id=1, source_target_pairs={{0,16},{8,24},{16,0},{24,8},{1,17},{9,25},{17,1},{25,9},{2,18},{10... | collective-permute-start | bytes 258056 | tf_op jit(solution)/shard_map/ppermute | solution.py:404
  6.9 6.8 %collective-permute-start.1 = (bf16[336,128]{1,0:T(8,128)(2,1)S(1)}, bf16[336,128]{1,0:T(8,128)(2,1)S(1)}, u32[]{:S(2)}, u32[]{:S(2)}) collective-permute-start(bf16[336,128]{1,0:T(8,128)(2,1)S(1)} %get-tuple-element.26), channel_id=1, source_target_pairs={{0,8},{8,16},{16,24},{24,0},{1,9},{9,17},{17,25},{25,1},{2,10},{10... | collective-permute-start | bytes 258056 | tf_op jit(solution)/shard_map/ppermute | solution.py:404
  8.5 5.6 %collective-permute-start.2 = (bf16[336,128]{1,0:T(8,128)(2,1)S(1)}, bf16[336,128]{1,0:T(8,128)(2,1)S(1)}, u32[]{:S(2)}, u32[]{:S(2)}) collective-permute-start(bf16[336,128]{1,0:T(8,128)(2,1)S(1)} %get-tuple-element.27), channel_id=1, source_target_pairs={{0,24},{8,0},{16,8},{24,16},{1,25},{9,1},{17,9},{25,17},{2,26},{10... | collective-permute-start | bytes 258056 | tf_op jit(solution)/shard_map/ppermute | solution.py:404
  11.5 27.0 %copy-start.2 = (bf16[1,576,576]{2,1,0:T(8,128)(2,1)S(1)}, bf16[1,576,576]{2,1,0:T(8,128)(2,1)}, u32[]{:S(2)}) copy-start(bf16[1,576,576]{2,1,0:T(8,128)(2,1)} %param.15) | copy-start | bytes 1990660
  11.5 27.0 %copy-start = (f32[1,576,576]{2,1,0:T(8,128)S(1)}, f32[1,576,576]{2,1,0:T(8,128)}, u32[]{:S(2)}) copy-start(f32[1,576,576]{2,1,0:T(8,128)} %param.17) | copy-start | bytes 3981316
  11.5 26.9 %copy-start.1 = (bf16[1,576,576]{2,1,0:T(8,128)(2,1)S(1)}, bf16[1,576,576]{2,1,0:T(8,128)(2,1)}, u32[]{:S(2)}) copy-start(bf16[1,576,576]{2,1,0:T(8,128)(2,1)} %param.14) | copy-start | bytes 1990660
  38.7 11.4 %all-to-all-start.1 = ((bf16[8,88,128]{2,1,0:T(8,128)(2,1)}), bf16[8,88,128]{2,1,0:T(8,128)(2,1)S(1)}, u32[]{:S(2)}, u32[]{:S(2)}) async-start(bf16[8,88,128]{2,1,0:T(8,128)(2,1)} %get-tuple-element.38), calls=%async_computation.1 | async-start | bytes 360448 | tf_op jit(solution)/shard_map/all_to_all | solution.py:453

commit v11 on v8

--- a/solution.py
+++ b/solution.py
@@ -218,25 +218,29 @@
             spread = fresh * lax.rsqrt(fresh) + 1e-08
             scaled[:, cols] = (rotated_mom * lax.rsqrt(spread * spread)).astype(jnp.bfloat16)
         total = matmul(scaled[...], back_basis[...])
-        result = matmul(lbasis[...], total.astype(jnp.bfloat16))
+        sums = total.astype(jnp.bfloat16)
         lane = lax.broadcasted_iota(jnp.int32, (SUBLANES, LANES), 1)
         tail_groups = rows // SUBLANES - 1
         width = LANES // tail_groups
-        for m in range(groups):
-            base = m * rows
-            back[groups - 1 - m, :rows, :] = result[base : base + rows, :LANES].astype(jnp.bfloat16)
-            mixed = result[base : base + SUBLANES, LANES:]
-            for g in range(1, tail_groups):
-                row = base + g * SUBLANES
-                mixed = jnp.where(
-                    lane < g * width, mixed, result[row : row + SUBLANES, LANES:]
-                )
-            back[groups - 1 - m, rows : rows + SUBLANES, :] = mixed.astype(jnp.bfloat16)
-            back[groups - 1 - m, rows + SUBLANES :, :] = result[
-                base + rows - SUBLANES : base + rows, LANES:
-            ].astype(jnp.bfloat16)
-        for copy in copies:
-            copy.start()
+        half_groups = groups // 2
+        for side in range(2):
+            first = side * half_groups
+            result = matmul(lbasis[first * rows : (first + half_groups) * rows, :], sums)
+            for m in range(first, first + half_groups):
+                off = (m - first) * rows
+                back[groups - 1 - m, :rows, :] = result[off : off + rows, :LANES].astype(jnp.bfloat16)
+                mixed = result[off : off + SUBLANES, LANES:]
+                for g in range(1, tail_groups):
+                    row = off + g * SUBLANES
+                    mixed = jnp.where(
+                        lane < g * width, mixed, result[row : row + SUBLANES, LANES:]
+                    )
+                back[groups - 1 - m, rows : rows + SUBLANES, :] = mixed.astype(jnp.bfloat16)
+                back[groups - 1 - m, rows + SUBLANES :, :] = result[
+                    off + rows - SUBLANES : off + rows, LANES:
+                ].astype(jnp.bfloat16)
+            for m in range(first, first + half_groups):
+                copies[groups - 1 - m].start()
         for copy in copies:
             copy.wait()
 

time: 50.3 us -> 50.5 us (level); the launches traced: 50 us -> 49.7 us
  Pallas kernels: 6.08 us -> 12.7 us
  waiting for transfers between devices: 4.56 us -> 0.82 us
  starting transfers between devices: 14.1 us -> 11 us
    pallas_call x6, Pallas kernels: 5.39 us -> 12 us  [run(): pl.pallas_call(kernel, out_shape=[pltpu.VMEM(o.shape, o.dtype) for o in o...]
    ppermute x3, waiting for transfers between devices: 3.86 us -> 0.54 us  [per_device_packed(): lax.ppermute(parts[s], 'dp', [(i, (i + s) % replicas) for i in range(repl...]
    all_to_all x1, starting transfers between devices: 7.09 us -> 3.93 us  [per_device_packed(): lax.all_to_all(back, 'mp', split_axis=0, concat_axis=0, tiled=True, axis_...]
  transfers between devices with their start and end apart: 4 -> 4, of which waited for: 4 -> 3; matrix products, arithmetic and copies ran while one was open for 0% -> 0% of each run, Pallas kernels for 8% -> 15%
where the time goes in v11:
time: 50.5 us; the launch traced here: 49.7 us
  blocking collectives  24.5 us (49%)
  Pallas kernels  12.7 us (25%)
  starting transfers between devices  11 us (22%)
  waiting for transfers between devices  0.82 us (2%)
  between operations  0.72 us (1%)
    all_to_all x1, blocking collectives, per_device_packed(): lax.all_to_all(outgoing, ('dp', 'mp'), split_axis=0, concat_axis=0, tiled...  24.5 us
    pallas_call x6, Pallas kernels, run(): pl.pallas_call(kernel, out_shape=[pltpu.VMEM(o.shape, o.dtype) for o in o...  12 us
    ppermute x3, starting transfers between devices, per_device_packed(): lax.ppermute(parts[s], 'dp', [(i, (i + s) % replicas) for i in range(repl...  7.04 us
    all_to_all x1, starting transfers between devices, per_device_packed(): lax.all_to_all(back, 'mp', split_axis=0, concat_axis=0, tiled=True, axis_...  3.93 us
  transfers between devices with their start and end apart: 4, of which 3 were waited for; matrix products, arithmetic and copies ran while one was open for 0% of the time, Pallas kernels for 15%

profile of v11, /device:TPU:0, one launch (start us, length us, event | category | flops | bytes accessed | tf_op | source)
XLA Modules:
  0.0 49.7 jit_solution(9111025490842592720)
XLA Ops:
  0.6 1.2 %pack.1 = (bf16[336,128]{1,0:T(8,128)(2,1)S(1)}, bf16[336,128]{1,0:T(8,128)(2,1)S(1)}, bf16[336,128]{1,0:T(8,128)(2,1)S(1)}, bf16[336,128]{1,0:T(8,128)(2,1)S(1)}) custom-call(s32[1]{0:T(128)} %bitcast.share_ref.me_ref, bf16[4,72,576]{2,1,0:T(8,128)(2,1)} %bitcast.28), custom_call_target="tpu_custom_call" | custom-call | bytes 675840 | tf_op jit(solution)/shard_map/pack/pallas_call | solution.py:347
  1.8 3.1 %collective-permute-start = (bf16[336,128]{1,0:T(8,128)(2,1)S(1)}, bf16[336,128]{1,0:T(8,128)(2,1)S(1)}, u32[]{:S(2)}, u32[]{:S(2)}) collective-permute-start(bf16[336,128]{1,0:T(8,128)(2,1)S(1)} %get-tuple-element.27), channel_id=1, source_target_pairs={{0,8},{8,16},{16,24},{24,0},{1,9},{9,17},{17,25},{25,1},{2,10},{10... | collective-permute-start | bytes 258056 | tf_op jit(solution)/shard_map/ppermute | solution.py:403
  4.9 2.6 %collective-permute-start.1 = (bf16[336,128]{1,0:T(8,128)(2,1)S(1)}, bf16[336,128]{1,0:T(8,128)(2,1)S(1)}, u32[]{:S(2)}, u32[]{:S(2)}) collective-permute-start(bf16[336,128]{1,0:T(8,128)(2,1)S(1)} %get-tuple-element.28), channel_id=1, source_target_pairs={{0,16},{8,24},{16,0},{24,8},{1,17},{9,25},{17,1},{25,9},{2,18},{10... | collective-permute-start | bytes 258056 | tf_op jit(solution)/shard_map/ppermute | solution.py:403
  7.5 1.3 %collective-permute-start.2 = (bf16[336,128]{1,0:T(8,128)(2,1)S(1)}, bf16[336,128]{1,0:T(8,128)(2,1)S(1)}, u32[]{:S(2)}, u32[]{:S(2)}) collective-permute-start(bf16[336,128]{1,0:T(8,128)(2,1)S(1)} %get-tuple-element.29), channel_id=1, source_target_pairs={{0,24},{8,0},{16,8},{24,16},{1,25},{9,1},{17,9},{25,17},{2,26},{10... | collective-permute-start | bytes 258056 | tf_op jit(solution)/shard_map/ppermute | solution.py:403
  8.8 0.7 %table.1 = s32[15]{0:T(128)S(4)} custom-call(s32[1]{0:T(128)} %bitcast.share_ref.me_ref, s32[1]{0:T(128)} %bitcast.1.group_ref, s32[4]{0:T(128)} %owner_ref.1, s32[4]{0:T(128)} %offset_ref.1), custom_call_target="tpu_custom_call" | custom-call | tf_op jit(solution)/shard_map/table/pallas_call | solution.py:406
  9.5 0.0 copy-start.2
  9.6 3.4 %prepare.1 = (bf16[576,576]{1,0:T(8,128)(2,1)S(1)}, f32[576,576]{1,0:T(8,128)S(1)}, bf16[576,256]{1,0:T(8,128)(2,1)S(1)}) custom-call(s32[15]{0:T(128)S(4)} %table.1, bf16[576,576]{1,0:T(8,128)(2,1)} %bitcast.22, bf16[576,576]{1,0:T(8,128)(2,1)} %bitcast.24, bf16[576,576]{1,0:T(8,128)(2,1)} %bitcast.26), custom_call_target="tpu_custom_call" | custom-call | flops 764411904 | bytes 4276224 | tf_op jit(solution)/shard_map/prepare/pallas_call | solution.py:347
  12.9 0.0 copy-start
  12.9 0.0 copy-start.1
  12.9 0.0 collective-permute-done.refs_1_
  12.9 0.3 collective-permute-done.1.refs_2_
  13.2 0.2 collective-permute-done.2.refs_3_
  13.5 0.2 route.1
  13.7 24.5 %all_to_all.10.arrived = bf16[32,88,128]{2,1,0:T(8,128)(2,1)S(1)} all-to-all(bf16[32,88,128]{2,1,0:T(8,128)(2,1)S(1)} %route.1), channel_id=1, replica_groups=mesh['dp'=4,'mp'=8] {'dp','mp'}, dimensions={0} | all-to-all | bytes 1441792 | tf_op jit(solution)/shard_map/all_to_all | solution.py:435
  38.2 0.0 copy-done.2
  38.2 0.0 copy-done
  38.2 0.0 copy-done.1
  38.2 3.3 %owner_step.1 = (bf16[576,576]{1,0:T(8,128)(2,1)S(1)}, f32[576,576]{1,0:T(8,128)S(1)}, bf16[8,88,128]{2,1,0:T(8,128)(2,1)}) custom-call(s32[15]{0:T(128)S(4)} %table.1, bf16[32,88,128]{2,1,0:T(8,128)(2,1)S(1)} %all_to_all.10.arrived, bf16[576,576]{1,0:T(8,128)(2,1)S(1)} %bitcast.23, bf16[576,576]{1,0:T(8,128)(2,1)S(1)} %bitcast.25, ...), custom_call_target="tpu_custom_call" | custom-call | flops 1146617856 | bytes 7831552 | tf_op jit(solution)/shard_map/owner_step/pallas_call | solution.py:347
  41.5 3.9 %all-to-all-start.1 = ((bf16[8,88,128]{2,1,0:T(8,128)(2,1)}), bf16[8,88,128]{2,1,0:T(8,128)(2,1)S(1)}, u32[]{:S(2)}, u32[]{:S(2)}) async-start(bf16[8,88,128]{2,1,0:T(8,128)(2,1)} %get-tuple-element.40), calls=%async_computation.1 | async-start | bytes 360448 | tf_op jit(solution)/shard_map/all_to_all | solution.py:449
  45.5 3.2 %factors.1 = (f32[576,576]{1,0:T(8,128)}, bf16[576,576]{1,0:T(8,128)(2,1)}, f32[144,576]{1,0:T(8,128)}, f32[144,576]{1,0:T(8,128)}) custom-call(s32[15]{0:T(128)S(4)} %table.1, bf16[576,576]{1,0:T(8,128)(2,1)S(1)} %get-tuple-element.41.gradient, f32[576,576]{1,0:T(8,128)S(1)} %get-tuple-element.42.second, bf16[576,576]{1,0:T(8,128)(2,1)} %bitcast.27, ...), custom_call_target="tpu_custom_call" | custom-call | flops 382205952 | bytes 5971968 | tf_op jit(solution)/shard_map/factors/pallas_call | solution.py:347
  48.7 0.3 all-to-all-done.1.returned
  49.0 0.8 %place.1 = bf16[4,72,144]{2,1,0:T(8,128)(2,1)} custom-call(s32[15]{0:T(128)S(4)} %table.1, bf16[8,88,128]{2,1,0:T(8,128)(2,1)S(1)} %all-to-all-done.1.returned), custom_call_target="tpu_custom_call" | custom-call | bytes 263168 | tf_op jit(solution)/shard_map/place/pallas_call | solution.py:347
Async XLA Ops:
  1.8 11.1 %collective-permute-start = (bf16[336,128]{1,0:T(8,128)(2,1)S(1)}, bf16[336,128]{1,0:T(8,128)(2,1)S(1)}, u32[]{:S(2)}, u32[]{:S(2)}) collective-permute-start(bf16[336,128]{1,0:T(8,128)(2,1)S(1)} %get-tuple-element.27), channel_id=1, source_target_pairs={{0,8},{8,16},{16,24},{24,0},{1,9},{9,17},{17,25},{25,1},{2,10},{10... | collective-permute-start | bytes 258056 | tf_op jit(solution)/shard_map/ppermute | solution.py:403
  4.9 8.3 %collective-permute-start.1 = (bf16[336,128]{1,0:T(8,128)(2,1)S(1)}, bf16[336,128]{1,0:T(8,128)(2,1)S(1)}, u32[]{:S(2)}, u32[]{:S(2)}) collective-permute-start(bf16[336,128]{1,0:T(8,128)(2,1)S(1)} %get-tuple-element.28), channel_id=1, source_target_pairs={{0,16},{8,24},{16,0},{24,8},{1,17},{9,25},{17,1},{25,9},{2,18},{10... | collective-permute-start | bytes 258056 | tf_op jit(solution)/shard_map/ppermute | solution.py:403
  7.5 6.0 %collective-permute-start.2 = (bf16[336,128]{1,0:T(8,128)(2,1)S(1)}, bf16[336,128]{1,0:T(8,128)(2,1)S(1)}, u32[]{:S(2)}, u32[]{:S(2)}) collective-permute-start(bf16[336,128]{1,0:T(8,128)(2,1)S(1)} %get-tuple-element.29), channel_id=1, source_target_pairs={{0,24},{8,0},{16,8},{24,16},{1,25},{9,1},{17,9},{25,17},{2,26},{10... | collective-permute-start | bytes 258056 | tf_op jit(solution)/shard_map/ppermute | solution.py:403
  9.5 28.7 %copy-start.2 = (bf16[1,576,576]{2,1,0:T(8,128)(2,1)S(1)}, bf16[1,576,576]{2,1,0:T(8,128)(2,1)}, u32[]{:S(2)}) copy-start(bf16[1,576,576]{2,1,0:T(8,128)(2,1)} %param.15) | copy-start | bytes 1990660
  12.9 25.3 %copy-start = (f32[1,576,576]{2,1,0:T(8,128)S(1)}, f32[1,576,576]{2,1,0:T(8,128)}, u32[]{:S(2)}) copy-start(f32[1,576,576]{2,1,0:T(8,128)} %param.17) | copy-start | bytes 3981316
  12.9 25.3 %copy-start.1 = (bf16[1,576,576]{2,1,0:T(8,128)(2,1)S(1)}, bf16[1,576,576]{2,1,0:T(8,128)(2,1)}, u32[]{:S(2)}) copy-start(bf16[1,576,576]{2,1,0:T(8,128)(2,1)} %param.14) | copy-start | bytes 1990660
  41.5 7.4 %all-to-all-start.1 = ((bf16[8,88,128]{2,1,0:T(8,128)(2,1)}), bf16[8,88,128]{2,1,0:T(8,128)(2,1)S(1)}, u32[]{:S(2)}, u32[]{:S(2)}) async-start(bf16[8,88,128]{2,1,0:T(8,128)(2,1)} %get-tuple-element.40), calls=%async_computation.1 | async-start | bytes 360448 | tf_op jit(solution)/shard_map/all_to_all | solution.py:449

commit v12 on v11

--- a/solution.py
+++ b/solution.py
@@ -59,40 +59,30 @@
 
 
 def pack_kernel(me_ref, grad_hbm, *refs):
-    outs, last, sems = refs[:-2], refs[-2], refs[-1]
+    outs, grad, sems = refs[:-2], refs[-2], refs[-1]
     replicas = len(outs)
     blocks, rows, columns = grad_hbm.shape
     half = LANES // 2
-    shares = [lax.rem(me_ref[0] + step, replicas) for step in range(replicas)]
     copies = [
-        pltpu.make_async_copy(
-            grad_hbm.at[:, :, columns - half :], last, sems.at[replicas * blocks]
-        )
+        pltpu.make_async_copy(grad_hbm.at[b], grad.at[b], sems.at[b]) for b in range(blocks)
     ]
-    for step in range(replicas):
-        col = pl.multiple_of(shares[step] * LANES, LANES)
-        for b in range(blocks):
-            copies.append(
-                pltpu.make_async_copy(
-                    grad_hbm.at[b, :, pl.ds(col, LANES)],
-                    outs[step].at[b * rows : (b + 1) * rows, :],
-                    sems.at[step * blocks + b],
-                )
-            )
     for copy in copies:
         copy.start()
-    copies[0].wait()
-    for step in range(replicas):
-        start = tail_start(shares[step])
-        for b, g, row, lane in tail_places(blocks, rows):
-            source = pl.multiple_of(
-                jnp.minimum(start + g, rows // SUBLANES - 1) * SUBLANES, SUBLANES
-            )
-            outs[step][row : row + SUBLANES, lane : lane + half] = last[
-                b, pl.ds(source, SUBLANES), :
-            ]
-    for copy in copies[1:]:
-        copy.wait()
+    shares = [lax.rem(me_ref[0] + step, replicas) for step in range(replicas)]
+    places = list(tail_places(blocks, rows))
+    for b in range(blocks):
+        copies[b].wait()
+        for step in range(replicas):
+            col = pl.multiple_of(shares[step] * LANES, LANES)
+            outs[step][b * rows : (b + 1) * rows, :] = grad[b, :, pl.ds(col, LANES)]
+            start = tail_start(shares[step])
+            for _, g, row, lane in places[3 * b : 3 * b + 3]:
+                source = pl.multiple_of(
+                    jnp.minimum(start + g, rows // SUBLANES - 1) * SUBLANES, SUBLANES
+                )
+                outs[step][row : row + SUBLANES, lane : lane + half] = grad[
+                    b, pl.ds(source, SUBLANES), columns - half :
+                ]
 
 
 SHARE, GROUP, FOUND, SLOTS = 0, 1, 2, 3
@@ -395,8 +385,8 @@
         [share],
         [pieces],
         [sent] * replicas,
-        scratch=[shape((blocks, rows, LANES // 2), bf16)],
-        sems=replicas * blocks + 1,
+        scratch=[shape(pieces.shape, bf16)],
+        sems=blocks,
         far=1,
     )
     parts = [parts[0]] + [

time: 50.5 us -> 50.7 us (level); the launches traced: 49.7 us -> 50.7 us
  Pallas kernels: 12.7 us -> 6.2 us
  starting transfers between devices: 11 us -> 15.1 us
  waiting for transfers between devices: 0.82 us -> 4.19 us
    pallas_call x6, Pallas kernels: 12 us -> 5.51 us  [run(): pl.pallas_call(kernel, out_shape=[pltpu.VMEM(o.shape, o.dtype) for o in o...]
    all_to_all x1, starting transfers between devices: 3.93 us -> 8.02 us  [per_device_packed(): lax.all_to_all(back, 'mp', split_axis=0, concat_axis=0, tiled=True, axis_...]
    ppermute x3, waiting for transfers between devices: 0.54 us -> 3.86 us  [per_device_packed(): lax.ppermute(parts[s], 'dp', [(i, (i + s) % replicas) for i in range(repl...]
  transfers between devices with their start and end apart: 4 -> 4, of which waited for: 3 -> 4; matrix products, arithmetic and copies ran while one was open for 0% -> 0% of each run, Pallas kernels for 15% -> 7%
where the time goes in v12:
time: 50.7 us
  blocking collectives  24.5 us (48%)
  starting transfers between devices  15.1 us (30%)
  Pallas kernels  6.2 us (12%)
  waiting for transfers between devices  4.19 us (8%)
  between operations  0.71 us (1%)
    all_to_all x1, blocking collectives, per_device_packed(): lax.all_to_all(outgoing, ('dp', 'mp'), split_axis=0, concat_axis=0, tiled...  24.5 us
    all_to_all x1, starting transfers between devices, per_device_packed(): lax.all_to_all(back, 'mp', split_axis=0, concat_axis=0, tiled=True, axis_...  8.02 us
    ppermute x3, starting transfers between devices, per_device_packed(): lax.ppermute(parts[s], 'dp', [(i, (i + s) % replicas) for i in range(repl...  7.04 us
    pallas_call x6, Pallas kernels, run(): pl.pallas_call(kernel, out_shape=[pltpu.VMEM(o.shape, o.dtype) for o in o...  5.51 us
    ppermute x3, waiting for transfers between devices, per_device_packed(): lax.ppermute(parts[s], 'dp', [(i, (i + s) % replicas) for i in range(repl...  3.86 us
  transfers between devices with their start and end apart: 4, of which 4 were waited for; matrix products, arithmetic and copies ran while one was open for 0% of the time, Pallas kernels for 7%

profile of v12, /device:TPU:0, one launch (start us, length us, event | category | flops | bytes accessed | tf_op | source)
XLA Modules:
  0.0 50.7 jit_solution(1895400534426216095)
XLA Ops:
  0.6 1.3 %pack.1 = (bf16[336,128]{1,0:T(8,128)(2,1)S(1)}, bf16[336,128]{1,0:T(8,128)(2,1)S(1)}, bf16[336,128]{1,0:T(8,128)(2,1)S(1)}, bf16[336,128]{1,0:T(8,128)(2,1)S(1)}) custom-call(s32[1]{0:T(128)} %bitcast.share_ref.me_ref, bf16[4,72,576]{2,1,0:T(8,128)(2,1)} %bitcast.28), custom_call_target="tpu_custom_call" | custom-call | bytes 675840 | tf_op jit(solution)/shard_map/pack/pallas_call | solution.py:337
  1.9 3.1 %collective-permute-start = (bf16[336,128]{1,0:T(8,128)(2,1)S(1)}, bf16[336,128]{1,0:T(8,128)(2,1)S(1)}, u32[]{:S(2)}, u32[]{:S(2)}) collective-permute-start(bf16[336,128]{1,0:T(8,128)(2,1)S(1)} %get-tuple-element.27), channel_id=1, source_target_pairs={{0,8},{8,16},{16,24},{24,0},{1,9},{9,17},{17,25},{25,1},{2,10},{10... | collective-permute-start | bytes 258056 | tf_op jit(solution)/shard_map/ppermute | solution.py:393
  5.0 2.6 %collective-permute-start.1 = (bf16[336,128]{1,0:T(8,128)(2,1)S(1)}, bf16[336,128]{1,0:T(8,128)(2,1)S(1)}, u32[]{:S(2)}, u32[]{:S(2)}) collective-permute-start(bf16[336,128]{1,0:T(8,128)(2,1)S(1)} %get-tuple-element.28), channel_id=1, source_target_pairs={{0,16},{8,24},{16,0},{24,8},{1,17},{9,25},{17,1},{25,9},{2,18},{10... | collective-permute-start | bytes 258056 | tf_op jit(solution)/shard_map/ppermute | solution.py:393
  7.6 1.3 %collective-permute-start.2 = (bf16[336,128]{1,0:T(8,128)(2,1)S(1)}, bf16[336,128]{1,0:T(8,128)(2,1)S(1)}, u32[]{:S(2)}, u32[]{:S(2)}) collective-permute-start(bf16[336,128]{1,0:T(8,128)(2,1)S(1)} %get-tuple-element.29), channel_id=1, source_target_pairs={{0,24},{8,0},{16,8},{24,16},{1,25},{9,1},{17,9},{25,17},{2,26},{10... | collective-permute-start | bytes 258056 | tf_op jit(solution)/shard_map/ppermute | solution.py:393
  9.0 0.7 %table.1 = s32[15]{0:T(128)S(4)} custom-call(s32[1]{0:T(128)} %bitcast.share_ref.me_ref, s32[1]{0:T(128)} %bitcast.1.group_ref, s32[4]{0:T(128)} %owner_ref.1, s32[4]{0:T(128)} %offset_ref.1), custom_call_target="tpu_custom_call" | custom-call | tf_op jit(solution)/shard_map/table/pallas_call | solution.py:396
  9.7 0.0 copy-start.2
  9.7 0.0 copy-start
  9.7 0.0 copy-start.1
  9.8 0.4 collective-permute-done.refs_1_
  10.2 3.2 %collective-permute-done.1.refs_2_ = bf16[336,128]{1,0:T(8,128)(2,1)S(1)} collective-permute-done((bf16[336,128]{1,0:T(8,128)(2,1)S(1)}, bf16[336,128]{1,0:T(8,128)(2,1)S(1)}, u32[]{:S(2)}, u32[]{:S(2)}) %collective-permute-start.1) | collective-permute-done | bytes 86048 | tf_op jit(solution)/shard_map/ppermute | solution.py:393
  13.4 0.2 collective-permute-done.2.refs_3_
  13.6 0.2 route.1
  13.8 24.5 %all_to_all.10.arrived = bf16[32,88,128]{2,1,0:T(8,128)(2,1)S(1)} all-to-all(bf16[32,88,128]{2,1,0:T(8,128)(2,1)S(1)} %route.1), channel_id=1, replica_groups=mesh['dp'=4,'mp'=8] {'dp','mp'}, dimensions={0} | all-to-all | bytes 1441792 | tf_op jit(solution)/shard_map/all_to_all | solution.py:425
  38.3 0.0 copy-done.2
  38.3 0.0 copy-done
  38.3 0.0 copy-done.1
  38.4 0.2 owner_step.1
  38.5 8.0 %all-to-all-start.1 = ((bf16[8,88,128]{2,1,0:T(8,128)(2,1)}), bf16[8,88,128]{2,1,0:T(8,128)(2,1)S(1)}, u32[]{:S(2)}, u32[]{:S(2)}) async-start(bf16[8,88,128]{2,1,0:T(8,128)(2,1)} %get-tuple-element.40), calls=%async_computation.1 | async-start | bytes 360448 | tf_op jit(solution)/shard_map/all_to_all | solution.py:439
  46.6 3.1 %factors.1 = (f32[576,576]{1,0:T(8,128)}, bf16[576,576]{1,0:T(8,128)(2,1)}, f32[144,576]{1,0:T(8,128)}, f32[144,576]{1,0:T(8,128)}) custom-call(s32[15]{0:T(128)S(4)} %table.1, bf16[576,576]{1,0:T(8,128)(2,1)S(1)} %get-tuple-element.41.gradient, f32[576,576]{1,0:T(8,128)S(1)} %get-tuple-element.42.second, bf16[576,576]{1,0:T(8,128)(2,1)} %bitcast.27, ...), custom_call_target="tpu_custom_call" | custom-call | flops 382205952 | bytes 5971968 | tf_op jit(solution)/shard_map/factors/pallas_call | solution.py:337
  49.6 0.3 all-to-all-done.1.returned
  49.9 0.8 %place.1 = bf16[4,72,144]{2,1,0:T(8,128)(2,1)} custom-call(s32[15]{0:T(128)S(4)} %table.1, bf16[8,88,128]{2,1,0:T(8,128)(2,1)S(1)} %all-to-all-done.1.returned), custom_call_target="tpu_custom_call" | custom-call | bytes 263168 | tf_op jit(solution)/shard_map/place/pallas_call | solution.py:337
  (1 shorter events, 0.0 us)
Async XLA Ops:
  1.9 8.3 %collective-permute-start = (bf16[336,128]{1,0:T(8,128)(2,1)S(1)}, bf16[336,128]{1,0:T(8,128)(2,1)S(1)}, u32[]{:S(2)}, u32[]{:S(2)}) collective-permute-start(bf16[336,128]{1,0:T(8,128)(2,1)S(1)} %get-tuple-element.27), channel_id=1, source_target_pairs={{0,8},{8,16},{16,24},{24,0},{1,9},{9,17},{17,25},{25,1},{2,10},{10... | collective-permute-start | bytes 258056 | tf_op jit(solution)/shard_map/ppermute | solution.py:393
  5.0 8.3 %collective-permute-start.1 = (bf16[336,128]{1,0:T(8,128)(2,1)S(1)}, bf16[336,128]{1,0:T(8,128)(2,1)S(1)}, u32[]{:S(2)}, u32[]{:S(2)}) collective-permute-start(bf16[336,128]{1,0:T(8,128)(2,1)S(1)} %get-tuple-element.28), channel_id=1, source_target_pairs={{0,16},{8,24},{16,0},{24,8},{1,17},{9,25},{17,1},{25,9},{2,18},{10... | collective-permute-start | bytes 258056 | tf_op jit(solution)/shard_map/ppermute | solution.py:393
  7.6 6.0 %collective-permute-start.2 = (bf16[336,128]{1,0:T(8,128)(2,1)S(1)}, bf16[336,128]{1,0:T(8,128)(2,1)S(1)}, u32[]{:S(2)}, u32[]{:S(2)}) collective-permute-start(bf16[336,128]{1,0:T(8,128)(2,1)S(1)} %get-tuple-element.29), channel_id=1, source_target_pairs={{0,24},{8,0},{16,8},{24,16},{1,25},{9,1},{17,9},{25,17},{2,26},{10... | collective-permute-start | bytes 258056 | tf_op jit(solution)/shard_map/ppermute | solution.py:393
  9.7 28.7 %copy-start.2 = (bf16[1,576,576]{2,1,0:T(8,128)(2,1)S(1)}, bf16[1,576,576]{2,1,0:T(8,128)(2,1)}, u32[]{:S(2)}) copy-start(bf16[1,576,576]{2,1,0:T(8,128)(2,1)} %param.15) | copy-start | bytes 1990660
  9.7 28.6 %copy-start = (f32[1,576,576]{2,1,0:T(8,128)S(1)}, f32[1,576,576]{2,1,0:T(8,128)}, u32[]{:S(2)}) copy-start(f32[1,576,576]{2,1,0:T(8,128)} %param.17) | copy-start | bytes 3981316
  9.7 28.6 %copy-start.1 = (bf16[1,576,576]{2,1,0:T(8,128)(2,1)S(1)}, bf16[1,576,576]{2,1,0:T(8,128)(2,1)}, u32[]{:S(2)}) copy-start(bf16[1,576,576]{2,1,0:T(8,128)(2,1)} %param.14) | copy-start | bytes 1990660
  38.5 11.4 %all-to-all-start.1 = ((bf16[8,88,128]{2,1,0:T(8,128)(2,1)}), bf16[8,88,128]{2,1,0:T(8,128)(2,1)S(1)}, u32[]{:S(2)}, u32[]{:S(2)}) async-start(bf16[8,88,128]{2,1,0:T(8,128)(2,1)} %get-tuple-element.40), calls=%async_computation.1 | async-start | bytes 360448 | tf_op jit(solution)/shard_map/all_to_all | solution.py:439

commit v13 on v11

--- a/solution.py
+++ b/solution.py
@@ -66,19 +66,18 @@
     shares = [lax.rem(me_ref[0] + step, replicas) for step in range(replicas)]
     copies = [
         pltpu.make_async_copy(
-            grad_hbm.at[:, :, columns - half :], last, sems.at[replicas * blocks]
+            grad_hbm.at[:, :, columns - half :], last, sems.at[replicas]
         )
     ]
     for step in range(replicas):
         col = pl.multiple_of(shares[step] * LANES, LANES)
-        for b in range(blocks):
-            copies.append(
-                pltpu.make_async_copy(
-                    grad_hbm.at[b, :, pl.ds(col, LANES)],
-                    outs[step].at[b * rows : (b + 1) * rows, :],
-                    sems.at[step * blocks + b],
-                )
+        copies.append(
+            pltpu.make_async_copy(
+                grad_hbm.at[:, :, pl.ds(col, LANES)],
+                outs[step].at[: blocks * rows, :].reshape(blocks, rows, LANES),
+                sems.at[step],
             )
+        )
     for copy in copies:
         copy.start()
     copies[0].wait()
@@ -165,7 +164,7 @@
         copies[1].wait()
         turned = matmul(transposed, moment[...]).astype(jnp.bfloat16)
         copies[2].wait()
-        old_part[...] = 0.9 * matmul(turned, rbasis[...])
+        old_part[...] = 9.0 * matmul(turned, rbasis[...])
         columns = rbasis.shape[0]
         col_share = columns // (columns // LANES)
         tail = col_share - LANES
@@ -214,10 +213,10 @@
             rotated = matmul(turned[...], rbasis[:, cols])
             fresh = 0.95 * second[:, cols] + 0.05 * rotated * rotated
             new_second[:, cols] = fresh
-            rotated_mom = old_part[:, cols] + 0.1 * rotated
+            rotated_mom = old_part[:, cols] + rotated
             spread = fresh * lax.rsqrt(fresh) + 1e-08
             scaled[:, cols] = (rotated_mom * lax.rsqrt(spread * spread)).astype(jnp.bfloat16)
-        total = matmul(scaled[...], back_basis[...])
+        total = 0.1 * matmul(scaled[...], back_basis[...])
         sums = total.astype(jnp.bfloat16)
         lane = lax.broadcasted_iota(jnp.int32, (SUBLANES, LANES), 1)
         tail_groups = rows // SUBLANES - 1
@@ -396,7 +395,7 @@
         [pieces],
         [sent] * replicas,
         scratch=[shape((blocks, rows, LANES // 2), bf16)],
-        sems=replicas * blocks + 1,
+        sems=replicas + 1,
         far=1,
     )
     parts = [parts[0]] + [

time: 50.5 us -> 50.1 us (level); the launches traced: 49.7 us -> 49.9 us
  no operation moved by 1% of the time
where the time goes in v13:
time: 50.1 us; the launch traced here: 49.9 us
  blocking collectives  24.5 us (49%)
  Pallas kernels  12.6 us (25%)
  starting transfers between devices  11 us (22%)
  waiting for transfers between devices  1.08 us (2%)
  between operations  0.72 us (1%)
    all_to_all x1, blocking collectives, per_device_packed(): lax.all_to_all(outgoing, ('dp', 'mp'), split_axis=0, concat_axis=0, tiled...  24.5 us
    pallas_call x6, Pallas kernels, run(): pl.pallas_call(kernel, out_shape=[pltpu.VMEM(o.shape, o.dtype) for o in o...  11.9 us
    ppermute x3, starting transfers between devices, per_device_packed(): lax.ppermute(parts[s], 'dp', [(i, (i + s) % replicas) for i in range(repl...  7.04 us
    all_to_all x1, starting transfers between devices, per_device_packed(): lax.all_to_all(back, 'mp', split_axis=0, concat_axis=0, tiled=True, axis_...  3.95 us
  transfers between devices with their start and end apart: 4, of which 3 were waited for; matrix products, arithmetic and copies ran while one was open for 0% of the time, Pallas kernels for 15%

profile of v13, /device:TPU:0, one launch (start us, length us, event | category | flops | bytes accessed | tf_op | source)
XLA Modules:
  0.0 49.9 jit_solution(693137478309665061)
XLA Ops:
  0.6 1.1 %pack.1 = (bf16[336,128]{1,0:T(8,128)(2,1)S(1)}, bf16[336,128]{1,0:T(8,128)(2,1)S(1)}, bf16[336,128]{1,0:T(8,128)(2,1)S(1)}, bf16[336,128]{1,0:T(8,128)(2,1)S(1)}) custom-call(s32[1]{0:T(128)} %bitcast.share_ref.me_ref, bf16[4,72,576]{2,1,0:T(8,128)(2,1)} %bitcast.28), custom_call_target="tpu_custom_call" | custom-call | bytes 675840 | tf_op jit(solution)/shard_map/pack/pallas_call | solution.py:346
  1.7 3.1 %collective-permute-start = (bf16[336,128]{1,0:T(8,128)(2,1)S(1)}, bf16[336,128]{1,0:T(8,128)(2,1)S(1)}, u32[]{:S(2)}, u32[]{:S(2)}) collective-permute-start(bf16[336,128]{1,0:T(8,128)(2,1)S(1)} %get-tuple-element.27), channel_id=1, source_target_pairs={{0,8},{8,16},{16,24},{24,0},{1,9},{9,17},{17,25},{25,1},{2,10},{10... | collective-permute-start | bytes 258056 | tf_op jit(solution)/shard_map/ppermute | solution.py:402
  4.8 2.6 %collective-permute-start.1 = (bf16[336,128]{1,0:T(8,128)(2,1)S(1)}, bf16[336,128]{1,0:T(8,128)(2,1)S(1)}, u32[]{:S(2)}, u32[]{:S(2)}) collective-permute-start(bf16[336,128]{1,0:T(8,128)(2,1)S(1)} %get-tuple-element.28), channel_id=1, source_target_pairs={{0,16},{8,24},{16,0},{24,8},{1,17},{9,25},{17,1},{25,9},{2,18},{10... | collective-permute-start | bytes 258056 | tf_op jit(solution)/shard_map/ppermute | solution.py:402
  7.4 1.3 %collective-permute-start.2 = (bf16[336,128]{1,0:T(8,128)(2,1)S(1)}, bf16[336,128]{1,0:T(8,128)(2,1)S(1)}, u32[]{:S(2)}, u32[]{:S(2)}) collective-permute-start(bf16[336,128]{1,0:T(8,128)(2,1)S(1)} %get-tuple-element.29), channel_id=1, source_target_pairs={{0,24},{8,0},{16,8},{24,16},{1,25},{9,1},{17,9},{25,17},{2,26},{10... | collective-permute-start | bytes 258056 | tf_op jit(solution)/shard_map/ppermute | solution.py:402
  8.8 0.7 %table.1 = s32[15]{0:T(128)S(4)} custom-call(s32[1]{0:T(128)} %bitcast.share_ref.me_ref, s32[1]{0:T(128)} %bitcast.1.group_ref, s32[4]{0:T(128)} %owner_ref.1, s32[4]{0:T(128)} %offset_ref.1), custom_call_target="tpu_custom_call" | custom-call | tf_op jit(solution)/shard_map/table/pallas_call | solution.py:405
  9.5 0.0 copy-start.2
  9.5 3.4 %prepare.1 = (bf16[576,576]{1,0:T(8,128)(2,1)S(1)}, f32[576,576]{1,0:T(8,128)S(1)}, bf16[576,256]{1,0:T(8,128)(2,1)S(1)}) custom-call(s32[15]{0:T(128)S(4)} %table.1, bf16[576,576]{1,0:T(8,128)(2,1)} %bitcast.22, bf16[576,576]{1,0:T(8,128)(2,1)} %bitcast.24, bf16[576,576]{1,0:T(8,128)(2,1)} %bitcast.26), custom_call_target="tpu_custom_call" | custom-call | flops 764411904 | bytes 4276224 | tf_op jit(solution)/shard_map/prepare/pallas_call | solution.py:346
  12.8 0.0 copy-start
  12.9 0.0 copy-start.1
  12.9 0.0 collective-permute-done.refs_1_
  12.9 0.3 collective-permute-done.1.refs_2_
  13.2 0.2 collective-permute-done.2.refs_3_
  13.4 0.2 route.1
  13.6 24.5 %all_to_all.10.arrived = bf16[32,88,128]{2,1,0:T(8,128)(2,1)S(1)} all-to-all(bf16[32,88,128]{2,1,0:T(8,128)(2,1)S(1)} %route.1), channel_id=1, replica_groups=mesh['dp'=4,'mp'=8] {'dp','mp'}, dimensions={0} | all-to-all | bytes 1441792 | tf_op jit(solution)/shard_map/all_to_all | solution.py:434
  38.1 0.0 copy-done.2
  38.1 0.0 copy-done
  38.1 0.0 copy-done.1
  38.1 3.3 %owner_step.1 = (bf16[576,576]{1,0:T(8,128)(2,1)S(1)}, f32[576,576]{1,0:T(8,128)S(1)}, bf16[8,88,128]{2,1,0:T(8,128)(2,1)}) custom-call(s32[15]{0:T(128)S(4)} %table.1, bf16[32,88,128]{2,1,0:T(8,128)(2,1)S(1)} %all_to_all.10.arrived, bf16[576,576]{1,0:T(8,128)(2,1)S(1)} %bitcast.23, bf16[576,576]{1,0:T(8,128)(2,1)S(1)} %bitcast.25, ...), custom_call_target="tpu_custom_call" | custom-call | flops 1146617856 | bytes 7831552 | tf_op jit(solution)/shard_map/owner_step/pallas_call | solution.py:346
  41.4 4.0 %all-to-all-start.1 = ((bf16[8,88,128]{2,1,0:T(8,128)(2,1)}), bf16[8,88,128]{2,1,0:T(8,128)(2,1)S(1)}, u32[]{:S(2)}, u32[]{:S(2)}) async-start(bf16[8,88,128]{2,1,0:T(8,128)(2,1)} %get-tuple-element.40), calls=%async_computation.1 | async-start | bytes 360448 | tf_op jit(solution)/shard_map/all_to_all | solution.py:448
  45.4 3.2 %factors.1 = (f32[576,576]{1,0:T(8,128)}, bf16[576,576]{1,0:T(8,128)(2,1)}, f32[144,576]{1,0:T(8,128)}, f32[144,576]{1,0:T(8,128)}) custom-call(s32[15]{0:T(128)S(4)} %table.1, bf16[576,576]{1,0:T(8,128)(2,1)S(1)} %get-tuple-element.41.gradient, f32[576,576]{1,0:T(8,128)S(1)} %get-tuple-element.42.second, bf16[576,576]{1,0:T(8,128)(2,1)} %bitcast.27, ...), custom_call_target="tpu_custom_call" | custom-call | flops 382205952 | bytes 5971968 | tf_op jit(solution)/shard_map/factors/pallas_call | solution.py:346
  48.6 0.5 %all-to-all-done.1.returned = bf16[8,88,128]{2,1,0:T(8,128)(2,1)S(1)} async-done(((bf16[8,88,128]{2,1,0:T(8,128)(2,1)}), bf16[8,88,128]{2,1,0:T(8,128)(2,1)S(1)}, u32[]{:S(2)}, u32[]{:S(2)}) %all-to-all-start.1) | async-done | bytes 180256 | tf_op jit(solution)/shard_map/all_to_all | solution.py:448
  49.1 0.8 %place.1 = bf16[4,72,144]{2,1,0:T(8,128)(2,1)} custom-call(s32[15]{0:T(128)S(4)} %table.1, bf16[8,88,128]{2,1,0:T(8,128)(2,1)S(1)} %all-to-all-done.1.returned), custom_call_target="tpu_custom_call" | custom-call | bytes 263168 | tf_op jit(solution)/shard_map/place/pallas_call | solution.py:346
Async XLA Ops:
  1.7 11.1 %collective-permute-start = (bf16[336,128]{1,0:T(8,128)(2,1)S(1)}, bf16[336,128]{1,0:T(8,128)(2,1)S(1)}, u32[]{:S(2)}, u32[]{:S(2)}) collective-permute-start(bf16[336,128]{1,0:T(8,128)(2,1)S(1)} %get-tuple-element.27), channel_id=1, source_target_pairs={{0,8},{8,16},{16,24},{24,0},{1,9},{9,17},{17,25},{25,1},{2,10},{10... | collective-permute-start | bytes 258056 | tf_op jit(solution)/shard_map/ppermute | solution.py:402
  4.8 8.3 %collective-permute-start.1 = (bf16[336,128]{1,0:T(8,128)(2,1)S(1)}, bf16[336,128]{1,0:T(8,128)(2,1)S(1)}, u32[]{:S(2)}, u32[]{:S(2)}) collective-permute-start(bf16[336,128]{1,0:T(8,128)(2,1)S(1)} %get-tuple-element.28), channel_id=1, source_target_pairs={{0,16},{8,24},{16,0},{24,8},{1,17},{9,25},{17,1},{25,9},{2,18},{10... | collective-permute-start | bytes 258056 | tf_op jit(solution)/shard_map/ppermute | solution.py:402
  7.4 6.0 %collective-permute-start.2 = (bf16[336,128]{1,0:T(8,128)(2,1)S(1)}, bf16[336,128]{1,0:T(8,128)(2,1)S(1)}, u32[]{:S(2)}, u32[]{:S(2)}) collective-permute-start(bf16[336,128]{1,0:T(8,128)(2,1)S(1)} %get-tuple-element.29), channel_id=1, source_target_pairs={{0,24},{8,0},{16,8},{24,16},{1,25},{9,1},{17,9},{25,17},{2,26},{10... | collective-permute-start | bytes 258056 | tf_op jit(solution)/shard_map/ppermute | solution.py:402
  9.5 28.7 %copy-start.2 = (bf16[1,576,576]{2,1,0:T(8,128)(2,1)S(1)}, bf16[1,576,576]{2,1,0:T(8,128)(2,1)}, u32[]{:S(2)}) copy-start(bf16[1,576,576]{2,1,0:T(8,128)(2,1)} %param.15) | copy-start | bytes 1990660
  12.8 25.3 %copy-start = (f32[1,576,576]{2,1,0:T(8,128)S(1)}, f32[1,576,576]{2,1,0:T(8,128)}, u32[]{:S(2)}) copy-start(f32[1,576,576]{2,1,0:T(8,128)} %param.17) | copy-start | bytes 3981316
  12.9 25.3 %copy-start.1 = (bf16[1,576,576]{2,1,0:T(8,128)(2,1)S(1)}, bf16[1,576,576]{2,1,0:T(8,128)(2,1)}, u32[]{:S(2)}) copy-start(bf16[1,576,576]{2,1,0:T(8,128)(2,1)} %param.14) | copy-start | bytes 1990660
  41.4 7.7 %all-to-all-start.1 = ((bf16[8,88,128]{2,1,0:T(8,128)(2,1)}), bf16[8,88,128]{2,1,0:T(8,128)(2,1)S(1)}, u32[]{:S(2)}, u32[]{:S(2)}) async-start(bf16[8,88,128]{2,1,0:T(8,128)(2,1)} %get-tuple-element.40), calls=%async_computation.1 | async-start | bytes 360448 | tf_op jit(solution)/shard_map/all_to_all | solution.py:448

commit v14 on v13

--- a/solution.py
+++ b/solution.py
@@ -308,33 +308,24 @@
     second_copy.wait()
 
 
-def place_kernel(table, returned, update, tails, sems):
+def place_kernel(table, returned, update, full, sems):
     blocks, rows, col_share = update.shape
     groups = returned.shape[0]
     tail_groups = rows // SUBLANES - 1
     width = col_share - LANES
-    copies = []
+    copies = [
+        pltpu.make_async_copy(full.at[place], update.at[place], sems.at[place])
+        for place in range(blocks)
+    ]
     for place in range(blocks):
         slot = table[SLOTS + groups + place]
-        copies.append(
-            pltpu.make_async_copy(
-                returned.at[slot, :rows], update.at[place, :, :LANES], sems.at[place]
-            )
-        )
-        copies[-1].start()
-    for place in range(blocks):
-        slot = table[SLOTS + groups + place]
+        full[place, :, :LANES] = returned[slot, :rows, :]
         for g in range(tail_groups):
-            tails[place, g * SUBLANES : (g + 1) * SUBLANES, :] = returned[
+            full[place, g * SUBLANES : (g + 1) * SUBLANES, LANES:] = returned[
                 slot, rows : rows + SUBLANES, g * width : (g + 1) * width
             ]
-        tails[place, rows - SUBLANES :, :] = returned[slot, rows + SUBLANES :, :width]
-        copies.append(
-            pltpu.make_async_copy(
-                tails.at[place], update.at[place, :, LANES:], sems.at[blocks + place]
-            )
-        )
-        copies[-1].start()
+        full[place, rows - SUBLANES :, LANES:] = returned[slot, rows + SUBLANES :, :width]
+        copies[place].start()
     for copy in copies:
         copy.wait()
 
@@ -471,8 +462,8 @@
         [table],
         [returned],
         [shape((blocks, rows, col_share), bf16)],
-        scratch=[shape((blocks, rows, col_share - LANES), bf16)],
-        sems=2 * blocks,
+        scratch=[shape((blocks, rows, col_share), bf16)],
+        sems=blocks,
         far_outs=1,
     )
     return (

time: 50.1 us -> 50.1 us (level)
  Pallas kernels: 12.6 us -> 5.99 us
  waiting for transfers between devices: 1.08 us -> 4.34 us
  starting transfers between devices: 11 us -> 14.1 us
    pallas_call x6, Pallas kernels: 11.9 us -> 5.3 us  [run(): pl.pallas_call(kernel, out_shape=[pltpu.VMEM(o.shape, o.dtype) for o in o...]
    ppermute x3, waiting for transfers between devices: 0.54 us -> 3.86 us  [per_device_packed(): lax.ppermute(parts[s], 'dp', [(i, (i + s) % replicas) for i in range(repl...]
    all_to_all x1, starting transfers between devices: 3.95 us -> 7.04 us  [per_device_packed(): lax.all_to_all(back, 'mp', split_axis=0, concat_axis=0, tiled=True, axis_...]
  transfers between devices with their start and end apart: 4 -> 4, of which waited for: 3 -> 4; matrix products, arithmetic and copies ran while one was open for 0% -> 0% of each run, Pallas kernels for 15% -> 8%
where the time goes in v14:
time: 50.1 us; the launch traced here: 49.7 us
  blocking collectives  24.5 us (49%)
  starting transfers between devices  14.1 us (28%)
  Pallas kernels  5.99 us (12%)
  waiting for transfers between devices  4.34 us (9%)
  between operations  0.71 us (1%)
    all_to_all x1, blocking collectives, per_device_packed(): lax.all_to_all(outgoing, ('dp', 'mp'), split_axis=0, concat_axis=0, tiled...  24.5 us
    ppermute x3, starting transfers between devices, per_device_packed(): lax.ppermute(parts[s], 'dp', [(i, (i + s) % replicas) for i in range(repl...  7.04 us
    all_to_all x1, starting transfers between devices, per_device_packed(): lax.all_to_all(back, 'mp', split_axis=0, concat_axis=0, tiled=True, axis_...  7.04 us
    pallas_call x6, Pallas kernels, run(): pl.pallas_call(kernel, out_shape=[pltpu.VMEM(o.shape, o.dtype) for o in o...  5.3 us
    ppermute x3, waiting for transfers between devices, per_device_packed(): lax.ppermute(parts[s], 'dp', [(i, (i + s) % replicas) for i in range(repl...  3.86 us
  transfers between devices with their start and end apart: 4, of which 4 were waited for; matrix products, arithmetic and copies ran while one was open for 0% of the time, Pallas kernels for 8%

profile of v14, /device:TPU:0, one launch (start us, length us, event | category | flops | bytes accessed | tf_op | source)
XLA Modules:
  0.0 49.7 jit_solution(17566624187561893090)
XLA Ops:
  0.6 1.1 %pack.1 = (bf16[336,128]{1,0:T(8,128)(2,1)S(1)}, bf16[336,128]{1,0:T(8,128)(2,1)S(1)}, bf16[336,128]{1,0:T(8,128)(2,1)S(1)}, bf16[336,128]{1,0:T(8,128)(2,1)S(1)}) custom-call(s32[1]{0:T(128)} %bitcast.share_ref.me_ref, bf16[4,72,576]{2,1,0:T(8,128)(2,1)} %bitcast.28), custom_call_target="tpu_custom_call" | custom-call | bytes 675840 | tf_op jit(solution)/shard_map/pack/pallas_call | solution.py:337
  1.7 3.1 %collective-permute-start = (bf16[336,128]{1,0:T(8,128)(2,1)S(1)}, bf16[336,128]{1,0:T(8,128)(2,1)S(1)}, u32[]{:S(2)}, u32[]{:S(2)}) collective-permute-start(bf16[336,128]{1,0:T(8,128)(2,1)S(1)} %get-tuple-element.27), channel_id=1, source_target_pairs={{0,8},{8,16},{16,24},{24,0},{1,9},{9,17},{17,25},{25,1},{2,10},{10... | collective-permute-start | bytes 258056 | tf_op jit(solution)/shard_map/ppermute | solution.py:393
  4.8 2.6 %collective-permute-start.1 = (bf16[336,128]{1,0:T(8,128)(2,1)S(1)}, bf16[336,128]{1,0:T(8,128)(2,1)S(1)}, u32[]{:S(2)}, u32[]{:S(2)}) collective-permute-start(bf16[336,128]{1,0:T(8,128)(2,1)S(1)} %get-tuple-element.28), channel_id=1, source_target_pairs={{0,16},{8,24},{16,0},{24,8},{1,17},{9,25},{17,1},{25,9},{2,18},{10... | collective-permute-start | bytes 258056 | tf_op jit(solution)/shard_map/ppermute | solution.py:393
  7.4 1.3 %collective-permute-start.2 = (bf16[336,128]{1,0:T(8,128)(2,1)S(1)}, bf16[336,128]{1,0:T(8,128)(2,1)S(1)}, u32[]{:S(2)}, u32[]{:S(2)}) collective-permute-start(bf16[336,128]{1,0:T(8,128)(2,1)S(1)} %get-tuple-element.29), channel_id=1, source_target_pairs={{0,24},{8,0},{16,8},{24,16},{1,25},{9,1},{17,9},{25,17},{2,26},{10... | collective-permute-start | bytes 258056 | tf_op jit(solution)/shard_map/ppermute | solution.py:393
  8.8 0.7 %table.1 = s32[15]{0:T(128)S(4)} custom-call(s32[1]{0:T(128)} %bitcast.share_ref.me_ref, s32[1]{0:T(128)} %bitcast.1.group_ref, s32[4]{0:T(128)} %owner_ref.1, s32[4]{0:T(128)} %offset_ref.1), custom_call_target="tpu_custom_call" | custom-call | tf_op jit(solution)/shard_map/table/pallas_call | solution.py:396
  9.5 0.0 copy-start.2
  9.5 0.0 copy-start
  9.5 0.0 copy-start.1
  9.6 0.4 collective-permute-done.refs_1_
  10.0 3.2 %collective-permute-done.1.refs_2_ = bf16[336,128]{1,0:T(8,128)(2,1)S(1)} collective-permute-done((bf16[336,128]{1,0:T(8,128)(2,1)S(1)}, bf16[336,128]{1,0:T(8,128)(2,1)S(1)}, u32[]{:S(2)}, u32[]{:S(2)}) %collective-permute-start.1) | collective-permute-done | bytes 86048 | tf_op jit(solution)/shard_map/ppermute | solution.py:393
  13.2 0.2 collective-permute-done.2.refs_3_
  13.4 0.2 route.1
  13.6 24.5 %all_to_all.10.arrived = bf16[32,88,128]{2,1,0:T(8,128)(2,1)S(1)} all-to-all(bf16[32,88,128]{2,1,0:T(8,128)(2,1)S(1)} %route.1), channel_id=1, replica_groups=mesh['dp'=4,'mp'=8] {'dp','mp'}, dimensions={0} | all-to-all | bytes 1441792 | tf_op jit(solution)/shard_map/all_to_all | solution.py:425
  38.1 0.0 copy-done.2
  38.1 0.0 copy-done
  38.1 0.0 copy-done.1
  38.1 0.2 owner_step.1
  38.3 7.0 %all-to-all-start.1 = ((bf16[8,88,128]{2,1,0:T(8,128)(2,1)}), bf16[8,88,128]{2,1,0:T(8,128)(2,1)S(1)}, u32[]{:S(2)}, u32[]{:S(2)}) async-start(bf16[8,88,128]{2,1,0:T(8,128)(2,1)} %get-tuple-element.40), calls=%async_computation.1 | async-start | bytes 360448 | tf_op jit(solution)/shard_map/all_to_all | solution.py:439
  45.4 3.1 %factors.1 = (f32[576,576]{1,0:T(8,128)}, bf16[576,576]{1,0:T(8,128)(2,1)}, f32[144,576]{1,0:T(8,128)}, f32[144,576]{1,0:T(8,128)}) custom-call(s32[15]{0:T(128)S(4)} %table.1, bf16[576,576]{1,0:T(8,128)(2,1)S(1)} %get-tuple-element.41.gradient, f32[576,576]{1,0:T(8,128)S(1)} %get-tuple-element.42.second, bf16[576,576]{1,0:T(8,128)(2,1)} %bitcast.27, ...), custom_call_target="tpu_custom_call" | custom-call | flops 382205952 | bytes 5971968 | tf_op jit(solution)/shard_map/factors/pallas_call | solution.py:337
  48.4 0.5 all-to-all-done.1.returned
  48.9 0.8 %place.1 = bf16[4,72,144]{2,1,0:T(8,128)(2,1)} custom-call(s32[15]{0:T(128)S(4)} %table.1, bf16[8,88,128]{2,1,0:T(8,128)(2,1)S(1)} %all-to-all-done.1.returned), custom_call_target="tpu_custom_call" | custom-call | bytes 263168 | tf_op jit(solution)/shard_map/place/pallas_call | solution.py:337
  (1 shorter events, 0.0 us)
Async XLA Ops:
  1.7 8.3 %collective-permute-start = (bf16[336,128]{1,0:T(8,128)(2,1)S(1)}, bf16[336,128]{1,0:T(8,128)(2,1)S(1)}, u32[]{:S(2)}, u32[]{:S(2)}) collective-permute-start(bf16[336,128]{1,0:T(8,128)(2,1)S(1)} %get-tuple-element.27), channel_id=1, source_target_pairs={{0,8},{8,16},{16,24},{24,0},{1,9},{9,17},{17,25},{25,1},{2,10},{10... | collective-permute-start | bytes 258056 | tf_op jit(solution)/shard_map/ppermute | solution.py:393
  4.8 8.3 %collective-permute-start.1 = (bf16[336,128]{1,0:T(8,128)(2,1)S(1)}, bf16[336,128]{1,0:T(8,128)(2,1)S(1)}, u32[]{:S(2)}, u32[]{:S(2)}) collective-permute-start(bf16[336,128]{1,0:T(8,128)(2,1)S(1)} %get-tuple-element.28), channel_id=1, source_target_pairs={{0,16},{8,24},{16,0},{24,8},{1,17},{9,25},{17,1},{25,9},{2,18},{10... | collective-permute-start | bytes 258056 | tf_op jit(solution)/shard_map/ppermute | solution.py:393
  7.4 6.0 %collective-permute-start.2 = (bf16[336,128]{1,0:T(8,128)(2,1)S(1)}, bf16[336,128]{1,0:T(8,128)(2,1)S(1)}, u32[]{:S(2)}, u32[]{:S(2)}) collective-permute-start(bf16[336,128]{1,0:T(8,128)(2,1)S(1)} %get-tuple-element.29), channel_id=1, source_target_pairs={{0,24},{8,0},{16,8},{24,16},{1,25},{9,1},{17,9},{25,17},{2,26},{10... | collective-permute-start | bytes 258056 | tf_op jit(solution)/shard_map/ppermute | solution.py:393
  9.5 28.7 %copy-start.2 = (bf16[1,576,576]{2,1,0:T(8,128)(2,1)S(1)}, bf16[1,576,576]{2,1,0:T(8,128)(2,1)}, u32[]{:S(2)}) copy-start(bf16[1,576,576]{2,1,0:T(8,128)(2,1)} %param.15) | copy-start | bytes 1990660
  9.5 28.6 %copy-start = (f32[1,576,576]{2,1,0:T(8,128)S(1)}, f32[1,576,576]{2,1,0:T(8,128)}, u32[]{:S(2)}) copy-start(f32[1,576,576]{2,1,0:T(8,128)} %param.17) | copy-start | bytes 3981316
  9.5 28.6 %copy-start.1 = (bf16[1,576,576]{2,1,0:T(8,128)(2,1)S(1)}, bf16[1,576,576]{2,1,0:T(8,128)(2,1)}, u32[]{:S(2)}) copy-start(bf16[1,576,576]{2,1,0:T(8,128)(2,1)} %param.14) | copy-start | bytes 1990660
  38.3 10.6 %all-to-all-start.1 = ((bf16[8,88,128]{2,1,0:T(8,128)(2,1)}), bf16[8,88,128]{2,1,0:T(8,128)(2,1)S(1)}, u32[]{:S(2)}, u32[]{:S(2)}) async-start(bf16[8,88,128]{2,1,0:T(8,128)(2,1)} %get-tuple-element.40), calls=%async_computation.1 | async-start | bytes 360448 | tf_op jit(solution)/shard_map/all_to_all | solution.py:439
